TPU v7x, 128 devices: a whole 4x4x4 slice. The times are simulated.
128 devices in a mesh: sky: 4 (over y), tm: 32 (over z, x, core).
Axes of the slice: x: 4, y: 4, z: 4, core: 2. Of those that a mesh axis runs over, the one named last changes fastest.
Arguments:
- attitude: bfloat16 [3, 8192], P(None, 'tm'), may hold values from -6 to 6
- win_start: int32 [8192], P(('sky', 'tm')), may hold values from 0 to 8128
- design: bfloat16 [8192, 256, 192], P(('sky', 'tm')), may hold values from -0.4375 to 0.4375
- obs_value: float32 [8192, 256], P(('sky', 'tm')), may hold values from -6 to 6
- star_design: float32 [8192, 5, 256], P(('sky', 'tm')), may hold values from -8 to 8
- star_local: int32 [8192, 256], P(('sky', 'tm')), may hold values from 0 to 16383
- block_dest: int32 [8192], P(('sky', 'tm')), may hold values from 0 to 3, as said below
- block_count: int32 [128], P(('sky', 'tm')), may hold values from 32 to 64, as said below
Outputs:
- residual_out: float32 [8192, 256], P(('sky', 'tm'))
- star_update: float32 [5, 65536], P(None, ('sky', 'tm'))
Inputs may be any that keep to these rules, and one draw needn't show every extreme that they name: `block_count`: every device has at least 32 live blocks, its first ones; some device has all 64. `block_dest`: no group is named by more than 32 of one device's live blocks, and exactly 32 of them name one group, which is the same group for all devices of one tm index.
All inputs are finite; a program needn't handle non-finite values.
Results may differ from a plain program's by a relative error of at most 0.0003.
Values may be sent and summed in bfloat16 or wider, within the bound.
No kernel may reach another device: no remote copies, remote signals or barrier semaphores. Data moves between devices by JAX's collectives and lax.ppermute only.
A program may use at most 128 MiB of HBM per device.

v0:
```python
import jax
import jax.numpy as jnp
from jax import lax
from jax.sharding import PartitionSpec as P

ROWS = 256
WIN = 64
CAP = 32
STAR_DEV = 512


ridge_term = 1.0


def pair_terms(partials, values):
    term_list = []
    for i in range(5):
        for j in range(i, 5):
            term_list.append(partials[:, i] * partials[:, j])
    for i in range(5):
        term_list.append(partials[:, i] * values)
    return jnp.stack(term_list).reshape(20, -1)


def solve_five(packed):
    entries = {}
    packed_row = 0
    for i in range(5):
        for j in range(i, 5):
            if i == j:
                entries[i, j] = packed[packed_row] + ridge_term
            else:
                entries[i, j] = packed[packed_row]
            packed_row += 1
    factor = {}
    for j in range(5):
        pivot_value = entries[j, j]
        for k in range(j):
            pivot_value = pivot_value - factor[j, k] * factor[j, k]
        factor[j, j] = jnp.sqrt(pivot_value)
        for i in range(j + 1, 5):
            running_value = entries[j, i]
            for k in range(j):
                running_value = running_value - factor[i, k] * factor[j, k]
            factor[i, j] = running_value / factor[j, j]
    forward = []
    for i in range(5):
        running_value = packed[15 + i]
        for k in range(i):
            running_value = running_value - factor[i, k] * forward[k]
        forward.append(running_value / factor[i, i])
    answer = [None] * 5
    for i in reversed(range(5)):
        running_value = forward[i]
        for k in range(i + 1, 5):
            running_value = running_value - factor[k, i] * answer[k]
        answer[i] = running_value / factor[i, i]
    return jnp.stack(answer)


def star_fit(partials, picked):
    summed = partials[:, 0] * picked[0]
    for c in range(1, 5):
        summed = summed + partials[:, c] * picked[c]
    return summed


def local(attitude, win_start, design, obs_value, star_design, star_local, block_dest, block_count):
    block_total = design.shape[0]
    groups = lax.axis_size("sky")
    star_group = STAR_DEV * lax.axis_size("tm")
    offsets = win_start[:, None] + jnp.arange(WIN, dtype=jnp.int32)[None, :]
    piece_knots = lax.all_gather(attitude, "tm", axis=1, tiled=True)
    piece_width = piece_knots.shape[1]
    inside = (offsets >= 0) & (offsets < piece_width)
    picked = piece_knots[:, jnp.clip(offsets, 0, piece_width - 1)]
    windows = jnp.where(inside[None], picked, jnp.zeros_like(picked))
    flat_window = jnp.transpose(windows, (1, 0, 2)).reshape(block_total, 3 * WIN)
    fitted = jnp.einsum("brc,bc->br", design, flat_window, preferred_element_type=jnp.float32)
    residual = obs_value - fitted
    live = jnp.arange(block_total, dtype=jnp.int32) < block_count[0]
    onehot = (
        (block_dest[:, None] == jnp.arange(groups, dtype=jnp.int32)[None, :]) & live[:, None]
    ).astype(jnp.int32)
    slot_rank = jnp.sum(jnp.cumsum(onehot, axis=0) * onehot, axis=1) - 1
    slot_index = jnp.where(live, block_dest * CAP + slot_rank, groups * CAP)
    payload = jnp.concatenate([star_design, residual[:, None, :]], axis=1)
    outgoing = (
        jnp.zeros((groups * CAP, 6, ROWS), jnp.float32).at[slot_index].set(payload, mode="drop")
    )
    out_stars = (
        jnp.zeros((groups * CAP, ROWS), jnp.int32).at[slot_index].set(star_local, mode="drop")
    )
    incoming, in_stars = (
        lax.all_to_all(outgoing, "sky", split_axis=0, concat_axis=0, tiled=True),
        lax.all_to_all(out_stars, "sky", split_axis=0, concat_axis=0, tiled=True),
    )
    in_partials = incoming[:, :5]
    in_residual = incoming[:, 5]
    partial_normals = (
        jnp.zeros((20, star_group), jnp.float32)
        .at[:, in_stars.reshape(-1)]
        .add(pair_terms(in_partials, in_residual))
    )
    summed = lax.psum(partial_normals, "tm")
    group_shift = solve_five(summed)
    own_update = lax.dynamic_slice_in_dim(group_shift, lax.axis_index("tm") * STAR_DEV, STAR_DEV, 1)
    owner_result = in_residual - star_fit(in_partials, group_shift[:, in_stars])
    returned = lax.all_to_all(owner_result, "sky", split_axis=0, concat_axis=0, tiled=True)
    gathered_back = returned[jnp.clip(slot_index, 0, groups * CAP - 1)]
    result = jnp.where(live[:, None], gathered_back, jnp.zeros_like(gathered_back))
    return (result, own_update)


def solution(mesh):
    placed = (
        P(None, "tm"),
        P(("sky", "tm")),
        P(("sky", "tm"), None, None),
        P(("sky", "tm"), None),
        P(("sky", "tm"), None, None),
        P(("sky", "tm"), None),
        P(("sky", "tm")),
        P(("sky", "tm")),
    )
    return jax.shard_map(
        local,
        mesh=mesh,
        in_specs=placed,
        out_specs=(P(("sky", "tm"), None), P(None, ("sky", "tm"))),
        check_vma=False,
    )
```

profile of v0, /device:TPU:0, one launch (start us, length us, event | category | flops | bytes accessed | tf_op | source)
XLA Modules:
  0.0 610.4 jit_solution(6821081962550460261)
XLA Ops:
  10.2 1.7 scatter_custom_fusion.1
  12.0 4.6 all-to-all-start.1
  18.8 27.4 %all_gather.3 = bf16[3,8192]{0,1:T(8,128)(2,1)S(1)} all-gather(bf16[3,256]{0,1:T(8,128)(2,1)S(1)} %copy.35), channel_id=1, replica_groups=mesh['sky'=4,'tm'=32] {'tm'}, dimensions={1}, use_global_device_ids=true | all-gather | bytes 50688 | tf_op jit(solution)/shard_map/all_gather | solution.py:73
  46.2 12.1 %gather_fusion = bf16[4096,3]{1,0:T(8,128)(2,1)S(1)} fusion(bf16[3,8192]{0,1:T(8,128)(2,1)S(1)} %all_gather.3, s32[4096]{0:T(1024)S(1)} %broadcast_clamp_fusion.1), kind=kCustom, calls=%fused_computation | custom fusion | bytes 65536 | tf_op jit(solution)/shard_map/gather | solution.py:76
  59.8 3.7 fusion.50
  65.8 7.3 %scatter_fusion = f32[128,6,256]{2,1,0:T(8,128)} fusion(f32[128,6,256]{2,1,0:T(8,128)} %broadcast_in_dim.53, s32[64]{0:T(128)S(1)} %compare_select_fusion.4, f32[64,6,256]{2,1,0:T(8,128)S(1)} %copy.37), kind=kCustom, calls=%fused_computation.3 | custom fusion | bytes 1179904 | tf_op jit(solution)/shard_map/scatter | solution.py:89
  73.1 4.5 all-to-all-start
  79.3 14.0 %all-to-all-done = f32[128,6,256]{2,1,0:T(8,128)S(1)} async-done(((f32[128,6,256]{2,1,0:T(8,128)}), f32[128,6,256]{2,1,0:T(8,128)S(1)}, u32[]{:S(2)}, u32[]{:S(2)}) %all-to-all-start) | async-done | bytes 786464 | tf_op jit(solution)/shard_map/all_to_all | solution.py:95
  93.3 2.0 fusion.47
  95.3 2.2 fusion.46
  97.4 8.0 %stack.4 = f32[20,32768]{1,0:T(8,128)S(1)} concatenate(f32[1,32768]{1,0:T(1,128)} %bitcast.78, f32[1,32768]{1,0:T(1,128)} %bitcast.79, f32[1,32768]{1,0:T(1,128)} %bitcast.81, f32[1,32768]{1,0:T(1,128)} %bitcast.84, f32[1,32768]{1,0:T(1,128)} %bitcast.88, f32[1,32768]{1,0:T(1,128)} %bitcast.80, f32[1,32768]{1,0:T(1,128)} %bitcast.82, f32[1,32768]{1,0:T(1,128)} %bitcast.85, ...), dimensions={0} | concatenate | bytes 5242880 | tf_op jit(solution)/shard_map/stack | solution.py:22
  105.4 9.0 %copy.38 = f32[32768,20]{1,0:T(8,128)} copy(f32[32768,20]{0,1:T(8,128)S(1)} %bitcast.65) | data formatting | bytes 5242880 | tf_op jit(solution)/shard_map/stack | solution.py:22
  114.5 177.9 %scatter_custom_fusion.2 = f32[20,16384]{0,1:T(8,128)} fusion(s32[32768]{0:T(1024)} %bitcast.102, f32[32768,20]{1,0:T(8,128)} %copy.38, f32[]{:T(128)} %constant.13.clone.1), kind=kCustom, calls=%fused_computation.6 | custom fusion | flops 655360 | bytes 1311232 | tf_op jit(solution)/shard_map/scatter-add | solution.py:103
  292.4 6.3 %copy.39 = f32[20,16384]{1,0:T(8,128)} copy(f32[20,16384]{0,1:T(8,128)} %scatter_custom_fusion.2) | data formatting | bytes 2621440 | tf_op jit(solution)/shard_map/scatter-add | solution.py:103
  298.7 2.5 fusion.48
  301.4 149.4 %all-reduce.2.cloned.1.call-done = f32[20,16384]{1,0:T(8,128)} async-done(((f32[20,16384]{1,0:T(8,128)}), f32[20,16384]{1,0:T(8,128)}) %all-reduce.2.cloned.1.call-update) | async-done | bytes 1310736 | tf_op jit(solution)/shard_map/psum | solution.py:105
  450.8 5.3 fusion.32
  456.1 3.7 fusion.33
  459.9 3.7 subtract_divide_fusion
  464.1 5.3 copy.40
  469.4 111.6 %gather_fusion.1 = f32[32768,5]{1,0:T(8,128)} fusion(f32[5,16384]{0,1:T(8,128)} %copy.40, s32[32768]{0:T(1024)S(1)} %broadcast_clamp_fusion), kind=kCustom, calls=%fused_computation.1 | custom fusion | bytes 1441792 | tf_op jit(solution)/shard_map/gather | solution.py:108
  581.0 10.0 %copy.41 = f32[128,256,5]{1,0,2:T(8,128)S(1)} copy(f32[128,256,5]{2,1,0:T(8,128)} %bitcast.64) | data formatting | bytes 1310720 | tf_op jit(solution)/shard_map/gather | solution.py:108
  591.9 4.3 all-to-all-start.2
  596.8 5.4 all-to-all-done.2
  (51 shorter events, 13.4 us)
Async XLA Ops:
  7.2 56.3 %copy-start.5 = (f32[64,256]{1,0:T(8,128)S(1)}, f32[64,256]{1,0:T(8,128)}, u32[]{:S(2)}) copy-start(f32[64,256]{1,0:T(8,128)} %param.11) | copy-start | bytes 196612
  12.0 61.1 %all-to-all-start.1 = ((s32[4,32,256]{2,1,0:T(8,128)}), s32[4,32,256]{2,1,0:T(8,128)S(1)}, u32[]{:S(2)}, u32[]{:S(2)}) async-start(s32[4,32,256]{2,1,0:T(8,128)} %bitcast.7), calls=%async_computation.1 | async-start | bytes 262144 | tf_op jit(solution)/shard_map/all_to_all | solution.py:96
  73.1 20.2 %all-to-all-start = ((f32[128,6,256]{2,1,0:T(8,128)}), f32[128,6,256]{2,1,0:T(8,128)S(1)}, u32[]{:S(2)}, u32[]{:S(2)}) async-start(f32[128,6,256]{2,1,0:T(8,128)} %scatter_fusion), calls=%async_computation | async-start | bytes 2097152 | tf_op jit(solution)/shard_map/all_to_all | solution.py:95
  77.6 373.2 %all-reduce.2.cloned.1.call-start = ((), (), s32[]{:S(2)}) async-start(), calls=%async_computation.3 | async-start | bytes 3145728 | tf_op jit(solution)/shard_map/psum | solution.py:105
  93.3 4.2 copy-start
  114.5 184.2 %copy-start.4 = (s32[16,2,8,128]{3,1,2,0:T(2,128)S(1)}, s32[16,2,8,128]{3,1,2,0:T(2,128)}, u32[]{:S(2)}) copy-start(s32[16,2,8,128]{3,1,2,0:T(2,128)} %copy.50) | copy-start | bytes 393220
  292.4 8.9 %copy-start.2 = (f32[128,1,256]{2,1,0:T(1,128)S(1)}, f32[128,1,256]{2,1,0:T(1,128)}, u32[]{:S(2)}) copy-start(f32[128,1,256]{2,1,0:T(1,128)} %get-tuple-element.41) | copy-start | bytes 393220
  292.4 9.0 %copy-start.1 = (f32[128,1,256]{2,1,0:T(1,128)S(1)}, f32[128,1,256]{2,1,0:T(1,128)}, u32[]{:S(2)}) copy-start(f32[128,1,256]{2,1,0:T(1,128)} %get-tuple-element.51) | copy-start | bytes 393220
  292.4 9.0 %copy-start.3 = (f32[128,1,256]{2,1,0:T(1,128)S(1)}, f32[128,1,256]{2,1,0:T(1,128)}, u32[]{:S(2)}) copy-start(f32[128,1,256]{2,1,0:T(1,128)} %get-tuple-element.29) | copy-start | bytes 393220
  591.9 10.3 %all-to-all-start.2 = ((f32[4,32,256]{2,1,0:T(8,128)}), f32[4,32,256]{2,1,0:T(8,128)S(1)}, u32[]{:S(2)}, u32[]{:S(2)}) async-start(f32[4,32,256]{2,1,0:T(8,128)} %add_subtract_fusion), calls=%async_computation.2 | async-start | bytes 262144 | tf_op jit(solution)/shard_map/all_to_all | solution.py:109
Sparse Core Ops, SparseCore 0:
  298.8 151.9 all-reduce.1
where the time goes:
time: 612 us; the launch traced here: 610 us
  other arithmetic  202 us (33%)
  local copies, waits for them, and re-layouts  180 us (29%)
  waiting for transfers between devices  169 us (28%)
  blocking collectives  27.4 us (4%)
  between operations  14.9 us (2%)
  starting transfers between devices  13.4 us (2%)
    scatter-add x1, other arithmetic, local(): partial_normals = jnp.zeros((20, star_group), jnp.float32).at[:, in_stars...  178 us
    psum x1, waiting for transfers between devices, local(): summed = lax.psum(partial_normals, 'tm')  149 us
    gather x2, local copies, waits for them, and re-layouts, local(): owner_result = in_residual - star_fit(in_partials, group_shift[:, in_stars])  122 us
    all_gather x1, blocking collectives, local(): piece_knots = lax.all_gather(attitude, 'tm', axis=1, tiled=True)  27.4 us
    another operation x2, local copies, waits for them, and re-layouts, pair_terms(): return jnp.stack(term_list).reshape(20, -1)  17 us
    all_to_all x1, waiting for transfers between devices, local(): lax.all_to_all(outgoing, 'sky', split_axis=0, concat_axis=0, tiled=True)  14 us
    gather x2, local copies, waits for them, and re-layouts, local(): picked = piece_knots[:, jnp.clip(offsets, 0, piece_width - 1)]  13.4 us
  transfers between devices with their start and end apart: 4, of which 3 were waited for; matrix products, arithmetic and copies ran while one was open for 6% of the time, Pallas kernels for 0%

commit v1 on v0

v1 whole, which is shorter than its diff:
```python
import jax
import jax.numpy as jnp
from jax import lax
from jax.experimental import pallas as pl
from jax.experimental.pallas import tpu as pltpu
from jax.sharding import PartitionSpec as P

ROWS = 256
WIN = 64
CAP = 32
NBLK = 64
SLOTS = 128
STAR_DEV = 512
HW = 16
NHI = 64
F32 = jnp.float32
BF16 = jnp.bfloat16
I32 = jnp.int32
VM = pl.BlockSpec(memory_space=pltpu.VMEM)
SM = pl.BlockSpec(memory_space=pltpu.SMEM)


def shape(dims, dtype=F32):
    return jax.ShapeDtypeStruct(dims, dtype)


def pack_kernel(dest, count, partials, stars, out, slots, used):
    out[...] = jnp.zeros_like(out)
    out[:, 160:192, :] = jnp.full((4, 32, ROWS), -1.0, F32)
    for g in range(4):
        used[g] = 0

    def place(b, carry):
        g = dest[b]
        k = used[g]
        used[g] = k + 1
        slots[b] = g * CAP + k
        for q in range(5):
            out[g, pl.ds(q * CAP + k, 1), :] = partials[b, q:q + 1, :]
        out[g, pl.ds(5 * CAP + k, 1), :] = stars[pl.ds(b, 1), :].astype(F32)
        return carry

    lax.fori_loop(0, count[0], place, 0)

    def skip(b, carry):
        slots[b] = -1
        return carry

    lax.fori_loop(count[0], NBLK, skip, 0)


def pack(dest, count, partials, stars):
    return pl.pallas_call(
        pack_kernel,
        name="pack",
        out_shape=(shape((4, 192, ROWS)), shape((NBLK,), I32)),
        in_specs=[SM, SM, VM, VM],
        out_specs=(VM, SM),
        scratch_shapes=[pltpu.SMEM((4,), I32)],
    )(dest, count, partials, stars)


def spread_kernel(slots, count, rows, out):
    out[...] = jnp.zeros_like(out)

    def place(b, carry):
        out[pl.ds(slots[b], 1), :] = rows[pl.ds(b, 1), :]
        return carry

    lax.fori_loop(0, count[0], place, 0)


def spread(slots, count, rows):
    return pl.pallas_call(
        spread_kernel, name="spread", out_shape=shape((SLOTS, ROWS)), in_specs=[SM, SM, VM], out_specs=VM
    )(slots, count, rows)


def collect_kernel(slots, count, rows, out):
    out[...] = jnp.zeros_like(out)

    def place(b, carry):
        out[pl.ds(b, 1), :] = rows[pl.ds(slots[b], 1), :]
        return carry

    lax.fori_loop(0, count[0], place, 0)


def collect(slots, count, rows):
    return pl.pallas_call(
        collect_kernel, name="collect", out_shape=shape((NBLK, ROWS)), in_specs=[SM, SM, VM], out_specs=VM
    )(slots, count, rows)


def window_kernel(start_s, start_v, knots, out, near, far):
    def place(b, carry):
        tile = start_s[b] // 128
        after = jnp.minimum(tile + 1, 63)
        for axis in range(3):
            near[axis, pl.ds(b, 1), :] = knots[tile // 2, pl.ds(3 * (tile % 2) + axis, 1), :]
            far[axis, pl.ds(b, 1), :] = knots[after // 2, pl.ds(3 * (after % 2) + axis, 1), :]
        return carry

    lax.fori_loop(0, NBLK, place, 0)
    lane = lax.broadcasted_iota(I32, (NBLK, 128), 1)
    at = lane + (start_v[...] & 127)
    wrapped = at & 127
    got = []
    for axis in range(3):
        a = jnp.take_along_axis(near[axis], wrapped, axis=1, mode="promise_in_bounds")
        b = jnp.take_along_axis(far[axis], wrapped, axis=1, mode="promise_in_bounds")
        got.append(jnp.where(at < 128, a, b))
    out[:, :128] = jnp.where(lane < WIN, got[0], pltpu.roll(got[1], WIN, 1)).astype(BF16)
    out[:, 128:] = got[2][:, :WIN].astype(BF16)


def windows_of(win_start, knots):
    return pl.pallas_call(
        window_kernel,
        name="windows",
        out_shape=shape((NBLK, 3 * WIN), BF16),
        in_specs=[SM, VM, VM],
        out_specs=VM,
        scratch_shapes=[pltpu.VMEM((3, NBLK, 128), F32), pltpu.VMEM((3, NBLK, 128), F32)],
    )(win_start, win_start.reshape(NBLK, 1), knots)


def sort_rows(cols):
    sub = lax.broadcasted_iota(I32, (8, 128), 0)
    k = 2
    while k <= ROWS:
        j = k // 2
        while j >= 1:
            if j >= 8:
                step = j // 8
                for v in range(32):
                    w = v ^ step
                    if v < w:
                        low = jnp.minimum(cols[v], cols[w])
                        high = jnp.maximum(cols[v], cols[w])
                        up = ((v * 8) & k) == 0
                        cols[v], cols[w] = (low, high) if up else (high, low)
            else:
                first = (sub & j) == 0
                for v in range(32):
                    x = cols[v]
                    if j == 4:
                        other = pltpu.roll(x, 4, 0)
                    else:
                        other = jnp.where(first, pltpu.roll(x, 8 - j, 0), pltpu.roll(x, j, 0))
                    low = jnp.minimum(x, other)
                    high = jnp.maximum(x, other)
                    if k >= 8:
                        take_low = first if ((v * 8) & k) == 0 else jnp.logical_not(first)
                    else:
                        take_low = first == ((sub & k) == 0)
                    cols[v] = jnp.where(take_low, low, high)
            j //= 2
        k *= 2
    return cols


def pick_lanes(x, idx):
    halves = []
    for h in range(2):
        at = idx[:, h * 128:(h + 1) * 128]
        near = at & 127
        a = jnp.take_along_axis(x[:, :128], near, axis=1, mode="promise_in_bounds")
        b = jnp.take_along_axis(x[:, 128:], near, axis=1, mode="promise_in_bounds")
        halves.append(jnp.where(at < 128, a, b))
    return jnp.concatenate(halves, axis=1)


def sort_kernel(inc, sk, skt, idx, inv, ps, bounds):
    ids = jnp.concatenate([inc[s, 160:192, :] for s in range(4)], axis=0)
    key = ids * 256.0 + lax.broadcasted_iota(I32, (SLOTS, ROWS), 1).astype(F32)
    kt = key.T
    skey = jnp.concatenate(sort_rows([kt[8 * v:8 * v + 8] for v in range(32)]), axis=0).astype(I32)
    star = skey >> 8
    sk[...] = star
    place = skey & 255
    hi = star >> 8
    for c in range(32):
        h = hi[8 * c:8 * c + 8]
        s = star[8 * c:8 * c + 8]
        bounds[c] = jnp.min(jnp.where(s >= 0, h, 999))
        bounds[32 + c] = jnp.max(jnp.where(s >= 0, h, -1))
    back = (place * 256 + lax.broadcasted_iota(I32, (ROWS, SLOTS), 0)).astype(F32)
    inv_rows = sort_rows([back[8 * v:8 * v + 8] for v in range(32)])
    inv[...] = (jnp.concatenate(inv_rows, axis=0).astype(I32) & 255).T
    start = star.T
    for h in range(2):
        skt[h] = start[:, h * 128:(h + 1) * 128]
    place_t = place.T
    idx[...] = place_t
    for q in range(5):
        p = jnp.concatenate([inc[s, q * CAP:(q + 1) * CAP, :] for s in range(4)], axis=0)
        ps[q * ROWS:(q + 1) * ROWS] = pick_lanes(p, place_t).T
    ps[5 * ROWS:] = jnp.zeros((3 * ROWS, SLOTS), F32)


def sort_slots(inc):
    return pl.pallas_call(
        sort_kernel,
        name="sort",
        out_shape=(
            shape((ROWS, SLOTS), I32),
            shape((2, 128, 128), I32),
            shape((SLOTS, ROWS), I32),
            shape((SLOTS, ROWS), I32),
            shape((8 * ROWS, SLOTS)),
            shape((64,), I32),
        ),
        in_specs=[VM],
        out_specs=(VM,) * 5 + (SM,),
    )(inc)


def scatter_kernel(bounds, core, sk, skt, idx, ps, res, out, acc, rs, tall, tb, oh, lhs):
    rs[...] = pick_lanes(res[...], idx[...]).T
    acc[...] = jnp.zeros_like(acc)
    rowh = (lax.broadcasted_iota(I32, (80, 128), 0) >= 40).astype(F32).astype(BF16)
    lane = lax.broadcasted_iota(I32, (128, 256), 1).astype(F32).astype(BF16)
    zero = jnp.zeros((), BF16)
    one = jnp.ones((), BF16)

    def chunk(c, carry):
        at = pl.multiple_of(c * 8, 8)
        p = [ps[pl.ds(pl.multiple_of(q * ROWS + c * 8, 8), 8), :] for q in range(5)]
        r = rs[pl.ds(at, 8), :]
        terms = [p[i] * p[j] for i in range(5) for j in range(i, 5)] + [p[i] * r for i in range(5)]
        for t, v in enumerate(terms):
            big = v.astype(BF16).astype(F32)
            tall[pl.ds(t * 8, 8), :] = big
            tall[pl.ds((20 + t) * 8, 8), :] = v - big
        lo = pltpu.roll(skt[c // 16] & 255, 128 - (c % 16) * 8, 1).astype(F32).astype(BF16)
        for s in range(8):
            got = tall[pl.ds(s, 40, stride=8), :].astype(BF16)
            tb[:40, s * 128:(s + 1) * 128] = got
            tb[40:, s * 128:(s + 1) * 128] = got
            col = jnp.broadcast_to(lo[:, s:s + 1], (128, 256))
            oh[s * 128:(s + 1) * 128, :] = jnp.where(col == lane, one, zero)
        h_low = bounds[c]
        hi = sk[pl.ds(at, 8), :] >> 8

        def window(w, carry):
            h0 = h_low + w * HW
            rel = (hi - h0).astype(F32)
            for s in range(8):
                diff = jnp.broadcast_to(rel[s:s + 1, :], (80, 128)).astype(BF16) - rowh
                t = tb[:, s * 128:(s + 1) * 128]
                for j in range(HW // 2):
                    lhs[j * 80:(j + 1) * 80, s * 128:(s + 1) * 128] = jnp.where(diff == 2.0 * j, t, zero)
            prod = jnp.dot(lhs[...], oh[...], preferred_element_type=F32)
            acc[pl.ds(h0, HW)] += prod.reshape(HW, 40, 256)
            return carry

        lax.fori_loop(0, (bounds[32 + c] - h_low) // HW + 1, window, 0)
        return carry

    lax.fori_loop(0, 32, chunk, 0)
    me = core[0]
    for g in range(16):
        for side in range(2):
            t = 2 * g + (me if side == 0 else 1 - me)
            for a in range(2):
                block = acc[2 * t + a]
                out[side, g, a * 20:(a + 1) * 20, :] = block[:20] + block[20:]


def scatter(bounds, core, sk, skt, idx, ps, res):
    return pl.pallas_call(
        scatter_kernel,
        name="scatter",
        out_shape=shape((2, 16, 40, 256)),
        in_specs=[SM, SM] + [VM] * 5,
        out_specs=VM,
        scratch_shapes=[
            pltpu.VMEM((NHI + HW, 40, 256), F32),
            pltpu.VMEM((ROWS, SLOTS), F32),
            pltpu.VMEM((320, 128), F32),
            pltpu.VMEM((80, 1024), BF16),
            pltpu.VMEM((1024, 256), BF16),
            pltpu.VMEM((40 * HW, 1024), BF16),
        ],
    )(bounds, core, sk, skt, idx, ps, res)


def solve_kernel(parts, update, packed, total):
    total[...] = jnp.sum(parts[...], axis=0)

    def row(r):
        return jnp.concatenate([total[r:r + 1, :], total[20 + r:21 + r, :]], axis=0)

    entries = {}
    r = 0
    for i in range(5):
        for j in range(i, 5):
            entries[i, j] = row(r) + 1.0 if i == j else row(r)
            r += 1
    factor = {}
    for j in range(5):
        pivot = entries[j, j]
        for k in range(j):
            pivot = pivot - factor[j, k] * factor[j, k]
        factor[j, j] = jnp.sqrt(pivot)
        for i in range(j + 1, 5):
            running = entries[j, i]
            for k in range(j):
                running = running - factor[i, k] * factor[j, k]
            factor[i, j] = running / factor[j, j]
    forward = []
    for i in range(5):
        running = row(15 + i)
        for k in range(i):
            running = running - factor[i, k] * forward[k]
        forward.append(running / factor[i, i])
    answer = [None] * 5
    for i in reversed(range(5)):
        running = forward[i]
        for k in range(i + 1, 5):
            running = running - factor[k, i] * answer[k]
        answer[i] = running / factor[i, i]
    packed[...] = jnp.zeros_like(packed)
    for i in range(5):
        for a in range(2):
            update[i:i + 1, a * 256:(a + 1) * 256] = answer[i][a:a + 1]
            packed[8 * a + i:8 * a + i + 1, :] = answer[i][a:a + 1]


def solve(parts):
    return pl.pallas_call(
        solve_kernel,
        name="solve",
        out_shape=(shape((5, STAR_DEV)), shape((16, 256))),
        in_specs=[VM],
        out_specs=(VM, VM),
        scratch_shapes=[pltpu.VMEM((40, 256), F32)],
    )(parts)


def fit_kernel(bounds, sk, inv, ps, res, table, out, xb, oh, got, fit):
    big = table[...].astype(BF16).astype(F32)
    xb[:NHI, :8, :] = big.astype(BF16)
    xb[:NHI, 8:, :] = (table[...] - big).astype(BF16)
    xb[NHI:] = jnp.zeros((HW, 16, 256), BF16)
    lo_row = lax.broadcasted_iota(I32, (256, 128), 0).astype(F32).astype(BF16)
    zero = jnp.zeros((), BF16)
    one = jnp.ones((), BF16)

    def chunk(c, carry):
        at = pl.multiple_of(c * 8, 8)
        star = sk[pl.ds(at, 8), :]
        lo = (star & 255).astype(F32)
        hi = star >> 8
        for s in range(8):
            row = jnp.broadcast_to(lo[s:s + 1, :], (256, 128)).astype(BF16)
            oh[:, s * 128:(s + 1) * 128] = jnp.where(row == lo_row, one, zero)
        h_low = bounds[c]

        def window(w, sums):
            h0 = h_low + w * HW
            got[...] = jnp.dot(
                xb[pl.ds(h0, HW)].reshape(HW * 16, 256), oh[...], preferred_element_type=F32
            )
            new = []
            for s in range(8):
                rel = jnp.broadcast_to(hi[s:s + 1, :] - h0, (8, 128))
                total = sums[s]
                for h in range(HW):
                    y = (
                        got[h * 16:h * 16 + 8, s * 128:(s + 1) * 128]
                        + got[h * 16 + 8:h * 16 + 16, s * 128:(s + 1) * 128]
                    )
                    total = jnp.where(rel == h, y, total)
                new.append(total)
            return tuple(new)

        sums = lax.fori_loop(
            0, (bounds[32 + c] - h_low) // HW + 1, window, tuple(jnp.zeros((8, 128), F32) for s in range(8))
        )
        for s in range(8):
            p = ps[pl.ds(c * 8 + s, 8, stride=ROWS), :]
            fit[pl.ds(c * 8 + s, 1), :] = jnp.sum(p * sums[s], axis=0, keepdims=True)
        return carry

    lax.fori_loop(0, 32, chunk, 0)
    out[...] = res[...] - pick_lanes(fit[...].T, inv[...])


def apply_fit(bounds, sk, inv, ps, res, table):
    return pl.pallas_call(
        fit_kernel,
        name="fit",
        out_shape=shape((SLOTS, ROWS)),
        in_specs=[SM] + [VM] * 5,
        out_specs=VM,
        scratch_shapes=[
            pltpu.VMEM((NHI + HW, 16, 256), BF16),
            pltpu.VMEM((256, 1024), BF16),
            pltpu.VMEM((HW * 16, 1024), F32),
            pltpu.VMEM((ROWS, SLOTS), F32),
        ],
    )(bounds, sk, inv, ps, res, table)


def local(attitude, win_start, design, obs_value, star_design, star_local, block_dest, block_count):
    tm = lax.axis_size("tm")
    core = (lax.axis_index("tm") % 2).astype(I32)
    swap = [(i, i ^ 1) for i in range(tm)]
    chips = [list(range(0, tm, 2)), list(range(1, tm, 2))]

    outgoing, slots = pack(block_dest, block_count, star_design, star_local)
    incoming = lax.all_to_all(outgoing, "sky", 0, 0, tiled=True)

    piece = attitude.astype(F32).reshape(3, 2, 128).transpose(1, 0, 2).reshape(6, 128)
    piece = jnp.pad(piece, ((0, 2), (0, 0)))
    knots = lax.all_to_all(jnp.broadcast_to(piece[None], (tm, 8, 128)), "tm", 0, 0, tiled=True)
    windows = windows_of(win_start, knots)
    fitted = jnp.einsum("brc,bc->br", design, windows, preferred_element_type=F32)
    residual = obs_value - fitted
    out_res = spread(slots, block_count, residual)
    in_res = lax.all_to_all(out_res.reshape(4, CAP, ROWS), "sky", 0, 0, tiled=True).reshape(SLOTS, ROWS)

    sk, skt, idx, inv, ps, bounds = sort_slots(incoming)
    partial = scatter(bounds, core[None], sk, skt, idx, ps, in_res)
    pair_sum = partial[0] + lax.ppermute(partial[1], "tm", swap)
    parts = lax.all_to_all(pair_sum, "tm", 0, 0, tiled=True, axis_index_groups=chips)
    own_update, packed = solve(parts)
    other = lax.ppermute(packed, "tm", swap)
    both = jnp.where(core == 0, jnp.stack([packed, other]), jnp.stack([other, packed]))
    table = lax.all_to_all(
        jnp.broadcast_to(both[None], (16, 2, 16, 256)), "tm", 0, 0, tiled=True, axis_index_groups=chips
    ).reshape(NHI, 8, 256)
    updated = apply_fit(bounds, sk, inv, ps, in_res, table)
    returned = lax.all_to_all(updated.reshape(4, CAP, ROWS), "sky", 0, 0, tiled=True).reshape(SLOTS, ROWS)
    result = collect(slots, block_count, returned)
    return (result, own_update)


def solution(mesh):
    placed = (
        P(None, "tm"),
        P(("sky", "tm")),
        P(("sky", "tm"), None, None),
        P(("sky", "tm"), None),
        P(("sky", "tm"), None, None),
        P(("sky", "tm"), None),
        P(("sky", "tm")),
        P(("sky", "tm")),
    )
    return jax.shard_map(
        local,
        mesh=mesh,
        in_specs=placed,
        out_specs=(P(("sky", "tm"), None), P(None, ("sky", "tm"))),
        check_vma=False,
    )
```

time: 612 us -> 148 us (0.24)
  other arithmetic: 202 us -> 2.62 us
  local copies, waits for them, and re-layouts: 180 us -> 6.57 us
  waiting for transfers between devices: 169 us -> 7.9 us
  Pallas kernels: 0 us -> 63.4 us
  blocking collectives: 27.4 us -> 45 us
  between operations: 14.9 us -> 1.37 us
    scatter-add x1 -> x0, other arithmetic: 178 us -> none  [local(): partial_normals = jnp.zeros((20, star_group), jnp.float32).at[:, in_stars...]
    psum x1 -> x0, waiting for transfers between devices: 149 us -> none  [local(): summed = lax.psum(partial_normals, 'tm')]
    gather x5 -> x0, local copies, waits for them, and re-layouts: 136 us -> none  [the longest x2 122 us: local(): owner_result = in_residual - star_fit(in_partials, group_shift[:, in_stars])]
    pallas_call x0 -> x8, Pallas kernels: none -> 63.4 us  [the longest x1 28.7 us: scatter(): pl.pallas_call(scatter_kernel, name='scatter', out_shape=shape((2, 16, 40...]
    all_to_all x0 -> x3, blocking collectives: none -> 45 us  [the longest x1 19.6 us: local(): lax.all_to_all(pair_sum, 'tm', 0, 0, tiled=True, axis_index_groups=chips)]
    all_gather x1 -> x0, blocking collectives: 27.4 us -> none  [local(): piece_knots = lax.all_gather(attitude, 'tm', axis=1, tiled=True)]
    another operation x4 -> x0, local copies, waits for them, and re-layouts: 22.9 us -> none  [the longest x2 17 us: pair_terms(): return jnp.stack(term_list).reshape(20, -1)]
    all_to_all x3, waiting for transfers between devices: 19.4 us -> 4.42 us  [the longest x1 2.83 us: local(): incoming = lax.all_to_all(outgoing, 'sky', 0, 0, tiled=True)]
  transfers between devices with their start and end apart: 4 -> 5, of which waited for: 3 -> 5; matrix products, arithmetic and copies ran while one was open for 6% -> 5% of each run, Pallas kernels for 0% -> 9%
where the time goes in v1:
time: 148 us; the launch traced here: 147 us
  Pallas kernels  63.4 us (43%)
  blocking collectives  45 us (30%)
  starting transfers between devices  16.1 us (11%)
  waiting for transfers between devices  7.9 us (5%)
  local copies, waits for them, and re-layouts  6.57 us (4%)
  matrix products  3.72 us (3%)
  other arithmetic  2.62 us (2%)
    pallas_call x1, Pallas kernels, scatter(): pl.pallas_call(scatter_kernel, name='scatter', out_shape=shape((2, 16, 40...  28.7 us
    all_to_all x1, blocking collectives, local(): lax.all_to_all(pair_sum, 'tm', 0, 0, tiled=True, axis_index_groups=chips)  19.6 us
    pallas_call x1, Pallas kernels, apply_fit(): pl.pallas_call(fit_kernel, name='fit', out_shape=shape((SLOTS, ROWS)), in...  17.5 us
    all_to_all x1, blocking collectives, local(): lax.all_to_all(jnp.broadcast_to(both[None], (16, 2, 16, 256)), 'tm', 0, 0...  15.4 us
    all_to_all x1, blocking collectives, local(): lax.all_to_all(updated.reshape(4, CAP, ROWS), 'sky', 0, 0, tiled=True)  9.98 us
    all_to_all x1, starting transfers between devices, local(): lax.all_to_all(jnp.broadcast_to(piece[None], (tm, 8, 128)), 'tm', 0, 0, t...  8.27 us
    pallas_call x1, Pallas kernels, sort_slots(): pl.pallas_call(sort_kernel, name='sort', out_shape=(shape((ROWS, SLOTS),...  4.78 us
    all_to_all x1, starting transfers between devices, local(): incoming = lax.all_to_all(outgoing, 'sky', 0, 0, tiled=True)  4.46 us
  transfers between devices with their start and end apart: 5, of which 5 were waited for; matrix products, arithmetic and copies ran while one was open for 5% of the time, Pallas kernels for 9%

profile of v1, /device:TPU:0, one launch (start us, length us, event | category | flops | bytes accessed | tf_op | source)
XLA Modules:
  0.0 146.7 jit_solution(17327111037425084359)
XLA Ops:
  2.0 8.3 %all-to-all-start.1 = ((f32[32,8,128]{2,1,0:T(8,128)}), f32[32,8,128]{2,1,0:T(8,128)S(1)}, u32[]{:S(2)}, u32[]{:S(2)}) async-start(f32[32,8,128]{2,1,0:T(8,128)} %broadcast_in_dim.6), calls=%async_computation.1 | async-start | bytes 262144 | tf_op jit(solution)/shard_map/all_to_all | solution.py:418
  11.0 1.4 copy.15.start_v
  12.3 2.0 %copy.13.partials = f32[64,5,256]{2,1,0:T(8,128)} copy(f32[64,5,256]{2,0,1:T(8,128)} %param.12) | data formatting | bytes 655360 | tf_op args[4]
  14.3 3.3 %pack.1 = (f32[4,192,256]{2,1,0:T(8,128)}, s32[64]{0:T(128)}) custom-call(s32[64]{0:T(128)} %dest.1, s32[1]{0:T(128)S(6)} %copy.21.count, f32[64,5,256]{2,1,0:T(8,128)} %copy.13.partials, s32[64,256]{1,0:T(8,128)} %stars.1), custom_call_target="tpu_custom_call" | custom-call | tf_op jit(solution)/shard_map/pack/pallas_call | solution.py:53
  18.1 4.5 %all-to-all-start = ((f32[4,192,256]{2,1,0:T(8,128)}), f32[4,192,256]{2,1,0:T(8,128)S(1)}, u32[]{:S(2)}, u32[]{:S(2)}) async-start(f32[4,192,256]{2,1,0:T(8,128)} %get-tuple-element.13), calls=%async_computation | async-start | bytes 1572864 | tf_op jit(solution)/shard_map/all_to_all | solution.py:414
  22.6 3.5 %windows.1 = bf16[64,192]{1,0:T(8,128)(2,1)} custom-call(s32[64]{0:T(128)} %start_s.1, s32[64,1]{1,0:T(8,128)} %copy.15.start_v, f32[32,8,128]{2,1,0:T(8,128)} %copy-done.2), custom_call_target="tpu_custom_call" | custom-call | tf_op jit(solution)/shard_map/windows/pallas_call | solution.py:118
  26.0 3.7 %fusion.1 = f32[64,1,256]{2,1,0:T(1,128)S(1)} fusion(bf16[64,256,192]{1,2,0:T(8,128)(2,1)} %param.10, bf16[64,192,1]{1,0,2:T(8,128)(2,1)} %bitcast.28), kind=kOutput, calls=%fused_computation.4 | convolution fusion | flops 6291456 | bytes 6381568 | tf_op jit(solution)/shard_map/brc,bc->br/dot_general | solution.py:420
  30.4 1.9 %spread.1 = f32[128,256]{1,0:T(8,128)} custom-call(s32[64]{0:T(128)} %get-tuple-element.12.slots, s32[1]{0:T(128)S(6)} %copy.21.count, f32[64,256]{1,0:T(8,128)} %bitcast_subtract_fusion.rows), custom_call_target="tpu_custom_call" | custom-call | tf_op jit(solution)/shard_map/spread/pallas_call | solution.py:74
  32.3 2.8 %all-to-all-done.inc = f32[4,192,256]{2,1,0:T(8,128)S(1)} async-done(((f32[4,192,256]{2,1,0:T(8,128)}), f32[4,192,256]{2,1,0:T(8,128)S(1)}, u32[]{:S(2)}, u32[]{:S(2)}) %all-to-all-start) | async-done | bytes 786464 | tf_op jit(solution)/shard_map/all_to_all | solution.py:414
  35.1 3.3 %all-to-all-start.2 = ((f32[4,32,256]{2,1,0:T(8,128)}), f32[4,32,256]{2,1,0:T(8,128)S(1)}, u32[]{:S(2)}, u32[]{:S(2)}) async-start(f32[4,32,256]{2,1,0:T(8,128)} %bitcast.26), calls=%async_computation.2 | async-start | bytes 262144 | tf_op jit(solution)/shard_map/all_to_all | solution.py:423
  38.5 4.8 %sort.1 = (s32[256,128]{1,0:T(8,128)}, s32[2,128,128]{2,1,0:T(8,128)}, s32[128,256]{1,0:T(8,128)}, s32[128,256]{1,0:T(8,128)}, f32[2048,128]{1,0:T(8,128)}, /*index=5*/s32[64]{0:T(128)}) custom-call(f32[4,192,256]{2,1,0:T(8,128)} %copy-done), custom_call_target="tpu_custom_call" | custom-call | tf_op jit(solution)/shard_map/sort/pallas_call | solution.py:203
  43.3 1.1 all-to-all-done.2
  45.0 28.7 %scatter.1 = f32[2,16,40,256]{3,2,1,0:T(8,128)} custom-call(s32[64]{0:T(128)} %get-tuple-element.14.bounds, s32[1]{0:T(128)} %bitcast.7.core, s32[256,128]{1,0:T(8,128)} %get-tuple-element.15.sk, s32[2,128,128]{2,1,0:T(8,128)} %get-tuple-element.18.skt, s32[128,256]{1,0:T(8,128)} %get-tuple-element.19.idx, f32[2048,128]{1,0:T(8,128)} %get-tuple-element.17.ps, ...), custom_call_target="tpu_custom_call" | custom-call | tf_op jit(solution)/shard_map/scatter/pallas_call | solution.py:272
  73.7 1.1 slice_bitcast_fusion
  75.0 2.1 %collective-permute-done = f32[16,40,256]{2,1,0:T(8,128)S(1)} collective-permute-done((f32[16,40,256]{2,1,0:T(8,128)S(1)}, f32[16,40,256]{2,1,0:T(8,128)S(1)}, u32[]{:S(2)}, u32[]{:S(2)}) %collective-permute-start) | collective-permute-done | bytes 655392 | tf_op jit(solution)/shard_map/ppermute | solution.py:427
  77.0 1.2 fusion
  78.2 19.6 %all_to_all.30.parts = f32[16,40,256]{2,1,0:T(8,128)} all-to-all(f32[16,40,256]{2,1,0:T(8,128)S(1)} %fusion), channel_id=1, replica_groups={{0,2,4,6,8,10,12,14,16,18,20,22,24,26,28,30},{1,3,5,7,9,11,13,15,17,19,..., dimensions={0} | all-to-all | bytes 1310720 | tf_op jit(solution)/shard_map/all_to_all | solution.py:428
  97.8 1.8 %solve.1 = (f32[5,512]{1,0:T(8,128)}, f32[16,256]{1,0:T(8,128)}) custom-call(f32[16,40,256]{2,1,0:T(8,128)} %all_to_all.30.parts), custom_call_target="tpu_custom_call" | custom-call | tf_op jit(solution)/shard_map/solve/pallas_call | solution.py:332
  99.6 1.4 collective-permute-done.1
  101.0 0.8 maximum_select_fusion
  101.9 15.4 %all_to_all.31 = f32[16,2,16,256]{3,2,1,0:T(8,128)} all-to-all(f32[16,2,16,256]{3,2,1,0:T(8,128)S(1)} %broadcast_in_dim.8), channel_id=1, replica_groups={{0,2,4,6,8,10,12,14,16,18,20,22,24,26,28,30},{1,3,5,7,9,11,13,15,17,19,..., dimensions={0} | all-to-all | bytes 1048576 | tf_op jit(solution)/shard_map/all_to_all | solution.py:432
  117.3 17.5 %fit.1 = f32[128,256]{1,0:T(8,128)} custom-call(s32[64]{0:T(128)} %get-tuple-element.14.bounds, s32[256,128]{1,0:T(8,128)} %get-tuple-element.15.sk, s32[128,256]{1,0:T(8,128)} %get-tuple-element.16.inv, f32[2048,128]{1,0:T(8,128)} %get-tuple-element.17.ps, f32[128,256]{1,0:T(8,128)} %bitcast.24, f32[64,8,256]{2,1,0:T(8,128)} %bitcast.22), custom_call_target="tpu_custom_call" | custom-call | tf_op jit(solution)/shard_map/fit/pallas_call | solution.py:392
  134.8 10.0 %all_to_all.32 = f32[4,32,256]{2,1,0:T(8,128)} all-to-all(f32[4,32,256]{2,1,0:T(8,128)} %bitcast.25), channel_id=1, replica_groups=mesh['sky'=4,'tm'=32] {'sky'}, dimensions={0} | all-to-all | bytes 262144 | tf_op jit(solution)/shard_map/all_to_all | solution.py:436
  144.8 1.9 %collect.1 = f32[64,256]{1,0:T(8,128)} custom-call(s32[64]{0:T(128)} %get-tuple-element.12.slots, s32[1]{0:T(128)S(6)} %copy.21.count, f32[128,256]{1,0:T(8,128)} %bitcast.27), custom_call_target="tpu_custom_call" | custom-call | tf_op jit(solution)/shard_map/collect/pallas_call | solution.py:90
  (16 shorter events, 3.3 us)
Async XLA Ops:
  0.6 29.1 %copy-start.3 = (f32[64,256]{1,0:T(8,128)S(1)}, f32[64,256]{1,0:T(8,128)}, u32[]{:S(2)}) copy-start(f32[64,256]{1,0:T(8,128)} %param.11) | copy-start | bytes 196612
  2.0 16.1 %all-to-all-start.1 = ((f32[32,8,128]{2,1,0:T(8,128)}), f32[32,8,128]{2,1,0:T(8,128)S(1)}, u32[]{:S(2)}, u32[]{:S(2)}) async-start(f32[32,8,128]{2,1,0:T(8,128)} %broadcast_in_dim.6), calls=%async_computation.1 | async-start | bytes 262144 | tf_op jit(solution)/shard_map/all_to_all | solution.py:418
  18.1 4.5 %copy-start.2 = (f32[32,8,128]{2,1,0:T(8,128)}, f32[32,8,128]{2,1,0:T(8,128)S(1)}, u32[]{:S(2)}) copy-start(f32[32,8,128]{2,1,0:T(8,128)S(1)} %all-to-all-done.1.knots) | copy-start | bytes 393220
  18.1 17.0 %all-to-all-start = ((f32[4,192,256]{2,1,0:T(8,128)}), f32[4,192,256]{2,1,0:T(8,128)S(1)}, u32[]{:S(2)}, u32[]{:S(2)}) async-start(f32[4,192,256]{2,1,0:T(8,128)} %get-tuple-element.13), calls=%async_computation | async-start | bytes 1572864 | tf_op jit(solution)/shard_map/all_to_all | solution.py:414
  35.1 3.3 %copy-start = (f32[4,192,256]{2,1,0:T(8,128)}, f32[4,192,256]{2,1,0:T(8,128)S(1)}, u32[]{:S(2)}) copy-start(f32[4,192,256]{2,1,0:T(8,128)S(1)} %all-to-all-done.inc) | copy-start | bytes 2359300
  35.1 9.3 %all-to-all-start.2 = ((f32[4,32,256]{2,1,0:T(8,128)}), f32[4,32,256]{2,1,0:T(8,128)S(1)}, u32[]{:S(2)}, u32[]{:S(2)}) async-start(f32[4,32,256]{2,1,0:T(8,128)} %bitcast.26), calls=%async_computation.2 | async-start | bytes 262144 | tf_op jit(solution)/shard_map/all_to_all | solution.py:423
  44.4 0.6 copy-start.1
  74.9 2.2 %collective-permute-start = (f32[16,40,256]{2,1,0:T(8,128)S(1)}, f32[16,40,256]{2,1,0:T(8,128)S(1)}, u32[]{:S(2)}, u32[]{:S(2)}) collective-permute-start(f32[16,40,256]{2,1,0:T(8,128)S(1)} %slice_bitcast_fusion), channel_id=1, source_target_pairs={{0,1},{1,0},{2,3},{3,2},{4,5},{5,4},{6,7},{7,6},{8,9},{9,8},{10,11... | collective-permute-start | bytes 1966088 | tf_op jit(solution)/shard_map/ppermute | solution.py:427
  99.6 1.4 collective-permute-start.1

commit v2 on v1

--- a/solution.py
+++ b/solution.py
@@ -36,7 +36,7 @@
         used[g] = k + 1
         slots[b] = g * CAP + k
         for q in range(5):
-            out[g, pl.ds(q * CAP + k, 1), :] = partials[b, q:q + 1, :]
+            out[g, pl.ds(q * CAP + k, 1), :] = partials[q, pl.ds(b, 1), :]
         out[g, pl.ds(5 * CAP + k, 1), :] = stars[pl.ds(b, 1), :].astype(F32)
         return carry
 
@@ -92,9 +92,10 @@
     )(slots, count, rows)
 
 
-def window_kernel(start_s, start_v, knots, out, near, far):
+def window_kernel(start, knots, out, near, far, shift):
     def place(b, carry):
-        tile = start_s[b] // 128
+        tile = start[b] // 128
+        shift[pl.ds(b, 1), :] = jnp.full((1, 128), start[b] % 128, I32)
         after = jnp.minimum(tile + 1, 63)
         for axis in range(3):
             near[axis, pl.ds(b, 1), :] = knots[tile // 2, pl.ds(3 * (tile % 2) + axis, 1), :]
@@ -103,7 +104,7 @@
 
     lax.fori_loop(0, NBLK, place, 0)
     lane = lax.broadcasted_iota(I32, (NBLK, 128), 1)
-    at = lane + (start_v[...] & 127)
+    at = lane + shift[...]
     wrapped = at & 127
     got = []
     for axis in range(3):
@@ -119,10 +120,14 @@
         window_kernel,
         name="windows",
         out_shape=shape((NBLK, 3 * WIN), BF16),
-        in_specs=[SM, VM, VM],
+        in_specs=[SM, VM],
         out_specs=VM,
-        scratch_shapes=[pltpu.VMEM((3, NBLK, 128), F32), pltpu.VMEM((3, NBLK, 128), F32)],
-    )(win_start, win_start.reshape(NBLK, 1), knots)
+        scratch_shapes=[
+            pltpu.VMEM((3, NBLK, 128), F32),
+            pltpu.VMEM((3, NBLK, 128), F32),
+            pltpu.VMEM((NBLK, 128), I32),
+        ],
+    )(win_start, knots)
 
 
 def sort_rows(cols):
@@ -183,7 +188,8 @@
     for c in range(32):
         h = hi[8 * c:8 * c + 8]
         s = star[8 * c:8 * c + 8]
-        bounds[c] = jnp.min(jnp.where(s >= 0, h, 999))
+        first = jnp.min(jnp.where(s >= 0, h, NHI - HW))
+        bounds[c] = jnp.minimum(first - first % 2, NHI - HW)
         bounds[32 + c] = jnp.max(jnp.where(s >= 0, h, -1))
     back = (place * 256 + lax.broadcasted_iota(I32, (ROWS, SLOTS), 0)).astype(F32)
     inv_rows = sort_rows([back[8 * v:8 * v + 8] for v in range(32)])
@@ -196,7 +202,6 @@
     for q in range(5):
         p = jnp.concatenate([inc[s, q * CAP:(q + 1) * CAP, :] for s in range(4)], axis=0)
         ps[q * ROWS:(q + 1) * ROWS] = pick_lanes(p, place_t).T
-    ps[5 * ROWS:] = jnp.zeros((3 * ROWS, SLOTS), F32)
 
 
 def sort_slots(inc):
@@ -208,7 +213,7 @@
             shape((2, 128, 128), I32),
             shape((SLOTS, ROWS), I32),
             shape((SLOTS, ROWS), I32),
-            shape((8 * ROWS, SLOTS)),
+            shape((5 * ROWS, SLOTS)),
             shape((64,), I32),
         ),
         in_specs=[VM],
@@ -216,72 +221,75 @@
     )(inc)
 
 
-def scatter_kernel(bounds, core, sk, skt, idx, ps, res, out, acc, rs, tall, tb, oh, lhs):
+def scatter_kernel(bounds, core, sk, skt, idx, ps, res, mine, theirs, acc, rs, tall, oh):
     rs[...] = pick_lanes(res[...], idx[...]).T
     acc[...] = jnp.zeros_like(acc)
-    rowh = (lax.broadcasted_iota(I32, (80, 128), 0) >= 40).astype(F32).astype(BF16)
+    rowh = (lax.broadcasted_iota(I32, (80, 128), 0) // 20).astype(F32).astype(BF16)
     lane = lax.broadcasted_iota(I32, (128, 256), 1).astype(F32).astype(BF16)
     zero = jnp.zeros((), BF16)
     one = jnp.ones((), BF16)
 
-    def chunk(c, carry):
+    def add_window(c, h_from, h0):
         at = pl.multiple_of(c * 8, 8)
         p = [ps[pl.ds(pl.multiple_of(q * ROWS + c * 8, 8), 8), :] for q in range(5)]
         r = rs[pl.ds(at, 8), :]
         terms = [p[i] * p[j] for i in range(5) for j in range(i, 5)] + [p[i] * r for i in range(5)]
         for t, v in enumerate(terms):
             big = v.astype(BF16).astype(F32)
-            tall[pl.ds(t * 8, 8), :] = big
-            tall[pl.ds((20 + t) * 8, 8), :] = v - big
+            small = v - big
+            tall[t * 8:t * 8 + 8, :] = big
+            tall[192 + t * 8:192 + t * 8 + 8, :] = small
+            if t < 4:
+                tall[160 + t * 8:160 + t * 8 + 8, :] = big
+                tall[352 + t * 8:352 + t * 8 + 8, :] = small
         lo = pltpu.roll(skt[c // 16] & 255, 128 - (c % 16) * 8, 1).astype(F32).astype(BF16)
+        hi = sk[pl.ds(at, 8), :] >> 8
+        rel = jnp.where(hi >= h_from, hi - h0, -1).astype(F32)
+        columns = [[], []]
         for s in range(8):
-            got = tall[pl.ds(s, 40, stride=8), :].astype(BF16)
-            tb[:40, s * 128:(s + 1) * 128] = got
-            tb[40:, s * 128:(s + 1) * 128] = got
             col = jnp.broadcast_to(lo[:, s:s + 1], (128, 256))
             oh[s * 128:(s + 1) * 128, :] = jnp.where(col == lane, one, zero)
+            diff = jnp.broadcast_to(rel[s:s + 1, :], (80, 128)).astype(BF16) - rowh
+            hit = [diff == 4.0 * j for j in range(HW // 4)]
+            for part in range(2):
+                five = [tall[pl.ds(192 * part + 8 * o + s, 8, stride=8), :] for o in (0, 8, 16, 4, 12)]
+                t = jnp.concatenate(five + five, axis=0).astype(BF16)
+                columns[part].append(jnp.concatenate([jnp.where(m, t, zero) for m in hit], axis=0))
+        lhs = jnp.concatenate(columns[0] + columns[1], axis=1)
+        rhs = jnp.concatenate([oh[...], oh[...]], axis=0)
+        acc[pl.ds(pl.multiple_of(h0 * 20, 8), HW * 20), :] += jnp.dot(lhs, rhs, preferred_element_type=F32)
+
+    def chunk(c, carry):
         h_low = bounds[c]
-        hi = sk[pl.ds(at, 8), :] >> 8
-
-        def window(w, carry):
-            h0 = h_low + w * HW
-            rel = (hi - h0).astype(F32)
-            for s in range(8):
-                diff = jnp.broadcast_to(rel[s:s + 1, :], (80, 128)).astype(BF16) - rowh
-                t = tb[:, s * 128:(s + 1) * 128]
-                for j in range(HW // 2):
-                    lhs[j * 80:(j + 1) * 80, s * 128:(s + 1) * 128] = jnp.where(diff == 2.0 * j, t, zero)
-            prod = jnp.dot(lhs[...], oh[...], preferred_element_type=F32)
-            acc[pl.ds(h0, HW)] += prod.reshape(HW, 40, 256)
+        add_window(c, h_low, h_low)
+
+        def more(w, carry):
+            h_from = h_low + w * HW
+            add_window(c, h_from, jnp.minimum(h_from, NHI - HW))
             return carry
 
-        lax.fori_loop(0, (bounds[32 + c] - h_low) // HW + 1, window, 0)
+        lax.fori_loop(1, (bounds[32 + c] - h_low) // HW + 1, more, 0)
         return carry
 
     lax.fori_loop(0, 32, chunk, 0)
     me = core[0]
     for g in range(16):
-        for side in range(2):
-            t = 2 * g + (me if side == 0 else 1 - me)
-            for a in range(2):
-                block = acc[2 * t + a]
-                out[side, g, a * 20:(a + 1) * 20, :] = block[:20] + block[20:]
+        mine[g] = acc[pl.ds(pl.multiple_of((2 * g + me) * 40, 8), 40), :]
+        theirs[g] = acc[pl.ds(pl.multiple_of((2 * g + 1 - me) * 40, 8), 40), :]
 
 
 def scatter(bounds, core, sk, skt, idx, ps, res):
     return pl.pallas_call(
         scatter_kernel,
         name="scatter",
-        out_shape=shape((2, 16, 40, 256)),
+        out_shape=(shape((16, 40, 256)), shape((16, 40, 256))),
         in_specs=[SM, SM] + [VM] * 5,
-        out_specs=VM,
+        out_specs=(VM, VM),
         scratch_shapes=[
-            pltpu.VMEM((NHI + HW, 40, 256), F32),
+            pltpu.VMEM((NHI * 20, 256), F32),
             pltpu.VMEM((ROWS, SLOTS), F32),
-            pltpu.VMEM((320, 128), F32),
-            pltpu.VMEM((80, 1024), BF16),
+            pltpu.VMEM((384, 128), F32),
             pltpu.VMEM((1024, 256), BF16),
-            pltpu.VMEM((40 * HW, 1024), BF16),
         ],
     )(bounds, core, sk, skt, idx, ps, res)
 
@@ -339,49 +347,34 @@
     )(parts)
 
 
-def fit_kernel(bounds, sk, inv, ps, res, table, out, xb, oh, got, fit):
-    big = table[...].astype(BF16).astype(F32)
-    xb[:NHI, :8, :] = big.astype(BF16)
-    xb[:NHI, 8:, :] = (table[...] - big).astype(BF16)
-    xb[NHI:] = jnp.zeros((HW, 16, 256), BF16)
-    lo_row = lax.broadcasted_iota(I32, (256, 128), 0).astype(F32).astype(BF16)
-    zero = jnp.zeros((), BF16)
-    one = jnp.ones((), BF16)
+def fit_kernel(bounds, sk, inv, ps, res, table, out, fit):
+    def look_up(c, h0, found):
+        star = sk[pl.ds(pl.multiple_of(c * 8, 8), 8), :]
+        at = star & 127
+        rel = (star >> 7) - 2 * h0
+        found = list(found)
+        for k in range(2 * HW):
+            hit = rel == k
+            for q in range(5):
+                row = table[h0 + k // 2, q:q + 1, (k % 2) * 128:(k % 2) * 128 + 128]
+                value = jnp.take_along_axis(
+                    jnp.broadcast_to(row, (8, 128)), at, axis=1, mode="promise_in_bounds"
+                )
+                found[q] = jnp.where(hit, value, found[q])
+        return tuple(found)
 
     def chunk(c, carry):
-        at = pl.multiple_of(c * 8, 8)
-        star = sk[pl.ds(at, 8), :]
-        lo = (star & 255).astype(F32)
-        hi = star >> 8
-        for s in range(8):
-            row = jnp.broadcast_to(lo[s:s + 1, :], (256, 128)).astype(BF16)
-            oh[:, s * 128:(s + 1) * 128] = jnp.where(row == lo_row, one, zero)
         h_low = bounds[c]
-
-        def window(w, sums):
-            h0 = h_low + w * HW
-            got[...] = jnp.dot(
-                xb[pl.ds(h0, HW)].reshape(HW * 16, 256), oh[...], preferred_element_type=F32
-            )
-            new = []
-            for s in range(8):
-                rel = jnp.broadcast_to(hi[s:s + 1, :] - h0, (8, 128))
-                total = sums[s]
-                for h in range(HW):
-                    y = (
-                        got[h * 16:h * 16 + 8, s * 128:(s + 1) * 128]
-                        + got[h * 16 + 8:h * 16 + 16, s * 128:(s + 1) * 128]
-                    )
-                    total = jnp.where(rel == h, y, total)
-                new.append(total)
-            return tuple(new)
-
-        sums = lax.fori_loop(
-            0, (bounds[32 + c] - h_low) // HW + 1, window, tuple(jnp.zeros((8, 128), F32) for s in range(8))
-        )
-        for s in range(8):
-            p = ps[pl.ds(c * 8 + s, 8, stride=ROWS), :]
-            fit[pl.ds(c * 8 + s, 1), :] = jnp.sum(p * sums[s], axis=0, keepdims=True)
+        found = look_up(c, h_low, (jnp.zeros((8, 128), F32),) * 5)
+
+        def more(w, found):
+            return look_up(c, jnp.minimum(h_low + w * HW, NHI - HW), found)
+
+        found = lax.fori_loop(1, (bounds[32 + c] - h_low) // HW + 1, more, found)
+        total = jnp.zeros((8, 128), F32)
+        for q in range(5):
+            total = total + ps[pl.ds(pl.multiple_of(q * ROWS + c * 8, 8), 8), :] * found[q]
+        fit[pl.ds(pl.multiple_of(c * 8, 8), 8), :] = total
         return carry
 
     lax.fori_loop(0, 32, chunk, 0)
@@ -395,12 +388,7 @@
         out_shape=shape((SLOTS, ROWS)),
         in_specs=[SM] + [VM] * 5,
         out_specs=VM,
-        scratch_shapes=[
-            pltpu.VMEM((NHI + HW, 16, 256), BF16),
-            pltpu.VMEM((256, 1024), BF16),
-            pltpu.VMEM((HW * 16, 1024), F32),
-            pltpu.VMEM((ROWS, SLOTS), F32),
-        ],
+        scratch_shapes=[pltpu.VMEM((ROWS, SLOTS), F32)],
     )(bounds, sk, inv, ps, res, table)
 
 
@@ -410,7 +398,7 @@
     swap = [(i, i ^ 1) for i in range(tm)]
     chips = [list(range(0, tm, 2)), list(range(1, tm, 2))]
 
-    outgoing, slots = pack(block_dest, block_count, star_design, star_local)
+    outgoing, slots = pack(block_dest, block_count, star_design.transpose(1, 0, 2), star_local)
     incoming = lax.all_to_all(outgoing, "sky", 0, 0, tiled=True)
 
     piece = attitude.astype(F32).reshape(3, 2, 128).transpose(1, 0, 2).reshape(6, 128)
@@ -423,8 +411,8 @@
     in_res = lax.all_to_all(out_res.reshape(4, CAP, ROWS), "sky", 0, 0, tiled=True).reshape(SLOTS, ROWS)
 
     sk, skt, idx, inv, ps, bounds = sort_slots(incoming)
-    partial = scatter(bounds, core[None], sk, skt, idx, ps, in_res)
-    pair_sum = partial[0] + lax.ppermute(partial[1], "tm", swap)
+    mine, theirs = scatter(bounds, core[None], sk, skt, idx, ps, in_res)
+    pair_sum = mine + lax.ppermute(theirs, "tm", swap)
     parts = lax.all_to_all(pair_sum, "tm", 0, 0, tiled=True, axis_index_groups=chips)
     own_update, packed = solve(parts)
     other = lax.ppermute(packed, "tm", swap)

time: 148 us -> 132 us (0.89)
  Pallas kernels: 63.4 us -> 51 us
  local copies, waits for them, and re-layouts: 6.57 us -> 2.11 us
  waiting for transfers between devices: 7.9 us -> 12.1 us
  blocking collectives: 45 us -> 42.5 us
    pallas_call x1, Pallas kernels: 17.5 us -> 10.3 us  [apply_fit(): pl.pallas_call(fit_kernel, name='fit', out_shape=shape((SLOTS, ROWS)), in...]
    pallas_call x1, Pallas kernels: 28.7 us -> 24.3 us  [scatter(): pl.pallas_call(scatter_kernel, name='scatter', out_shape=(shape((16, 40,...]
    all_to_all x1, waiting for transfers between devices: 0.46 us -> 4.19 us  [local(): lax.all_to_all(jnp.broadcast_to(piece[None], (tm, 8, 128)), 'tm', 0, 0, t...]
    all_to_all x1, blocking collectives: 19.6 us -> 17.1 us  [local(): lax.all_to_all(pair_sum, 'tm', 0, 0, tiled=True, axis_index_groups=chips)]
    unnamed x9 -> x8, local copies, waits for them, and re-layouts: 2.64 us -> 0.67 us
  transfers between devices with their start and end apart: 5 -> 5, of which waited for: 5 -> 5; matrix products, arithmetic and copies ran while one was open for 5% -> 3% of each run, Pallas kernels for 9% -> 10%
where the time goes in v2:
time: 132 us; the launch traced here: 131 us
  Pallas kernels  51 us (39%)
  blocking collectives  42.5 us (32%)
  starting transfers between devices  16.1 us (12%)
  waiting for transfers between devices  12.1 us (9%)
  matrix products  3.72 us (3%)
  other arithmetic  2.62 us (2%)
  local copies, waits for them, and re-layouts  2.11 us (2%)
  between operations  1.36 us (1%)
    pallas_call x1, Pallas kernels, scatter(): pl.pallas_call(scatter_kernel, name='scatter', out_shape=(shape((16, 40,...  24.3 us
    all_to_all x1, blocking collectives, local(): lax.all_to_all(pair_sum, 'tm', 0, 0, tiled=True, axis_index_groups=chips)  17.1 us
    all_to_all x1, blocking collectives, local(): lax.all_to_all(jnp.broadcast_to(both[None], (16, 2, 16, 256)), 'tm', 0, 0...  15.4 us
    pallas_call x1, Pallas kernels, apply_fit(): pl.pallas_call(fit_kernel, name='fit', out_shape=shape((SLOTS, ROWS)), in...  10.3 us
    all_to_all x1, blocking collectives, local(): lax.all_to_all(updated.reshape(4, CAP, ROWS), 'sky', 0, 0, tiled=True)  9.97 us
    all_to_all x1, starting transfers between devices, local(): lax.all_to_all(jnp.broadcast_to(piece[None], (tm, 8, 128)), 'tm', 0, 0, t...  8.27 us
    pallas_call x1, Pallas kernels, sort_slots(): pl.pallas_call(sort_kernel, name='sort', out_shape=(shape((ROWS, SLOTS),...  4.67 us
    all_to_all x1, starting transfers between devices, local(): incoming = lax.all_to_all(outgoing, 'sky', 0, 0, tiled=True)  4.46 us
  transfers between devices with their start and end apart: 5, of which 5 were waited for; matrix products, arithmetic and copies ran while one was open for 3% of the time, Pallas kernels for 10%

profile of v2, /device:TPU:0, one launch (start us, length us, event | category | flops | bytes accessed | tf_op | source)
XLA Modules:
  0.0 131.5 jit_solution(14223908210138055798)
XLA Ops:
  0.6 0.7 reshape.62
  2.0 8.3 %all-to-all-start.1 = ((f32[32,8,128]{2,1,0:T(8,128)}), f32[32,8,128]{2,1,0:T(8,128)S(1)}, u32[]{:S(2)}, u32[]{:S(2)}) async-start(f32[32,8,128]{2,1,0:T(8,128)} %broadcast_in_dim.6), calls=%async_computation.1 | async-start | bytes 262144 | tf_op jit(solution)/shard_map/all_to_all | solution.py:406
  11.0 2.9 %pack.1 = (f32[4,192,256]{2,1,0:T(8,128)}, s32[64]{0:T(128)}) custom-call(s32[64]{0:T(128)} %dest.1, s32[1]{0:T(128)S(6)} %copy.17.count, f32[5,64,256]{2,1,0:T(8,128)} %bitcast.22, s32[64,256]{1,0:T(8,128)} %stars.1), custom_call_target="tpu_custom_call" | custom-call | tf_op jit(solution)/shard_map/pack/pallas_call | solution.py:53
  13.9 4.2 %all-to-all-done.1.knots = f32[32,8,128]{2,1,0:T(8,128)S(1)} async-done(((f32[32,8,128]{2,1,0:T(8,128)}), f32[32,8,128]{2,1,0:T(8,128)S(1)}, u32[]{:S(2)}, u32[]{:S(2)}) %all-to-all-start.1) | async-done | bytes 131104 | tf_op jit(solution)/shard_map/all_to_all | solution.py:406
  18.1 4.5 %all-to-all-start = ((f32[4,192,256]{2,1,0:T(8,128)}), f32[4,192,256]{2,1,0:T(8,128)S(1)}, u32[]{:S(2)}, u32[]{:S(2)}) async-start(f32[4,192,256]{2,1,0:T(8,128)} %get-tuple-element.15), calls=%async_computation | async-start | bytes 1572864 | tf_op jit(solution)/shard_map/all_to_all | solution.py:402
  22.6 3.4 %windows.1 = bf16[64,192]{1,0:T(8,128)(2,1)} custom-call(s32[64]{0:T(128)} %start.1, f32[32,8,128]{2,1,0:T(8,128)} %copy-done.2), custom_call_target="tpu_custom_call" | custom-call | tf_op jit(solution)/shard_map/windows/pallas_call | solution.py:119
  26.0 3.7 %fusion = f32[64,1,256]{2,1,0:T(1,128)S(1)} fusion(bf16[64,256,192]{1,2,0:T(8,128)(2,1)} %param.10, bf16[64,192,1]{1,0,2:T(8,128)(2,1)} %bitcast.23), kind=kOutput, calls=%fused_computation.1 | convolution fusion | flops 6291456 | bytes 6381568 | tf_op jit(solution)/shard_map/brc,bc->br/dot_general | solution.py:408
  30.4 1.7 %spread.1 = f32[128,256]{1,0:T(8,128)} custom-call(s32[64]{0:T(128)} %get-tuple-element.14.slots, s32[1]{0:T(128)S(6)} %copy.17.count, f32[64,256]{1,0:T(8,128)} %bitcast_subtract_fusion.rows), custom_call_target="tpu_custom_call" | custom-call | tf_op jit(solution)/shard_map/spread/pallas_call | solution.py:74
  32.1 3.0 %all-to-all-done.inc = f32[4,192,256]{2,1,0:T(8,128)S(1)} async-done(((f32[4,192,256]{2,1,0:T(8,128)}), f32[4,192,256]{2,1,0:T(8,128)S(1)}, u32[]{:S(2)}, u32[]{:S(2)}) %all-to-all-start) | async-done | bytes 786464 | tf_op jit(solution)/shard_map/all_to_all | solution.py:402
  35.1 3.3 %all-to-all-start.2 = ((f32[4,32,256]{2,1,0:T(8,128)}), f32[4,32,256]{2,1,0:T(8,128)S(1)}, u32[]{:S(2)}, u32[]{:S(2)}) async-start(f32[4,32,256]{2,1,0:T(8,128)} %bitcast.20), calls=%async_computation.2 | async-start | bytes 262144 | tf_op jit(solution)/shard_map/all_to_all | solution.py:411
  38.5 4.7 %sort.1 = (s32[256,128]{1,0:T(8,128)}, s32[2,128,128]{2,1,0:T(8,128)}, s32[128,256]{1,0:T(8,128)}, s32[128,256]{1,0:T(8,128)}, f32[1280,128]{1,0:T(8,128)}, /*index=5*/s32[64]{0:T(128)}) custom-call(f32[4,192,256]{2,1,0:T(8,128)} %copy-done), custom_call_target="tpu_custom_call" | custom-call | tf_op jit(solution)/shard_map/sort/pallas_call | solution.py:208
  43.1 1.2 all-to-all-done.2
  44.4 0.7 copy-done.1
  45.0 24.3 %scatter.1 = (f32[16,40,256]{2,1,0:T(8,128)}, f32[16,40,256]{2,1,0:T(8,128)}) custom-call(s32[64]{0:T(128)} %get-tuple-element.16.bounds, s32[1]{0:T(128)} %bitcast.7.core, s32[256,128]{1,0:T(8,128)} %get-tuple-element.17.sk, s32[2,128,128]{2,1,0:T(8,128)} %get-tuple-element.20.skt, s32[128,256]{1,0:T(8,128)} %get-tuple-element.21.idx, ...), custom_call_target="tpu_custom_call" | custom-call | tf_op jit(solution)/shard_map/scatter/pallas_call | solution.py:282
  69.3 2.3 %collective-permute-done = f32[16,40,256]{2,1,0:T(8,128)S(1)} collective-permute-done((f32[16,40,256]{2,1,0:T(8,128)}, f32[16,40,256]{2,1,0:T(8,128)S(1)}, u32[]{:S(2)}, u32[]{:S(2)}) %collective-permute-start) | collective-permute-done | bytes 655392 | tf_op jit(solution)/shard_map/ppermute | solution.py:415
  71.6 1.2 add.10
  72.8 17.1 %all_to_all.30.parts = f32[16,40,256]{2,1,0:T(8,128)} all-to-all(f32[16,40,256]{2,1,0:T(8,128)S(1)} %add.10), channel_id=1, replica_groups={{0,2,4,6,8,10,12,14,16,18,20,22,24,26,28,30},{1,3,5,7,9,11,13,15,17,19,..., dimensions={0} | all-to-all | bytes 1310720 | tf_op jit(solution)/shard_map/all_to_all | solution.py:416
  89.9 1.8 %solve.1 = (f32[5,512]{1,0:T(8,128)}, f32[16,256]{1,0:T(8,128)}) custom-call(f32[16,40,256]{2,1,0:T(8,128)} %all_to_all.30.parts), custom_call_target="tpu_custom_call" | custom-call | tf_op jit(solution)/shard_map/solve/pallas_call | solution.py:340
  91.7 1.4 %collective-permute-done.1 = f32[16,256]{1,0:T(8,128)S(1)} collective-permute-done((f32[16,256]{1,0:T(8,128)}, f32[16,256]{1,0:T(8,128)S(1)}, u32[]{:S(2)}, u32[]{:S(2)}) %collective-permute-start.1) | collective-permute-done | bytes 16416 | tf_op jit(solution)/shard_map/ppermute | solution.py:418
  93.1 0.8 maximum_select_fusion
  94.0 15.4 %all_to_all.31 = f32[16,2,16,256]{3,2,1,0:T(8,128)} all-to-all(f32[16,2,16,256]{3,2,1,0:T(8,128)S(1)} %broadcast_in_dim.8), channel_id=1, replica_groups={{0,2,4,6,8,10,12,14,16,18,20,22,24,26,28,30},{1,3,5,7,9,11,13,15,17,19,..., dimensions={0} | all-to-all | bytes 1048576 | tf_op jit(solution)/shard_map/all_to_all | solution.py:420
  109.4 10.3 %fit.1 = f32[128,256]{1,0:T(8,128)} custom-call(s32[64]{0:T(128)} %get-tuple-element.16.bounds, s32[256,128]{1,0:T(8,128)} %get-tuple-element.17.sk, s32[128,256]{1,0:T(8,128)} %get-tuple-element.18.inv, f32[1280,128]{1,0:T(8,128)} %get-tuple-element.19.ps, f32[128,256]{1,0:T(8,128)} %bitcast.18, f32[64,8,256]{2,1,0:T(8,128)} %bitcast.16), custom_call_target="tpu_custom_call" | custom-call | tf_op jit(solution)/shard_map/fit/pallas_call | solution.py:385
  119.7 10.0 %all_to_all.32 = f32[4,32,256]{2,1,0:T(8,128)} all-to-all(f32[4,32,256]{2,1,0:T(8,128)} %bitcast.19), channel_id=1, replica_groups=mesh['sky'=4,'tm'=32] {'sky'}, dimensions={0} | all-to-all | bytes 262144 | tf_op jit(solution)/shard_map/all_to_all | solution.py:424
  129.7 1.8 %collect.1 = f32[64,256]{1,0:T(8,128)} custom-call(s32[64]{0:T(128)} %get-tuple-element.14.slots, s32[1]{0:T(128)S(6)} %copy.17.count, f32[128,256]{1,0:T(8,128)} %bitcast.21), custom_call_target="tpu_custom_call" | custom-call | tf_op jit(solution)/shard_map/collect/pallas_call | solution.py:90
  (13 shorter events, 1.4 us)
Async XLA Ops:
  0.6 29.1 %copy-start.3 = (f32[64,256]{1,0:T(8,128)S(1)}, f32[64,256]{1,0:T(8,128)}, u32[]{:S(2)}) copy-start(f32[64,256]{1,0:T(8,128)} %param.11) | copy-start | bytes 196612
  2.0 16.1 %all-to-all-start.1 = ((f32[32,8,128]{2,1,0:T(8,128)}), f32[32,8,128]{2,1,0:T(8,128)S(1)}, u32[]{:S(2)}, u32[]{:S(2)}) async-start(f32[32,8,128]{2,1,0:T(8,128)} %broadcast_in_dim.6), calls=%async_computation.1 | async-start | bytes 262144 | tf_op jit(solution)/shard_map/all_to_all | solution.py:406
  18.1 4.5 %copy-start.2 = (f32[32,8,128]{2,1,0:T(8,128)}, f32[32,8,128]{2,1,0:T(8,128)S(1)}, u32[]{:S(2)}) copy-start(f32[32,8,128]{2,1,0:T(8,128)S(1)} %all-to-all-done.1.knots) | copy-start | bytes 393220
  18.1 17.0 %all-to-all-start = ((f32[4,192,256]{2,1,0:T(8,128)}), f32[4,192,256]{2,1,0:T(8,128)S(1)}, u32[]{:S(2)}, u32[]{:S(2)}) async-start(f32[4,192,256]{2,1,0:T(8,128)} %get-tuple-element.15), calls=%async_computation | async-start | bytes 1572864 | tf_op jit(solution)/shard_map/all_to_all | solution.py:402
  35.1 3.3 %copy-start = (f32[4,192,256]{2,1,0:T(8,128)}, f32[4,192,256]{2,1,0:T(8,128)S(1)}, u32[]{:S(2)}) copy-start(f32[4,192,256]{2,1,0:T(8,128)S(1)} %all-to-all-done.inc) | copy-start | bytes 2359300
  35.1 9.3 %all-to-all-start.2 = ((f32[4,32,256]{2,1,0:T(8,128)}), f32[4,32,256]{2,1,0:T(8,128)S(1)}, u32[]{:S(2)}, u32[]{:S(2)}) async-start(f32[4,32,256]{2,1,0:T(8,128)} %bitcast.20), calls=%async_computation.2 | async-start | bytes 262144 | tf_op jit(solution)/shard_map/all_to_all | solution.py:411
  44.4 0.7 copy-start.1
  69.3 2.3 %collective-permute-start = (f32[16,40,256]{2,1,0:T(8,128)}, f32[16,40,256]{2,1,0:T(8,128)S(1)}, u32[]{:S(2)}, u32[]{:S(2)}) collective-permute-start(f32[16,40,256]{2,1,0:T(8,128)} %get-tuple-element.23), channel_id=1, source_target_pairs={{0,1},{1,0},{2,3},{3,2},{4,5},{5,4},{6,7},{7,6},{8,9},{9,8},{10,11... | collective-permute-start | bytes 1966088 | tf_op jit(solution)/shard_map/ppermute | solution.py:415
  91.7 1.4 %collective-permute-start.1 = (f32[16,256]{1,0:T(8,128)}, f32[16,256]{1,0:T(8,128)S(1)}, u32[]{:S(2)}, u32[]{:S(2)}) collective-permute-start(f32[16,256]{1,0:T(8,128)} %get-tuple-element.24), channel_id=1, source_target_pairs={{0,1},{1,0},{2,3},{3,2},{4,5},{5,4},{6,7},{7,6},{8,9},{9,8},{10,11... | collective-permute-start | bytes 49160 | tf_op jit(solution)/shard_map/ppermute | solution.py:418

commit v3 on v2

v3 whole, which is shorter than its diff:
```python
import jax
import jax.numpy as jnp
from jax import lax
from jax.experimental import pallas as pl
from jax.experimental.pallas import tpu as pltpu
from jax.sharding import PartitionSpec as P


ROWS = 256
WIN = 64
CAP = 32
NBLK = 64
SLOTS = 128
STAR_DEV = 512
PAIR = 8
HW = 16
NHI = 64
F32 = jnp.float32
BF16 = jnp.bfloat16
I32 = jnp.int32
VM = pl.BlockSpec(memory_space=pltpu.VMEM)
SM = pl.BlockSpec(memory_space=pltpu.SMEM)


def shape(dims, dtype=F32):
    return jax.ShapeDtypeStruct(dims, dtype)


def pack_kernel(sky, dest, count, partials, stars, out0, out1, out2, out3, slots, out, used):
    out[...] = jnp.zeros_like(out)
    out[:, 160:192, :] = jnp.full((4, 32, ROWS), -1.0, F32)
    for g in range(4):
        used[g] = 0

    def place(b, carry):
        g = (dest[b] - sky[0]) & 3
        k = used[g]
        used[g] = k + 1
        slots[b] = g * CAP + k
        for q in range(5):
            out[g, pl.ds(q * CAP + k, 1), :] = partials[q, pl.ds(b, 1), :]
        out[g, pl.ds(5 * CAP + k, 1), :] = stars[pl.ds(b, 1), :].astype(F32)
        return carry

    lax.fori_loop(0, count[0], place, 0)

    def skip(b, carry):
        slots[b] = -1
        return carry

    lax.fori_loop(count[0], NBLK, skip, 0)
    for d, ref in enumerate((out0, out1, out2, out3)):
        ref[...] = out[d]


def pack(sky, dest, count, partials, stars):
    *slabs, slots = pl.pallas_call(
        pack_kernel,
        name="pack",
        out_shape=(shape((192, ROWS)),) * 4 + (shape((NBLK,), I32),),
        in_specs=[SM, SM, SM, VM, VM],
        out_specs=(VM,) * 4 + (SM,),
        scratch_shapes=[pltpu.VMEM((4, 192, ROWS), F32), pltpu.SMEM((4,), I32)],
    )(sky, dest, count, partials, stars)
    return slabs, slots


def collect_kernel(slots, count, rows0, rows1, rows2, rows3, out, rows):
    out[...] = jnp.zeros_like(out)
    for d, ref in enumerate((rows0, rows1, rows2, rows3)):
        rows[d * CAP:(d + 1) * CAP] = ref[...]

    def place(b, carry):
        out[pl.ds(b, 1), :] = rows[pl.ds(slots[b], 1), :]
        return carry

    lax.fori_loop(0, count[0], place, 0)


def collect(slots, count, slabs):
    return pl.pallas_call(
        collect_kernel,
        name="collect",
        out_shape=shape((NBLK, ROWS)),
        in_specs=[SM, SM] + [VM] * 4,
        out_specs=VM,
        scratch_shapes=[pltpu.VMEM((SLOTS, ROWS), F32)],
    )(slots, count, *slabs)


STEP = 16


def residual_kernel(
    start, tiles, slots, count, knots, obs, design, out0, out1, out2, out3, near, far, shift, win, res, out
):
    step = pl.program_id(0)

    @pl.when(step == 0)
    def _():
        def place(b, carry):
            tile = tiles[b]
            after = jnp.minimum(tile + 1, 63)
            shift[pl.ds(b, 1), :] = jnp.full((1, 128), start[b] % 128, I32)
            for axis in range(3):
                near[axis, pl.ds(b, 1), :] = knots[tile // 2, pl.ds(3 * (tile % 2) + axis, 1), :]
                far[axis, pl.ds(b, 1), :] = knots[after // 2, pl.ds(3 * (after % 2) + axis, 1), :]
            return carry

        lax.fori_loop(0, NBLK, place, 0, unroll=4)
        lane = lax.broadcasted_iota(I32, (NBLK, 128), 1)
        at = lane + shift[...]
        wrapped = at & 127
        got = []
        for axis in range(3):
            a = jnp.take_along_axis(near[axis], wrapped, axis=1, mode="promise_in_bounds")
            b = jnp.take_along_axis(far[axis], wrapped, axis=1, mode="promise_in_bounds")
            got.append(jnp.where(at < 128, a, b))
        win[:, :128] = jnp.where(lane < WIN, got[0], pltpu.roll(got[1], WIN, 1)).astype(BF16)
        win[:, 128:] = got[2][:, :WIN].astype(BF16)

    at = pl.multiple_of(step * STEP, STEP)
    group = win[pl.ds(at, STEP), :]
    rows = [jnp.dot(group, design[u], preferred_element_type=F32)[u:u + 1] for u in range(STEP)]
    res[pl.ds(at, STEP), :] = obs[pl.ds(at, STEP), :] - jnp.concatenate(rows, axis=0)

    @pl.when(step == NBLK // STEP - 1)
    def _():
        out[...] = jnp.zeros_like(out)

        def place(b, carry):
            out[pl.ds(slots[b], 1), :] = res[pl.ds(b, 1), :]
            return carry

        lax.fori_loop(0, count[0], place, 0)
        for d, ref in enumerate((out0, out1, out2, out3)):
            ref[...] = out[d * CAP:(d + 1) * CAP]


def residuals(start, tiles, slots, count, knots, obs, design):
    return pl.pallas_call(
        residual_kernel,
        name="residuals",
        grid=(NBLK // STEP,),
        out_shape=(shape((CAP, ROWS)),) * 4,
        in_specs=[
            SM,
            SM,
            SM,
            SM,
            pl.BlockSpec((32, 8, 128), lambda i: (0, 0, 0)),
            pl.BlockSpec((NBLK, ROWS), lambda i: (0, 0)),
            pl.BlockSpec((STEP, 3 * WIN, ROWS), lambda i: (i, 0, 0)),
        ],
        out_specs=(pl.BlockSpec((CAP, ROWS), lambda i: (0, 0)),) * 4,
        scratch_shapes=[
            pltpu.VMEM((3, NBLK, 128), F32),
            pltpu.VMEM((3, NBLK, 128), F32),
            pltpu.VMEM((NBLK, 128), I32),
            pltpu.VMEM((NBLK, 3 * WIN), BF16),
            pltpu.VMEM((NBLK, ROWS), F32),
            pltpu.VMEM((SLOTS, ROWS), F32),
        ],
    )(start, tiles, slots, count, knots, obs, design)


def sort_rows(cols):
    sub = lax.broadcasted_iota(I32, (8, 128), 0)
    k = 2
    while k <= ROWS:
        j = k // 2
        while j >= 1:
            if j >= 8:
                step = j // 8
                for v in range(32):
                    w = v ^ step
                    if v < w:
                        low = jnp.minimum(cols[v], cols[w])
                        high = jnp.maximum(cols[v], cols[w])
                        up = ((v * 8) & k) == 0
                        cols[v], cols[w] = (low, high) if up else (high, low)
            else:
                first = (sub & j) == 0
                for v in range(32):
                    x = cols[v]
                    if j == 4:
                        other = pltpu.roll(x, 4, 0)
                    else:
                        other = jnp.where(first, pltpu.roll(x, 8 - j, 0), pltpu.roll(x, j, 0))
                    low = jnp.minimum(x, other)
                    high = jnp.maximum(x, other)
                    if k >= 8:
                        take_low = first if ((v * 8) & k) == 0 else jnp.logical_not(first)
                    else:
                        take_low = first == ((sub & k) == 0)
                    cols[v] = jnp.where(take_low, low, high)
            j //= 2
        k *= 2
    return cols


def pick_lanes(x, idx):
    halves = []
    for h in range(2):
        at = idx[:, h * 128:(h + 1) * 128]
        near = at & 127
        a = jnp.take_along_axis(x[:, :128], near, axis=1, mode="promise_in_bounds")
        b = jnp.take_along_axis(x[:, 128:], near, axis=1, mode="promise_in_bounds")
        halves.append(jnp.where(at < 128, a, b))
    return jnp.concatenate(halves, axis=1)


def sort_kernel(inc0, inc1, inc2, inc3, sk, skt, idx, inv, ps, bounds):
    inc = (inc0, inc1, inc2, inc3)
    ids = jnp.concatenate([ref[160:192, :] for ref in inc], axis=0)
    key = ids * 256.0 + lax.broadcasted_iota(I32, (SLOTS, ROWS), 1).astype(F32)
    kt = key.T
    skey = jnp.concatenate(sort_rows([kt[8 * v:8 * v + 8] for v in range(32)]), axis=0).astype(I32)
    star = skey >> 8
    sk[...] = star
    place = skey & 255
    hi = star >> 8
    wide = 0
    for c in range(32):
        h = hi[8 * c:8 * c + 8]
        s = star[8 * c:8 * c + 8]
        first = jnp.min(jnp.where(s >= 0, h, NHI - HW))
        first = jnp.minimum(first - first % 2, NHI - HW)
        last = jnp.max(jnp.where(s >= 0, h, -1))
        bounds[c] = first
        bounds[32 + c] = last
        wide = jnp.maximum(wide, last - first)
    bounds[64] = jnp.where(wide >= HW, 32, 0)
    back = (place * 256 + lax.broadcasted_iota(I32, (ROWS, SLOTS), 0)).astype(F32)
    inv_rows = sort_rows([back[8 * v:8 * v + 8] for v in range(32)])
    inv[...] = (jnp.concatenate(inv_rows, axis=0).astype(I32) & 255).T
    start = star.T
    for h in range(2):
        skt[h] = start[:, h * 128:(h + 1) * 128]
    place_t = place.T
    idx[...] = place_t
    for q in range(5):
        p = jnp.concatenate([ref[q * CAP:(q + 1) * CAP, :] for ref in inc], axis=0)
        ps[q * ROWS:(q + 1) * ROWS] = pick_lanes(p, place_t).T


def sort_slots(slabs):
    return pl.pallas_call(
        sort_kernel,
        name="sort",
        out_shape=(
            shape((ROWS, SLOTS), I32),
            shape((2, 128, 128), I32),
            shape((SLOTS, ROWS), I32),
            shape((SLOTS, ROWS), I32),
            shape((5 * ROWS, SLOTS)),
            shape((65,), I32),
        ),
        in_specs=[VM] * 4,
        out_specs=(VM,) * 5 + (SM,),
    )(*slabs)


def stacked(*refs):
    return jnp.concatenate([ref[...] for ref in refs], axis=0)


def scatter_kernel(
    bounds, core, sk, skt, idx, ps, res0, res1, res2, res3, mine, theirs, acc, rs, tall, oh
):
    rs[...] = pick_lanes(stacked(res0, res1, res2, res3), idx[...]).T
    acc[...] = jnp.zeros_like(acc)
    rowh = (lax.broadcasted_iota(I32, (80, 128), 0) // 20).astype(F32).astype(BF16)
    lane = lax.broadcasted_iota(I32, (128, 256), 1).astype(F32).astype(BF16)
    zero = jnp.zeros((), BF16)
    one = jnp.ones((), BF16)

    def add_window(c, h_from, h0, tall, oh):
        at = pl.multiple_of(c * 8, 8)
        p = [ps[pl.ds(pl.multiple_of(q * ROWS + c * 8, 8), 8), :] for q in range(5)]
        r = rs[pl.ds(at, 8), :]
        terms = [p[i] * p[j] for i in range(5) for j in range(i, 5)] + [p[i] * r for i in range(5)]
        for t, v in enumerate(terms):
            big = v.astype(BF16).astype(F32)
            small = v - big
            tall[t * 8:t * 8 + 8, :] = big
            tall[192 + t * 8:192 + t * 8 + 8, :] = small
            if t < 4:
                tall[160 + t * 8:160 + t * 8 + 8, :] = big
                tall[352 + t * 8:352 + t * 8 + 8, :] = small
        lo = pltpu.roll(skt[c // 16] & 255, 128 - (c % 16) * 8, 1).astype(F32).astype(BF16)
        hi = sk[pl.ds(at, 8), :] >> 8
        rel = jnp.where(hi >= h_from, hi - h0, -1).astype(F32)
        columns = []
        for s in range(8):
            col = jnp.broadcast_to(lo[:, s:s + 1], (128, 256))
            oh[s * 128:(s + 1) * 128, :] = jnp.where(col == lane, one, zero)
            diff = jnp.broadcast_to(rel[s:s + 1, :], (80, 128)).astype(BF16) - rowh
            hit = [diff == 4.0 * j for j in range(HW // 4)]
            both = []
            for part in range(2):
                five = [tall[pl.ds(192 * part + 8 * o + s, 8, stride=8), :] for o in (0, 8, 16, 4, 12)]
                t = jnp.concatenate(five + five, axis=0).astype(BF16)
                both += [jnp.where(m, t, zero) for m in hit]
            columns.append(jnp.concatenate(both, axis=0))
        prod = jnp.dot(jnp.concatenate(columns, axis=1), oh[...], preferred_element_type=F32)
        acc[pl.ds(pl.multiple_of(h0 * 20, 8), HW * 20), :] += prod[:HW * 20] + prod[HW * 20:]

    def chunks(n, carry):
        for u in range(PAIR):
            c = n * PAIR + u
            add_window(c, bounds[c], bounds[c], tall.at[u], oh.at[u])
        return carry

    lax.fori_loop(0, 32 // PAIR, chunks, 0)

    def rest(c, carry):
        def more(w, carry):
            h_from = bounds[c] + w * HW
            add_window(c, h_from, jnp.minimum(h_from, NHI - HW), tall.at[0], oh.at[0])
            return carry

        lax.fori_loop(1, (bounds[32 + c] - bounds[c]) // HW + 1, more, 0)
        return carry

    lax.fori_loop(0, bounds[64], rest, 0)
    me = core[0]
    for g in range(16):
        mine[g] = acc[pl.ds(pl.multiple_of((2 * g + me) * 40, 8), 40), :]
        theirs[g] = acc[pl.ds(pl.multiple_of((2 * g + 1 - me) * 40, 8), 40), :]


def scatter(bounds, core, sk, skt, idx, ps, res):
    return pl.pallas_call(
        scatter_kernel,
        name="scatter",
        out_shape=(shape((16, 40, 256)), shape((16, 40, 256))),
        in_specs=[SM, SM] + [VM] * 8,
        out_specs=(VM, VM),
        scratch_shapes=[
            pltpu.VMEM((NHI * 20, 256), F32),
            pltpu.VMEM((ROWS, SLOTS), F32),
            pltpu.VMEM((PAIR, 384, 128), F32),
            pltpu.VMEM((PAIR, 1024, 256), BF16),
        ],
    )(bounds, core, sk, skt, idx, ps, *res)


def solve_kernel(parts, update, packed, total):
    total[...] = jnp.sum(parts[...], axis=0)

    def row(r):
        return jnp.concatenate([total[r:r + 1, :], total[20 + r:21 + r, :]], axis=0)

    entries = {}
    r = 0
    for i in range(5):
        for j in range(i, 5):
            entries[i, j] = row(r) + 1.0 if i == j else row(r)
            r += 1
    factor = {}
    for j in range(5):
        pivot = entries[j, j]
        for k in range(j):
            pivot = pivot - factor[j, k] * factor[j, k]
        factor[j, j] = jnp.sqrt(pivot)
        for i in range(j + 1, 5):
            running = entries[j, i]
            for k in range(j):
                running = running - factor[i, k] * factor[j, k]
            factor[i, j] = running / factor[j, j]
    forward = []
    for i in range(5):
        running = row(15 + i)
        for k in range(i):
            running = running - factor[i, k] * forward[k]
        forward.append(running / factor[i, i])
    answer = [None] * 5
    for i in reversed(range(5)):
        running = forward[i]
        for k in range(i + 1, 5):
            running = running - factor[k, i] * answer[k]
        answer[i] = running / factor[i, i]
    packed[...] = jnp.zeros_like(packed)
    for i in range(5):
        for a in range(2):
            update[i:i + 1, a * 256:(a + 1) * 256] = answer[i][a:a + 1]
            packed[8 * a + i:8 * a + i + 1, :] = answer[i][a:a + 1]


def solve(parts):
    return pl.pallas_call(
        solve_kernel,
        name="solve",
        out_shape=(shape((5, STAR_DEV)), shape((16, 256))),
        in_specs=[VM],
        out_specs=(VM, VM),
        scratch_shapes=[pltpu.VMEM((40, 256), F32)],
    )(parts)


def fit_kernel(bounds, sk, inv, ps, table, res0, res1, res2, res3, out0, out1, out2, out3, fit):
    def look_up(c, h_from, h0):
        star = sk[pl.ds(pl.multiple_of(c * 8, 8), 8), :]
        at = star & 127
        rel = jnp.where(star >= h_from * 256, (star >> 7) - 2 * h0, -1)
        found = [jnp.zeros((8, 128), F32)] * 5
        for k in range(2 * HW):
            hit = rel == k
            for q in range(5):
                row = table[h0 + k // 2, q:q + 1, (k % 2) * 128:(k % 2) * 128 + 128]
                value = jnp.take_along_axis(
                    jnp.broadcast_to(row, (8, 128)), at, axis=1, mode="promise_in_bounds"
                )
                found[q] = jnp.where(hit, value, found[q])
        total = ps[pl.ds(pl.multiple_of(c * 8, 8), 8), :] * found[0]
        for q in range(1, 5):
            total = total + ps[pl.ds(pl.multiple_of(q * ROWS + c * 8, 8), 8), :] * found[q]
        return total

    def chunks(n, carry):
        for u in range(PAIR):
            c = n * PAIR + u
            fit[pl.ds(pl.multiple_of(c * 8, 8), 8), :] = look_up(c, bounds[c], bounds[c])
        return carry

    lax.fori_loop(0, 32 // PAIR, chunks, 0)

    def rest(c, carry):
        def more(w, carry):
            h_from = bounds[c] + w * HW
            fit[pl.ds(pl.multiple_of(c * 8, 8), 8), :] += look_up(c, h_from, jnp.minimum(h_from, NHI - HW))
            return carry

        lax.fori_loop(1, (bounds[32 + c] - bounds[c]) // HW + 1, more, 0)
        return carry

    lax.fori_loop(0, bounds[64], rest, 0)
    total = stacked(res0, res1, res2, res3) - pick_lanes(fit[...].T, inv[...])
    for d, ref in enumerate((out0, out1, out2, out3)):
        ref[...] = total[d * CAP:(d + 1) * CAP]


def apply_fit(bounds, sk, inv, ps, table, res):
    return pl.pallas_call(
        fit_kernel,
        name="fit",
        out_shape=(shape((CAP, ROWS)),) * 4,
        in_specs=[SM] + [VM] * 8,
        out_specs=(VM,) * 4,
        scratch_shapes=[pltpu.VMEM((ROWS, SLOTS), F32)],
    )(bounds, sk, inv, ps, table, *res)


def to_sky(slabs, sign):
    n = lax.axis_size("sky")
    moved = {
        d: lax.ppermute(slabs[d], "sky", [(i, (i + sign * d) % n) for i in range(n)]) for d in (2, 1, 3)
    }
    return [slabs[0]] + [moved[d] for d in (1, 2, 3)]


def steps(attitude, win_start, design, obs_value, star_design, star_local, block_dest, block_count):
    tm = lax.axis_size("tm")
    core = (lax.axis_index("tm") % 2).astype(I32)
    swap = [(i, i ^ 1) for i in range(tm)]
    chips = [list(range(0, tm, 2)), list(range(1, tm, 2))]

    sky = lax.axis_index("sky").astype(I32)[None]
    outgoing, slots = pack(sky, block_dest, block_count, star_design.transpose(1, 0, 2), star_local)
    incoming = to_sky(outgoing, 1)

    piece = attitude.astype(F32).reshape(3, 2, 128).transpose(1, 0, 2).reshape(6, 128)
    piece = jnp.pad(piece, ((0, 2), (0, 0)))
    knots = lax.all_to_all(jnp.broadcast_to(piece[None], (tm, 8, 128)), "tm", 0, 0, tiled=True)
    tiles = win_start >> 7
    out_res = residuals(win_start, tiles, slots, block_count, knots, obs_value, design.transpose(0, 2, 1))
    in_res = to_sky(out_res, 1)

    sk, skt, idx, inv, ps, bounds = sort_slots(incoming)
    mine, theirs = scatter(bounds, core[None], sk, skt, idx, ps, in_res)
    pair_sum = mine + lax.ppermute(theirs, "tm", swap)
    parts = lax.all_to_all(pair_sum, "tm", 0, 0, tiled=True, axis_index_groups=chips)
    own_update, packed = solve(parts)
    other = lax.ppermute(packed, "tm", swap)
    both = jnp.where(core == 0, jnp.stack([packed, other]), jnp.stack([other, packed]))
    table = lax.all_to_all(
        jnp.broadcast_to(both[None], (16, 2, 16, 256)), "tm", 0, 0, tiled=True, axis_index_groups=chips
    ).reshape(NHI, 8, 256)
    updated = apply_fit(bounds, sk, inv, ps, table, in_res)
    returned = to_sky(updated, -1)
    result = collect(slots, block_count, returned)
    return (result, own_update)


def solution(mesh):
    placed = (
        P(None, "tm"),
        P(("sky", "tm")),
        P(("sky", "tm"), None, None),
        P(("sky", "tm"), None),
        P(("sky", "tm"), None, None),
        P(("sky", "tm"), None),
        P(("sky", "tm")),
        P(("sky", "tm")),
    )
    return jax.shard_map(
        steps,
        mesh=mesh,
        in_specs=placed,
        out_specs=(P(("sky", "tm"), None), P(None, ("sky", "tm"))),
        check_vma=False,
    )
```

time: 132 us -> 118 us (0.89)
  Pallas kernels: 51 us -> 41.4 us
  starting transfers between devices: 16.1 us -> 24.1 us
  blocking collectives: 42.5 us -> 35.7 us
  waiting for transfers between devices: 12.1 us -> 7.71 us
  matrix products: 3.72 us -> 0 us
  local copies, waits for them, and re-layouts: 2.11 us -> 4.02 us
    ppermute x2 -> x11, starting transfers between devices: 0.01 us -> 15.8 us  [the longest x9 15.8 us: to_sky(): lax.ppermute(slabs[d], 'sky', [(i, (i + sign * d) % n) for i in range(n)])]
    pallas_call x1, Pallas kernels: 24.3 us -> 15.5 us  [scatter(): pl.pallas_call(scatter_kernel, name='scatter', out_shape=(shape((16, 40,...]
    all_to_all x3 -> x1, waiting for transfers between devices: 8.44 us -> 0.01 us  [steps(): lax.all_to_all(jnp.broadcast_to(piece[None], (tm, 8, 128)), 'tm', 0, 0, t...]
    all_to_all x3 -> x1, starting transfers between devices: 16.1 us -> 8.27 us  [steps(): lax.all_to_all(jnp.broadcast_to(piece[None], (tm, 8, 128)), 'tm', 0, 0, t...]
    all_to_all x3 -> x2, blocking collectives: 42.5 us -> 35.7 us  [the longest x1 20.3 us: steps(): lax.all_to_all(pair_sum, 'tm', 0, 0, tiled=True, axis_index_groups=chips)]
    ppermute x2 -> x11, waiting for transfers between devices: 3.7 us -> 7.7 us  [the longest x9 4.01 us: to_sky(): lax.ppermute(slabs[d], 'sky', [(i, (i + sign * d) % n) for i in range(n)])]
    dot_general x1 -> x0, matrix products: 3.72 us -> none  [local(): jnp.einsum('brc,bc->br', design, windows, preferred_element_type=F32)]
    unnamed x8 -> x20, local copies, waits for them, and re-layouts: 0.67 us -> 2.6 us
  transfers between devices with their start and end apart: 5 -> 12, of which waited for: 5 -> 4; matrix products, arithmetic and copies ran while one was open for 3% -> 1% of each run, Pallas kernels for 10% -> 12%
where the time goes in v3:
time: 118 us; the launch traced here: 117 us
  Pallas kernels  41.4 us (35%)
  blocking collectives  35.7 us (30%)
  starting transfers between devices  24.1 us (20%)
  waiting for transfers between devices  7.71 us (7%)
  local copies, waits for them, and re-layouts  4.02 us (3%)
  other arithmetic  3.14 us (3%)
  between operations  1.41 us (1%)
    all_to_all x1, blocking collectives, steps(): lax.all_to_all(pair_sum, 'tm', 0, 0, tiled=True, axis_index_groups=chips)  20.3 us
    ppermute x9, starting transfers between devices, to_sky(): lax.ppermute(slabs[d], 'sky', [(i, (i + sign * d) % n) for i in range(n)])  15.8 us
    pallas_call x1, Pallas kernels, scatter(): pl.pallas_call(scatter_kernel, name='scatter', out_shape=(shape((16, 40,...  15.5 us
    all_to_all x1, blocking collectives, steps(): lax.all_to_all(jnp.broadcast_to(both[None], (16, 2, 16, 256)), 'tm', 0, 0...  15.4 us
    all_to_all x1, starting transfers between devices, steps(): lax.all_to_all(jnp.broadcast_to(piece[None], (tm, 8, 128)), 'tm', 0, 0, t...  8.27 us
    pallas_call x1, Pallas kernels, apply_fit(): pl.pallas_call(fit_kernel, name='fit', out_shape=(shape((CAP, ROWS)),) *...  8.08 us
    pallas_call x1, Pallas kernels, residuals(): pl.pallas_call(residual_kernel, name='residuals', grid=(NBLK // STEP,), o...  6.31 us
    pallas_call x1, Pallas kernels, sort_slots(): pl.pallas_call(sort_kernel, name='sort', out_shape=(shape((ROWS, SLOTS),...  4.74 us
  transfers between devices with their start and end apart: 12, of which 4 were waited for; matrix products, arithmetic and copies ran while one was open for 1% of the time, Pallas kernels for 12%

profile of v3, /device:TPU:0, one launch (start us, length us, event | category | flops | bytes accessed | tf_op | source)
XLA Modules:
  0.0 117.5 jit_solution(17530683387419208590)
XLA Ops:
  2.0 8.3 %all-to-all-start = ((f32[32,8,128]{2,1,0:T(8,128)}), f32[32,8,128]{2,1,0:T(8,128)S(1)}, u32[]{:S(2)}, u32[]{:S(2)}) async-start(f32[32,8,128]{2,1,0:T(8,128)} %broadcast_in_dim.20), calls=%async_computation | async-start | bytes 262144 | tf_op jit(solution)/shard_map/all_to_all | solution.py:475
  10.9 3.2 %pack.1 = (f32[192,256]{1,0:T(8,128)}, f32[192,256]{1,0:T(8,128)}, f32[192,256]{1,0:T(8,128)}, f32[192,256]{1,0:T(8,128)}, s32[64]{0:T(128)}) custom-call(s32[1]{0:T(128)} %bitcast.sky, s32[64]{0:T(128)} %dest.1, s32[1]{0:T(128)S(6)} %copy.12.count, f32[5,64,256]{2,1,0:T(8,128)} %bitcast.12, s32[64,256]{1,0:T(8,128)} %stars.1), custom_call_target="tpu_custom_call" | custom-call | tf_op jit(solution)/shard_map/pack/pallas_call | solution.py:57
  14.1 1.6 %collective-permute-start = (f32[192,256]{1,0:T(8,128)}, f32[192,256]{1,0:T(8,128)S(1)}, u32[]{:S(2)}, u32[]{:S(2)}) collective-permute-start(f32[192,256]{1,0:T(8,128)} %get-tuple-element.27), channel_id=1, source_target_pairs={{0,32},{32,64},{64,96},{96,0},{1,33},{33,65},{65,97},{97,1},{2,34}... | collective-permute-start | bytes 589832 | tf_op jit(solution)/shard_map/ppermute | solution.py:458
  15.7 2.9 %collective-permute-start.1 = (f32[192,256]{1,0:T(8,128)}, f32[192,256]{1,0:T(8,128)S(1)}, u32[]{:S(2)}, u32[]{:S(2)}) collective-permute-start(f32[192,256]{1,0:T(8,128)} %get-tuple-element.28), channel_id=1, source_target_pairs={{0,64},{32,96},{64,0},{96,32},{1,65},{33,97},{65,1},{97,33},{2,66}... | collective-permute-start | bytes 589832 | tf_op jit(solution)/shard_map/ppermute | solution.py:458
  18.6 1.2 %collective-permute-start.2 = (f32[192,256]{1,0:T(8,128)}, f32[192,256]{1,0:T(8,128)S(1)}, u32[]{:S(2)}, u32[]{:S(2)}) collective-permute-start(f32[192,256]{1,0:T(8,128)} %get-tuple-element.29), channel_id=1, source_target_pairs={{0,96},{32,0},{64,32},{96,64},{1,97},{33,1},{65,33},{97,65},{2,98}... | collective-permute-start | bytes 589832 | tf_op jit(solution)/shard_map/ppermute | solution.py:458
  19.8 1.2 broadcast_shift-right-arithmetic_fusion.tiles
  21.6 6.3 %residuals.1 = (f32[32,256]{1,0:T(8,128)}, f32[32,256]{1,0:T(8,128)}, f32[32,256]{1,0:T(8,128)}, f32[32,256]{1,0:T(8,128)}) custom-call(s32[64]{0:T(128)} %start.1, s32[64]{0:T(128)} %broadcast_shift-right-arithmetic_fusion.tiles, s32[64]{0:T(128)} %get-tuple-element.25.slots, s32[1]{0:T(128)S(6)} %copy.12.count, f32[32,8,128]{2,1,0:T(8,128)} %copy-done, ...), custom_call_target="tpu_custom_call" | custom-call | tf_op jit(solution)/shard_map/residuals/pallas_call | solution.py:141
  27.9 0.8 collective-permute-start.3
  29.5 2.0 %collective-permute-start.5 = (f32[32,256]{1,0:T(8,128)}, f32[32,256]{1,0:T(8,128)S(1)}, u32[]{:S(2)}, u32[]{:S(2)}) collective-permute-start(f32[32,256]{1,0:T(8,128)} %get-tuple-element.39), channel_id=1, source_target_pairs={{0,96},{32,0},{64,32},{96,64},{1,97},{33,1},{65,33},{97,65},{2,98}... | collective-permute-start | bytes 98312 | tf_op jit(solution)/shard_map/ppermute | solution.py:458
  32.2 4.7 %sort.1 = (s32[256,128]{1,0:T(8,128)}, s32[2,128,128]{2,1,0:T(8,128)}, s32[128,256]{1,0:T(8,128)}, s32[128,256]{1,0:T(8,128)}, f32[1280,128]{1,0:T(8,128)}, /*index=5*/s32[65]{0:T(128)}) custom-call(f32[192,256]{1,0:T(8,128)} %get-tuple-element.26.inc0, f32[192,256]{1,0:T(8,128)} %copy-done.1, f32[192,256]{1,0:T(8,128)} %copy-done.2, f32[192,256]{1,0:T(8,128)} %copy-done.3), custom_call_target="tpu_custom_call" | custom-call | tf_op jit(solution)/shard_map/sort/pallas_call | solution.py:248
  37.7 15.5 %scatter.1 = (f32[16,40,256]{2,1,0:T(8,128)}, f32[16,40,256]{2,1,0:T(8,128)}) custom-call(s32[65]{0:T(128)} %get-tuple-element.30.bounds, s32[1]{0:T(128)} %bitcast.2.core, s32[256,128]{1,0:T(8,128)} %get-tuple-element.31.sk, s32[2,128,128]{2,1,0:T(8,128)} %get-tuple-element.34.skt, s32[128,256]{1,0:T(8,128)} %get-tuple-element.35.idx, ...), custom_call_target="tpu_custom_call" | custom-call | tf_op jit(solution)/shard_map/scatter/pallas_call | solution.py:334
  53.1 2.3 %collective-permute-done.6 = f32[16,40,256]{2,1,0:T(8,128)S(1)} collective-permute-done((f32[16,40,256]{2,1,0:T(8,128)}, f32[16,40,256]{2,1,0:T(8,128)S(1)}, u32[]{:S(2)}, u32[]{:S(2)}) %collective-permute-start.6) | collective-permute-done | bytes 655392 | tf_op jit(solution)/shard_map/ppermute | solution.py:482
  55.5 1.2 add.10
  56.6 20.3 %all_to_all.15.parts = f32[16,40,256]{2,1,0:T(8,128)} all-to-all(f32[16,40,256]{2,1,0:T(8,128)S(1)} %add.10), channel_id=1, replica_groups={{0,2,4,6,8,10,12,14,16,18,20,22,24,26,28,30},{1,3,5,7,9,11,13,15,17,19,..., dimensions={0} | all-to-all | bytes 1310720 | tf_op jit(solution)/shard_map/all_to_all | solution.py:483
  76.9 1.8 %solve.1 = (f32[5,512]{1,0:T(8,128)}, f32[16,256]{1,0:T(8,128)}) custom-call(f32[16,40,256]{2,1,0:T(8,128)} %all_to_all.15.parts), custom_call_target="tpu_custom_call" | custom-call | tf_op jit(solution)/shard_map/solve/pallas_call | solution.py:392
  78.8 1.4 %collective-permute-done.7 = f32[16,256]{1,0:T(8,128)S(1)} collective-permute-done((f32[16,256]{1,0:T(8,128)}, f32[16,256]{1,0:T(8,128)S(1)}, u32[]{:S(2)}, u32[]{:S(2)}) %collective-permute-start.7) | collective-permute-done | bytes 16416 | tf_op jit(solution)/shard_map/ppermute | solution.py:485
  80.2 0.8 maximum_select_fusion
  81.0 15.4 %all_to_all.16 = f32[16,2,16,256]{3,2,1,0:T(8,128)} all-to-all(f32[16,2,16,256]{3,2,1,0:T(8,128)S(1)} %broadcast_in_dim.21), channel_id=1, replica_groups={{0,2,4,6,8,10,12,14,16,18,20,22,24,26,28,30},{1,3,5,7,9,11,13,15,17,19,..., dimensions={0} | all-to-all | bytes 1048576 | tf_op jit(solution)/shard_map/all_to_all | solution.py:487
  96.4 8.1 %fit.1 = (f32[32,256]{1,0:T(8,128)}, f32[32,256]{1,0:T(8,128)}, f32[32,256]{1,0:T(8,128)}, f32[32,256]{1,0:T(8,128)}) custom-call(s32[65]{0:T(128)} %get-tuple-element.30.bounds, s32[256,128]{1,0:T(8,128)} %get-tuple-element.31.sk, s32[128,256]{1,0:T(8,128)} %get-tuple-element.32.inv, f32[1280,128]{1,0:T(8,128)} %get-tuple-element.33.ps, ...), custom_call_target="tpu_custom_call" | custom-call | tf_op jit(solution)/shard_map/fit/pallas_call | solution.py:445
  104.5 1.4 %collective-permute-start.8 = (f32[32,256]{1,0:T(8,128)}, f32[32,256]{1,0:T(8,128)S(1)}, u32[]{:S(2)}, u32[]{:S(2)}) collective-permute-start(f32[32,256]{1,0:T(8,128)} %get-tuple-element.44), channel_id=1, source_target_pairs={{0,96},{32,0},{64,32},{96,64},{1,97},{33,1},{65,33},{97,65},{2,98}... | collective-permute-start | bytes 98312 | tf_op jit(solution)/shard_map/ppermute | solution.py:458
  105.9 3.8 %collective-permute-start.9 = (f32[32,256]{1,0:T(8,128)}, f32[32,256]{1,0:T(8,128)S(1)}, u32[]{:S(2)}, u32[]{:S(2)}) collective-permute-start(f32[32,256]{1,0:T(8,128)} %get-tuple-element.45), channel_id=1, source_target_pairs={{0,64},{32,96},{64,0},{96,32},{1,65},{33,97},{65,1},{97,33},{2,66}... | collective-permute-start | bytes 98312 | tf_op jit(solution)/shard_map/ppermute | solution.py:458
  109.8 1.3 %collective-permute-start.10 = (f32[32,256]{1,0:T(8,128)}, f32[32,256]{1,0:T(8,128)S(1)}, u32[]{:S(2)}, u32[]{:S(2)}) collective-permute-start(f32[32,256]{1,0:T(8,128)} %get-tuple-element.46), channel_id=1, source_target_pairs={{0,32},{32,64},{64,96},{96,0},{1,33},{33,65},{65,97},{97,1},{2,34}... | collective-permute-start | bytes 98312 | tf_op jit(solution)/shard_map/ppermute | solution.py:458
  111.9 3.2 %collective-permute-done.10.rows3 = f32[32,256]{1,0:T(8,128)S(1)} collective-permute-done((f32[32,256]{1,0:T(8,128)}, f32[32,256]{1,0:T(8,128)S(1)}, u32[]{:S(2)}, u32[]{:S(2)}) %collective-permute-start.10) | collective-permute-done | bytes 32800 | tf_op jit(solution)/shard_map/ppermute | solution.py:458
  115.7 1.7 %collect.1 = f32[64,256]{1,0:T(8,128)} custom-call(s32[64]{0:T(128)} %get-tuple-element.25.slots, s32[1]{0:T(128)S(6)} %copy.12.count, f32[32,256]{1,0:T(8,128)} %get-tuple-element.43.rows0, f32[32,256]{1,0:T(8,128)} %copy-done.7, f32[32,256]{1,0:T(8,128)} %copy-done.8, f32[32,256]{1,0:T(8,128)} %copy-done.9), custom_call_target="tpu_custom_call" | custom-call | tf_op jit(solution)/shard_map/collect/pallas_call | solution.py:81
  (36 shorter events, 5.5 us)
Async XLA Ops:
  2.0 19.0 %all-to-all-start = ((f32[32,8,128]{2,1,0:T(8,128)}), f32[32,8,128]{2,1,0:T(8,128)S(1)}, u32[]{:S(2)}, u32[]{:S(2)}) async-start(f32[32,8,128]{2,1,0:T(8,128)} %broadcast_in_dim.20), calls=%async_computation | async-start | bytes 262144 | tf_op jit(solution)/shard_map/all_to_all | solution.py:475
  14.1 15.4 %collective-permute-start = (f32[192,256]{1,0:T(8,128)}, f32[192,256]{1,0:T(8,128)S(1)}, u32[]{:S(2)}, u32[]{:S(2)}) collective-permute-start(f32[192,256]{1,0:T(8,128)} %get-tuple-element.27), channel_id=1, source_target_pairs={{0,32},{32,64},{64,96},{96,0},{1,33},{33,65},{65,97},{97,1},{2,34}... | collective-permute-start | bytes 589832 | tf_op jit(solution)/shard_map/ppermute | solution.py:458
  15.7 15.8 %collective-permute-start.1 = (f32[192,256]{1,0:T(8,128)}, f32[192,256]{1,0:T(8,128)S(1)}, u32[]{:S(2)}, u32[]{:S(2)}) collective-permute-start(f32[192,256]{1,0:T(8,128)} %get-tuple-element.28), channel_id=1, source_target_pairs={{0,64},{32,96},{64,0},{96,32},{1,65},{33,97},{65,1},{97,33},{2,66}... | collective-permute-start | bytes 589832 | tf_op jit(solution)/shard_map/ppermute | solution.py:458
  18.6 12.9 %collective-permute-start.2 = (f32[192,256]{1,0:T(8,128)}, f32[192,256]{1,0:T(8,128)S(1)}, u32[]{:S(2)}, u32[]{:S(2)}) collective-permute-start(f32[192,256]{1,0:T(8,128)} %get-tuple-element.29), channel_id=1, source_target_pairs={{0,96},{32,0},{64,32},{96,64},{1,97},{33,1},{65,33},{97,65},{2,98}... | collective-permute-start | bytes 589832 | tf_op jit(solution)/shard_map/ppermute | solution.py:458
  21.0 0.7 copy-start
  27.9 9.1 %collective-permute-start.3 = (f32[32,256]{1,0:T(8,128)}, f32[32,256]{1,0:T(8,128)S(1)}, u32[]{:S(2)}, u32[]{:S(2)}) collective-permute-start(f32[32,256]{1,0:T(8,128)} %get-tuple-element.37), channel_id=1, source_target_pairs={{0,32},{32,64},{64,96},{96,0},{1,33},{33,65},{65,97},{97,1},{2,34}... | collective-permute-start | bytes 98312 | tf_op jit(solution)/shard_map/ppermute | solution.py:458
  28.8 8.3 %collective-permute-start.4 = (f32[32,256]{1,0:T(8,128)}, f32[32,256]{1,0:T(8,128)S(1)}, u32[]{:S(2)}, u32[]{:S(2)}) collective-permute-start(f32[32,256]{1,0:T(8,128)} %get-tuple-element.38), channel_id=1, source_target_pairs={{0,64},{32,96},{64,0},{96,32},{1,65},{33,97},{65,1},{97,33},{2,66}... | collective-permute-start | bytes 98312 | tf_op jit(solution)/shard_map/ppermute | solution.py:458
  29.5 2.0 %copy-start.1 = (f32[192,256]{1,0:T(8,128)}, f32[192,256]{1,0:T(8,128)S(1)}, u32[]{:S(2)}) copy-start(f32[192,256]{1,0:T(8,128)S(1)} %collective-permute-done.inc1) | copy-start | bytes 589828
  29.5 7.5 %collective-permute-start.5 = (f32[32,256]{1,0:T(8,128)}, f32[32,256]{1,0:T(8,128)S(1)}, u32[]{:S(2)}, u32[]{:S(2)}) collective-permute-start(f32[32,256]{1,0:T(8,128)} %get-tuple-element.39), channel_id=1, source_target_pairs={{0,96},{32,0},{64,32},{96,64},{1,97},{33,1},{65,33},{97,65},{2,98}... | collective-permute-start | bytes 98312 | tf_op jit(solution)/shard_map/ppermute | solution.py:458
  31.5 0.7 copy-start.2
  31.5 0.7 copy-start.3
  37.0 0.6 copy-start.4
  37.0 0.6 copy-start.5
  37.0 0.6 copy-start.6
  53.1 2.3 %collective-permute-start.6 = (f32[16,40,256]{2,1,0:T(8,128)}, f32[16,40,256]{2,1,0:T(8,128)S(1)}, u32[]{:S(2)}, u32[]{:S(2)}) collective-permute-start(f32[16,40,256]{2,1,0:T(8,128)} %get-tuple-element.41), channel_id=1, source_target_pairs={{0,1},{1,0},{2,3},{3,2},{4,5},{5,4},{6,7},{7,6},{8,9},{9,8},{10,11... | collective-permute-start | bytes 1966088 | tf_op jit(solution)/shard_map/ppermute | solution.py:482
  78.8 1.4 %collective-permute-start.7 = (f32[16,256]{1,0:T(8,128)}, f32[16,256]{1,0:T(8,128)S(1)}, u32[]{:S(2)}, u32[]{:S(2)}) collective-permute-start(f32[16,256]{1,0:T(8,128)} %get-tuple-element.42), channel_id=1, source_target_pairs={{0,1},{1,0},{2,3},{3,2},{4,5},{5,4},{6,7},{7,6},{8,9},{9,8},{10,11... | collective-permute-start | bytes 49160 | tf_op jit(solution)/shard_map/ppermute | solution.py:485
  104.5 6.6 %collective-permute-start.8 = (f32[32,256]{1,0:T(8,128)}, f32[32,256]{1,0:T(8,128)S(1)}, u32[]{:S(2)}, u32[]{:S(2)}) collective-permute-start(f32[32,256]{1,0:T(8,128)} %get-tuple-element.44), channel_id=1, source_target_pairs={{0,96},{32,0},{64,32},{96,64},{1,97},{33,1},{65,33},{97,65},{2,98}... | collective-permute-start | bytes 98312 | tf_op jit(solution)/shard_map/ppermute | solution.py:458
  105.9 5.9 %collective-permute-start.9 = (f32[32,256]{1,0:T(8,128)}, f32[32,256]{1,0:T(8,128)S(1)}, u32[]{:S(2)}, u32[]{:S(2)}) collective-permute-start(f32[32,256]{1,0:T(8,128)} %get-tuple-element.45), channel_id=1, source_target_pairs={{0,64},{32,96},{64,0},{96,32},{1,65},{33,97},{65,1},{97,33},{2,66}... | collective-permute-start | bytes 98312 | tf_op jit(solution)/shard_map/ppermute | solution.py:458
  109.8 5.3 %collective-permute-start.10 = (f32[32,256]{1,0:T(8,128)}, f32[32,256]{1,0:T(8,128)S(1)}, u32[]{:S(2)}, u32[]{:S(2)}) collective-permute-start(f32[32,256]{1,0:T(8,128)} %get-tuple-element.46), channel_id=1, source_target_pairs={{0,32},{32,64},{64,96},{96,0},{1,33},{33,65},{65,97},{97,1},{2,34}... | collective-permute-start | bytes 98312 | tf_op jit(solution)/shard_map/ppermute | solution.py:458
  111.1 4.0 %copy-start.7 = (f32[32,256]{1,0:T(8,128)}, f32[32,256]{1,0:T(8,128)S(1)}, u32[]{:S(2)}) copy-start(f32[32,256]{1,0:T(8,128)S(1)} %collective-permute-done.8.rows1) | copy-start | bytes 98308
  111.9 3.2 %copy-start.8 = (f32[32,256]{1,0:T(8,128)}, f32[32,256]{1,0:T(8,128)S(1)}, u32[]{:S(2)}) copy-start(f32[32,256]{1,0:T(8,128)S(1)} %collective-permute-done.9.rows2) | copy-start | bytes 98308
  115.1 0.6 copy-start.9

commit v4 on v3

--- a/solution.py
+++ b/solution.py
@@ -13,7 +13,7 @@
 SLOTS = 128
 STAR_DEV = 512
 PAIR = 8
-HW = 16
+HW = 12
 NHI = 64
 F32 = jnp.float32
 BF16 = jnp.bfloat16
@@ -28,7 +28,7 @@
 
 def pack_kernel(sky, dest, count, partials, stars, out0, out1, out2, out3, slots, out, used):
     out[...] = jnp.zeros_like(out)
-    out[:, 160:192, :] = jnp.full((4, 32, ROWS), -1.0, F32)
+    out[:, 160:192, :] = lax.broadcasted_iota(I32, (4, 32, ROWS), 2).astype(F32) * (NHI * 256 // ROWS)
     for g in range(4):
         used[g] = 0
 
@@ -86,6 +86,18 @@
         out_specs=VM,
         scratch_shapes=[pltpu.VMEM((SLOTS, ROWS), F32)],
     )(slots, count, *slabs)
+
+
+def piece_kernel(attitude, out):
+    values = attitude[...].astype(F32)
+    rows = jnp.concatenate([values[:, :128], values[:, 128:], jnp.zeros((2, 128), F32)], axis=0)
+    out[...] = jnp.broadcast_to(rows[None], out.shape)
+
+
+def pieces(attitude, copies):
+    return pl.pallas_call(
+        piece_kernel, name="pieces", out_shape=shape((copies, 8, 128)), in_specs=[VM], out_specs=VM
+    )(attitude)
 
 
 STEP = 16
@@ -164,11 +176,20 @@
     )(start, tiles, slots, count, knots, obs, design)
 
 
-def sort_rows(cols):
+def sort_rows(key):
     sub = lax.broadcasted_iota(I32, (8, 128), 0)
+    left = lax.broadcasted_iota(I32, (8, 128), 1) < 64
+    sign = jnp.where(left, 1.0, -1.0)
+    cols = [key[8 * v:8 * v + 8] * sign for v in range(32)]
     k = 2
-    while k <= ROWS:
+    while k <= 2 * ROWS:
         j = k // 2
+        if k == 2 * ROWS:
+            for v in range(32):
+                x = cols[v] * sign
+                other = pltpu.roll(x, 64, 1)
+                cols[v] = jnp.where(left, jnp.minimum(x, other), jnp.maximum(x, other))
+            j //= 2
         while j >= 1:
             if j >= 8:
                 step = j // 8
@@ -196,52 +217,80 @@
                     cols[v] = jnp.where(take_low, low, high)
             j //= 2
         k *= 2
-    return cols
-
-
-def pick_lanes(x, idx):
-    halves = []
-    for h in range(2):
-        at = idx[:, h * 128:(h + 1) * 128]
-        near = at & 127
-        a = jnp.take_along_axis(x[:, :128], near, axis=1, mode="promise_in_bounds")
-        b = jnp.take_along_axis(x[:, 128:], near, axis=1, mode="promise_in_bounds")
-        halves.append(jnp.where(at < 128, a, b))
-    return jnp.concatenate(halves, axis=1)
-
-
-def sort_kernel(inc0, inc1, inc2, inc3, sk, skt, idx, inv, ps, bounds):
+    return jnp.concatenate(cols, axis=0)
+
+
+def pick_rows(x, rank):
+    tops = []
+    for top in range(2):
+        halves = []
+        for h in range(2):
+            at = rank[64 * top:64 * top + 64, 128 * h:128 * h + 128]
+            near = at & 127
+            got = None
+            for code in range(4):
+                piece = x[64 * (code // 2):64 * (code // 2) + 64, 128 * (code % 2):128 * (code % 2) + 128]
+                value = jnp.take_along_axis(piece, near, axis=1, mode="promise_in_bounds")
+                got = value if code == 0 else jnp.where((at >> 7) == code, value, got)
+            halves.append(got)
+        tops.append(jnp.concatenate(halves, axis=1))
+    return jnp.concatenate(tops, axis=0)
+
+
+def to_chunks(xt):
+    left = lax.broadcasted_iota(I32, (8, 128), 1) < 64
+    low, high = [], []
+    for n in range(16):
+        a = xt[16 * n:16 * n + 8]
+        b = xt[16 * n + 8:16 * n + 16]
+        low.append(jnp.where(left, a, pltpu.roll(b, 64, 1)))
+        high.append(jnp.where(left, pltpu.roll(a, 64, 1), b))
+    return low + high
+
+
+def from_chunks(chunks):
+    left = lax.broadcasted_iota(I32, (8, 128), 1) < 64
+    rows = []
+    for n in range(16):
+        low, high = chunks[n], chunks[16 + n]
+        rows.append(jnp.where(left, low, pltpu.roll(high, 64, 1)))
+        rows.append(jnp.where(left, pltpu.roll(low, 64, 1), high))
+    return jnp.concatenate(rows, axis=0)
+
+
+def sort_kernel(inc0, inc1, inc2, inc3, star, skt, rank, came, ps, bounds):
     inc = (inc0, inc1, inc2, inc3)
     ids = jnp.concatenate([ref[160:192, :] for ref in inc], axis=0)
-    key = ids * 256.0 + lax.broadcasted_iota(I32, (SLOTS, ROWS), 1).astype(F32)
-    kt = key.T
-    skey = jnp.concatenate(sort_rows([kt[8 * v:8 * v + 8] for v in range(32)]), axis=0).astype(I32)
-    star = skey >> 8
-    sk[...] = star
-    place = skey & 255
-    hi = star >> 8
+    slot = lax.broadcasted_iota(I32, (SLOTS, ROWS), 0)
+    row = lax.broadcasted_iota(I32, (SLOTS, ROWS), 1)
+    key = ids * 512.0 + ((slot >> 6) * 256 + row).astype(F32)
+    srt = sort_rows(key.T).astype(I32)
+    ids_t = srt >> 9
+    place = srt & 511
     wide = 0
-    for c in range(32):
-        h = hi[8 * c:8 * c + 8]
-        s = star[8 * c:8 * c + 8]
-        first = jnp.min(jnp.where(s >= 0, h, NHI - HW))
+    for c, piece in enumerate(to_chunks(ids_t)):
+        star[c] = piece
+        h = piece >> 8
+        first = jnp.min(jnp.where(piece >= 0, h, NHI - HW))
         first = jnp.minimum(first - first % 2, NHI - HW)
-        last = jnp.max(jnp.where(s >= 0, h, -1))
+        last = jnp.max(jnp.where(piece >= 0, h, -1))
         bounds[c] = first
         bounds[32 + c] = last
         wide = jnp.maximum(wide, last - first)
     bounds[64] = jnp.where(wide >= HW, 32, 0)
-    back = (place * 256 + lax.broadcasted_iota(I32, (ROWS, SLOTS), 0)).astype(F32)
-    inv_rows = sort_rows([back[8 * v:8 * v + 8] for v in range(32)])
-    inv[...] = (jnp.concatenate(inv_rows, axis=0).astype(I32) & 255).T
-    start = star.T
-    for h in range(2):
-        skt[h] = start[:, h * 128:(h + 1) * 128]
-    place_t = place.T
-    idx[...] = place_t
+    came[...] = place
+    ids_a = ids_t.T
+    ahead = jnp.concatenate([ids_a[:, 8:], ids_a[:, :8]], axis=1)
+    for half in range(2):
+        both = jnp.concatenate([ids_a[64 * half:64 * half + 64], ahead[64 * half:64 * half + 64]], axis=0)
+        for h in range(2):
+            skt[2 * half + h] = both[:, 128 * h:128 * h + 128]
+    rank_a = place.T
+    rank[...] = rank_a
     for q in range(5):
         p = jnp.concatenate([ref[q * CAP:(q + 1) * CAP, :] for ref in inc], axis=0)
-        ps[q * ROWS:(q + 1) * ROWS] = pick_lanes(p, place_t).T
+        for c, piece in enumerate(to_chunks(pick_rows(p, rank_a).T)):
+            ps[q * 32 + c] = piece
 
 
 def sort_slots(slabs):
@@ -249,11 +298,11 @@
         sort_kernel,
         name="sort",
         out_shape=(
+            shape((32, 8, 128), I32),
+            shape((4, 128, 128), I32),
+            shape((SLOTS, ROWS), I32),
             shape((ROWS, SLOTS), I32),
-            shape((2, 128, 128), I32),
-            shape((SLOTS, ROWS), I32),
-            shape((SLOTS, ROWS), I32),
-            shape((5 * ROWS, SLOTS)),
+            shape((160, 8, 128)),
             shape((65,), I32),
         ),
         in_specs=[VM] * 4,
@@ -261,14 +310,28 @@
     )(*slabs)
 
 
+def invert_kernel(came, inv):
+    slot = lax.broadcasted_iota(I32, (ROWS, SLOTS), 1)
+    row = lax.broadcasted_iota(I32, (ROWS, SLOTS), 0)
+    back = (came[...] * 512 + (slot >> 6) * 256 + row).astype(F32)
+    inv[...] = (sort_rows(back).astype(I32) & 511).T
+
+
+def invert(came):
+    return pl.pallas_call(
+        invert_kernel, name="invert", out_shape=shape((SLOTS, ROWS), I32), in_specs=[VM], out_specs=VM
+    )(came)
+
+
 def stacked(*refs):
     return jnp.concatenate([ref[...] for ref in refs], axis=0)
 
 
 def scatter_kernel(
-    bounds, core, sk, skt, idx, ps, res0, res1, res2, res3, mine, theirs, acc, rs, tall, oh
+    bounds, core, star, skt, rank, ps, res0, res1, res2, res3, mine, theirs, acc, rs, tall, oh
 ):
-    rs[...] = pick_lanes(stacked(res0, res1, res2, res3), idx[...]).T
+    for c, piece in enumerate(to_chunks(pick_rows(stacked(res0, res1, res2, res3), rank[...]).T)):
+        rs[c] = piece
     acc[...] = jnp.zeros_like(acc)
     rowh = (lax.broadcasted_iota(I32, (80, 128), 0) // 20).astype(F32).astype(BF16)
     lane = lax.broadcasted_iota(I32, (128, 256), 1).astype(F32).astype(BF16)
@@ -276,9 +339,8 @@
     one = jnp.ones((), BF16)
 
     def add_window(c, h_from, h0, tall, oh):
-        at = pl.multiple_of(c * 8, 8)
-        p = [ps[pl.ds(pl.multiple_of(q * ROWS + c * 8, 8), 8), :] for q in range(5)]
-        r = rs[pl.ds(at, 8), :]
+        p = [ps[q * 32 + c] for q in range(5)]
+        r = rs[c]
         terms = [p[i] * p[j] for i in range(5) for j in range(i, 5)] + [p[i] * r for i in range(5)]
         for t, v in enumerate(terms):
             big = v.astype(BF16).astype(F32)
@@ -288,8 +350,8 @@
             if t < 4:
                 tall[160 + t * 8:160 + t * 8 + 8, :] = big
                 tall[352 + t * 8:352 + t * 8 + 8, :] = small
-        lo = pltpu.roll(skt[c // 16] & 255, 128 - (c % 16) * 8, 1).astype(F32).astype(BF16)
-        hi = sk[pl.ds(at, 8), :] >> 8
+        lo = pltpu.roll(skt[c // 8] & 255, 128 - (c % 8) * 16, 1).astype(F32).astype(BF16)
+        hi = star[c] >> 8
         rel = jnp.where(hi >= h_from, hi - h0, -1).astype(F32)
         columns = []
         for s in range(8):
@@ -330,7 +392,7 @@
         theirs[g] = acc[pl.ds(pl.multiple_of((2 * g + 1 - me) * 40, 8), 40), :]
 
 
-def scatter(bounds, core, sk, skt, idx, ps, res):
+def scatter(bounds, core, star, skt, rank, ps, res):
     return pl.pallas_call(
         scatter_kernel,
         name="scatter",
@@ -339,14 +401,14 @@
         out_specs=(VM, VM),
         scratch_shapes=[
             pltpu.VMEM((NHI * 20, 256), F32),
-            pltpu.VMEM((ROWS, SLOTS), F32),
+            pltpu.VMEM((32, 8, 128), F32),
             pltpu.VMEM((PAIR, 384, 128), F32),
             pltpu.VMEM((PAIR, 1024, 256), BF16),
         ],
-    )(bounds, core, sk, skt, idx, ps, *res)
-
-
-def solve_kernel(parts, update, packed, total):
+    )(bounds, core, star, skt, rank, ps, *res)
+
+
+def solve_kernel(parts, update, packed, total, own):
     total[...] = jnp.sum(parts[...], axis=0)
 
     def row(r):
@@ -381,29 +443,41 @@
         for k in range(i + 1, 5):
             running = running - factor[k, i] * answer[k]
         answer[i] = running / factor[i, i]
-    packed[...] = jnp.zeros_like(packed)
+    own[20:] = jnp.zeros((4, 128), F32)
     for i in range(5):
         for a in range(2):
             update[i:i + 1, a * 256:(a + 1) * 256] = answer[i][a:a + 1]
-            packed[8 * a + i:8 * a + i + 1, :] = answer[i][a:a + 1]
+            for half in range(2):
+                at = 10 * a + 5 * half + i
+                own[at:at + 1, :] = answer[i][a:a + 1, 128 * half:128 * half + 128]
+    packed[...] = jnp.broadcast_to(own[...][None], packed.shape)
 
 
 def solve(parts):
     return pl.pallas_call(
         solve_kernel,
         name="solve",
-        out_shape=(shape((5, STAR_DEV)), shape((16, 256))),
+        out_shape=(shape((5, STAR_DEV)), shape((16, 24, 128))),
         in_specs=[VM],
         out_specs=(VM, VM),
-        scratch_shapes=[pltpu.VMEM((40, 256), F32)],
+        scratch_shapes=[pltpu.VMEM((40, 256), F32), pltpu.VMEM((24, 128), F32)],
     )(parts)
 
 
-def fit_kernel(bounds, sk, inv, ps, table, res0, res1, res2, res3, out0, out1, out2, out3, fit):
+def fit_kernel(
+    bounds, core, star, inv, ps, near, far, res0, res1, res2, res3, out0, out1, out2, out3, table, fit
+):
+    for g in range(16):
+        for a in range(2):
+            for half in range(2):
+                rows = slice(10 * a + 5 * half, 10 * a + 5 * half + 5)
+                table[4 * g + 2 * core[0] + a, :5, 128 * half:128 * half + 128] = near[g, rows, :]
+                table[4 * g + 2 - 2 * core[0] + a, :5, 128 * half:128 * half + 128] = far[g, rows, :]
+
     def look_up(c, h_from, h0):
-        star = sk[pl.ds(pl.multiple_of(c * 8, 8), 8), :]
-        at = star & 127
-        rel = jnp.where(star >= h_from * 256, (star >> 7) - 2 * h0, -1)
+        ids = star[c]
+        at = ids & 127
+        rel = jnp.where(ids >= h_from * 256, (ids >> 7) - 2 * h0, -1)
         found = [jnp.zeros((8, 128), F32)] * 5
         for k in range(2 * HW):
             hit = rel == k
@@ -413,15 +487,15 @@
                     jnp.broadcast_to(row, (8, 128)), at, axis=1, mode="promise_in_bounds"
                 )
                 found[q] = jnp.where(hit, value, found[q])
-        total = ps[pl.ds(pl.multiple_of(c * 8, 8), 8), :] * found[0]
+        total = ps[c] * found[0]
         for q in range(1, 5):
-            total = total + ps[pl.ds(pl.multiple_of(q * ROWS + c * 8, 8), 8), :] * found[q]
+            total = total + ps[q * 32 + c] * found[q]
         return total
 
     def chunks(n, carry):
         for u in range(PAIR):
             c = n * PAIR + u
-            fit[pl.ds(pl.multiple_of(c * 8, 8), 8), :] = look_up(c, bounds[c], bounds[c])
+            fit[c] = look_up(c, bounds[c], bounds[c])
         return carry
 
     lax.fori_loop(0, 32 // PAIR, chunks, 0)
@@ -429,27 +503,27 @@
     def rest(c, carry):
         def more(w, carry):
             h_from = bounds[c] + w * HW
-            fit[pl.ds(pl.multiple_of(c * 8, 8), 8), :] += look_up(c, h_from, jnp.minimum(h_from, NHI - HW))
+            fit[c] += look_up(c, h_from, jnp.minimum(h_from, NHI - HW))
             return carry
 
         lax.fori_loop(1, (bounds[32 + c] - bounds[c]) // HW + 1, more, 0)
         return carry
 
     lax.fori_loop(0, bounds[64], rest, 0)
-    total = stacked(res0, res1, res2, res3) - pick_lanes(fit[...].T, inv[...])
+    total = stacked(res0, res1, res2, res3) - pick_rows(from_chunks([fit[c] for c in range(32)]).T, inv[...])
     for d, ref in enumerate((out0, out1, out2, out3)):
         ref[...] = total[d * CAP:(d + 1) * CAP]
 
 
-def apply_fit(bounds, sk, inv, ps, table, res):
+def apply_fit(bounds, core, star, inv, ps, near, far, res):
     return pl.pallas_call(
         fit_kernel,
         name="fit",
         out_shape=(shape((CAP, ROWS)),) * 4,
-        in_specs=[SM] + [VM] * 8,
+        in_specs=[SM, SM] + [VM] * 9,
         out_specs=(VM,) * 4,
-        scratch_shapes=[pltpu.VMEM((ROWS, SLOTS), F32)],
-    )(bounds, sk, inv, ps, table, *res)
+        scratch_shapes=[pltpu.VMEM((NHI, 8, 256), F32), pltpu.VMEM((32, 8, 128), F32)],
+    )(bounds, core, star, inv, ps, near, far, *res)
 
 
 def to_sky(slabs, sign):
@@ -470,24 +544,20 @@
     outgoing, slots = pack(sky, block_dest, block_count, star_design.transpose(1, 0, 2), star_local)
     incoming = to_sky(outgoing, 1)
 
-    piece = attitude.astype(F32).reshape(3, 2, 128).transpose(1, 0, 2).reshape(6, 128)
-    piece = jnp.pad(piece, ((0, 2), (0, 0)))
-    knots = lax.all_to_all(jnp.broadcast_to(piece[None], (tm, 8, 128)), "tm", 0, 0, tiled=True)
+    knots = lax.all_to_all(pieces(attitude, tm), "tm", 0, 0, tiled=True)
     tiles = win_start >> 7
     out_res = residuals(win_start, tiles, slots, block_count, knots, obs_value, design.transpose(0, 2, 1))
     in_res = to_sky(out_res, 1)
 
-    sk, skt, idx, inv, ps, bounds = sort_slots(incoming)
-    mine, theirs = scatter(bounds, core[None], sk, skt, idx, ps, in_res)
+    star, skt, rank, came, ps, bounds = sort_slots(incoming)
+    mine, theirs = scatter(bounds, core[None], star, skt, rank, ps, in_res)
     pair_sum = mine + lax.ppermute(theirs, "tm", swap)
     parts = lax.all_to_all(pair_sum, "tm", 0, 0, tiled=True, axis_index_groups=chips)
     own_update, packed = solve(parts)
-    other = lax.ppermute(packed, "tm", swap)
-    both = jnp.where(core == 0, jnp.stack([packed, other]), jnp.stack([other, packed]))
-    table = lax.all_to_all(
-        jnp.broadcast_to(both[None], (16, 2, 16, 256)), "tm", 0, 0, tiled=True, axis_index_groups=chips
-    ).reshape(NHI, 8, 256)
-    updated = apply_fit(bounds, sk, inv, ps, table, in_res)
+    near = lax.all_to_all(packed, "tm", 0, 0, tiled=True, axis_index_groups=chips)
+    inv = invert(came)
+    far = lax.ppermute(near, "tm", swap)
+    updated = apply_fit(bounds, core[None], star, inv, ps, near, far, in_res)
     returned = to_sky(updated, -1)
     result = collect(slots, block_count, returned)
     return (result, own_update)

time: 118 us -> 113 us (0.958)
  blocking collectives: 35.7 us -> 32.1 us
  Pallas kernels: 41.4 us -> 43.1 us
  waiting for transfers between devices: 7.71 us -> 6.31 us
    pallas_call x1 -> x3, Pallas kernels: 4.74 us -> 9.87 us  [the longest x1 6.06 us: sort_slots(): pl.pallas_call(sort_kernel, name='sort', out_shape=(shape((32, 8, 128), I...]
    all_to_all x1, blocking collectives: 15.4 us -> 11.8 us  [steps(): lax.all_to_all(packed, 'tm', 0, 0, tiled=True, axis_index_groups=chips)]
    pallas_call x1, Pallas kernels: 15.5 us -> 13.1 us  [scatter(): pl.pallas_call(scatter_kernel, name='scatter', out_shape=(shape((16, 40,...]
    ppermute x1, waiting for transfers between devices: 1.39 us -> 0.01 us  [steps(): far = lax.ppermute(near, 'tm', swap)]
    unnamed x20 -> x24, local copies, waits for them, and re-layouts: 2.6 us -> 3.3 us
  transfers between devices with their start and end apart: 12 -> 12, of which waited for: 4 -> 3; matrix products, arithmetic and copies ran while one was open for 1% -> 1% of each run, Pallas kernels for 12% -> 16%
where the time goes in v4:
time: 113 us; the launch traced here: 112 us
  Pallas kernels  43.1 us (38%)
  blocking collectives  32.1 us (28%)
  starting transfers between devices  23.5 us (21%)
  waiting for transfers between devices  6.31 us (6%)
  local copies, waits for them, and re-layouts  3.3 us (3%)
  other arithmetic  2.34 us (2%)
  between operations  1.4 us (1%)
    all_to_all x1, blocking collectives, steps(): lax.all_to_all(pair_sum, 'tm', 0, 0, tiled=True, axis_index_groups=chips)  20.3 us
    ppermute x9, starting transfers between devices, to_sky(): lax.ppermute(slabs[d], 'sky', [(i, (i + sign * d) % n) for i in range(n)])  15.2 us
    pallas_call x1, Pallas kernels, scatter(): pl.pallas_call(scatter_kernel, name='scatter', out_shape=(shape((16, 40,...  13.1 us
    all_to_all x1, blocking collectives, steps(): lax.all_to_all(packed, 'tm', 0, 0, tiled=True, axis_index_groups=chips)  11.8 us
    all_to_all x1, starting transfers between devices, steps(): knots = lax.all_to_all(pieces(attitude, tm), 'tm', 0, 0, tiled=True)  8.27 us
    pallas_call x1, Pallas kernels, apply_fit(): pl.pallas_call(fit_kernel, name='fit', out_shape=(shape((CAP, ROWS)),) *...  7.06 us
    pallas_call x1, Pallas kernels, residuals(): pl.pallas_call(residual_kernel, name='residuals', grid=(NBLK // STEP,), o...  6.31 us
    pallas_call x1, Pallas kernels, sort_slots(): pl.pallas_call(sort_kernel, name='sort', out_shape=(shape((32, 8, 128), I...  6.06 us
  transfers between devices with their start and end apart: 12, of which 3 were waited for; matrix products, arithmetic and copies ran while one was open for 1% of the time, Pallas kernels for 16%

profile of v4, /device:TPU:0, one launch (start us, length us, event | category | flops | bytes accessed | tf_op | source)
XLA Modules:
  0.0 112.1 jit_solution(16769714096210537953)
XLA Ops:
  0.6 1.4 %pieces.1 = f32[32,8,128]{2,1,0:T(8,128)} custom-call(bf16[3,256]{1,0:T(4,128)(2,1)} %attitude.1), custom_call_target="tpu_custom_call" | custom-call | tf_op jit(solution)/shard_map/pieces/pallas_call | solution.py:98
  2.0 8.3 %all-to-all-start = ((f32[32,8,128]{2,1,0:T(8,128)}), f32[32,8,128]{2,1,0:T(8,128)S(1)}, u32[]{:S(2)}, u32[]{:S(2)}) async-start(f32[32,8,128]{2,1,0:T(8,128)} %pieces.1), calls=%async_computation | async-start | bytes 262144 | tf_op jit(solution)/shard_map/all_to_all | solution.py:547
  10.9 3.1 %pack.1 = (f32[192,256]{1,0:T(8,128)}, f32[192,256]{1,0:T(8,128)}, f32[192,256]{1,0:T(8,128)}, f32[192,256]{1,0:T(8,128)}, s32[64]{0:T(128)}) custom-call(s32[1]{0:T(128)} %bitcast.sky, s32[64]{0:T(128)} %dest.1, s32[1]{0:T(128)S(6)} %copy.10.count, f32[5,64,256]{2,1,0:T(8,128)} %bitcast.5, s32[64,256]{1,0:T(8,128)} %stars.1), custom_call_target="tpu_custom_call" | custom-call | tf_op jit(solution)/shard_map/pack/pallas_call | solution.py:57
  14.1 1.6 %collective-permute-start = (f32[192,256]{1,0:T(8,128)}, f32[192,256]{1,0:T(8,128)S(1)}, u32[]{:S(2)}, u32[]{:S(2)}) collective-permute-start(f32[192,256]{1,0:T(8,128)} %get-tuple-element.27), channel_id=1, source_target_pairs={{0,32},{32,64},{64,96},{96,0},{1,33},{33,65},{65,97},{97,1},{2,34}... | collective-permute-start | bytes 589832 | tf_op jit(solution)/shard_map/ppermute | solution.py:532
  15.7 2.9 %collective-permute-start.1 = (f32[192,256]{1,0:T(8,128)}, f32[192,256]{1,0:T(8,128)S(1)}, u32[]{:S(2)}, u32[]{:S(2)}) collective-permute-start(f32[192,256]{1,0:T(8,128)} %get-tuple-element.28), channel_id=1, source_target_pairs={{0,64},{32,96},{64,0},{96,32},{1,65},{33,97},{65,1},{97,33},{2,66}... | collective-permute-start | bytes 589832 | tf_op jit(solution)/shard_map/ppermute | solution.py:532
  18.6 1.2 %collective-permute-start.2 = (f32[192,256]{1,0:T(8,128)}, f32[192,256]{1,0:T(8,128)S(1)}, u32[]{:S(2)}, u32[]{:S(2)}) collective-permute-start(f32[192,256]{1,0:T(8,128)} %get-tuple-element.29), channel_id=1, source_target_pairs={{0,96},{32,0},{64,32},{96,64},{1,97},{33,1},{65,33},{97,65},{2,98}... | collective-permute-start | bytes 589832 | tf_op jit(solution)/shard_map/ppermute | solution.py:532
  19.8 1.2 %broadcast_shift-right-arithmetic_fusion.tiles = s32[64]{0:T(128)} fusion(s32[64]{0:T(128)} %start.1), kind=kLoop, calls=%fused_computation | loop fusion | flops 64 | bytes 512 | tf_op jit(solution)/shard_map/shift_right_arithmetic | solution.py:548
  21.6 6.3 %residuals.1 = (f32[32,256]{1,0:T(8,128)}, f32[32,256]{1,0:T(8,128)}, f32[32,256]{1,0:T(8,128)}, f32[32,256]{1,0:T(8,128)}) custom-call(s32[64]{0:T(128)} %start.1, s32[64]{0:T(128)} %broadcast_shift-right-arithmetic_fusion.tiles, s32[64]{0:T(128)} %get-tuple-element.25.slots, s32[1]{0:T(128)S(6)} %copy.10.count, f32[32,8,128]{2,1,0:T(8,128)} %copy-done.1, ...), custom_call_target="tpu_custom_call" | custom-call | tf_op jit(solution)/shard_map/residuals/pallas_call | solution.py:153
  29.5 2.0 %collective-permute-start.5 = (f32[32,256]{1,0:T(8,128)}, f32[32,256]{1,0:T(8,128)S(1)}, u32[]{:S(2)}, u32[]{:S(2)}) collective-permute-start(f32[32,256]{1,0:T(8,128)} %get-tuple-element.39), channel_id=1, source_target_pairs={{0,96},{32,0},{64,32},{96,64},{1,97},{33,1},{65,33},{97,65},{2,98}... | collective-permute-start | bytes 98312 | tf_op jit(solution)/shard_map/ppermute | solution.py:532
  32.2 6.1 %sort.1 = (s32[32,8,128]{2,1,0:T(8,128)}, s32[4,128,128]{2,1,0:T(8,128)}, s32[128,256]{1,0:T(8,128)}, s32[256,128]{1,0:T(8,128)}, f32[160,8,128]{2,1,0:T(8,128)}, /*index=5*/s32[65]{0:T(128)}) custom-call(f32[192,256]{1,0:T(8,128)} %get-tuple-element.26.inc0, f32[192,256]{1,0:T(8,128)} %copy-done.3, f32[192,256]{1,0:T(8,128)} %copy-done.4, f32[192,256]{1,0:T(8,128)} %copy-done.5), custom_call_target="tpu_custom_call" | custom-call | tf_op jit(solution)/shard_map/sort/pallas_call | solution.py:297
  39.0 13.1 %scatter.1 = (f32[16,40,256]{2,1,0:T(8,128)}, f32[16,40,256]{2,1,0:T(8,128)}) custom-call(s32[65]{0:T(128)} %get-tuple-element.30.bounds, s32[1]{0:T(128)} %bitcast.2.core, s32[32,8,128]{2,1,0:T(8,128)} %get-tuple-element.31.star, s32[4,128,128]{2,1,0:T(8,128)} %get-tuple-element.34.skt, s32[128,256]{1,0:T(8,128)} %get-tuple-element.35.rank, ...), custom_call_target="tpu_custom_call" | custom-call | tf_op jit(solution)/shard_map/scatter/pallas_call | solution.py:396
  52.0 2.3 %collective-permute-done.6 = f32[16,40,256]{2,1,0:T(8,128)S(1)} collective-permute-done((f32[16,40,256]{2,1,0:T(8,128)}, f32[16,40,256]{2,1,0:T(8,128)S(1)}, u32[]{:S(2)}, u32[]{:S(2)}) %collective-permute-start.6) | collective-permute-done | bytes 655392 | tf_op jit(solution)/shard_map/ppermute | solution.py:554
  54.4 1.2 %add.8 = f32[16,40,256]{2,1,0:T(8,128)S(1)} add(f32[16,40,256]{2,1,0:T(8,128)} %get-tuple-element.40, f32[16,40,256]{2,1,0:T(8,128)S(1)} %collective-permute-done.6) | non-fusion elementwise | flops 163840 | bytes 1966080 | tf_op jit(solution)/shard_map/add | solution.py:554
  55.5 20.3 %all_to_all.15.parts = f32[16,40,256]{2,1,0:T(8,128)} all-to-all(f32[16,40,256]{2,1,0:T(8,128)S(1)} %add.8), channel_id=1, replica_groups={{0,2,4,6,8,10,12,14,16,18,20,22,24,26,28,30},{1,3,5,7,9,11,13,15,17,19,..., dimensions={0} | all-to-all | bytes 1310720 | tf_op jit(solution)/shard_map/all_to_all | solution.py:555
  75.8 1.9 %solve.1 = (f32[5,512]{1,0:T(8,128)}, f32[16,24,128]{2,1,0:T(8,128)}) custom-call(f32[16,40,256]{2,1,0:T(8,128)} %all_to_all.15.parts), custom_call_target="tpu_custom_call" | custom-call | tf_op jit(solution)/shard_map/solve/pallas_call | solution.py:457
  77.7 11.8 %all_to_all.16.near = f32[16,24,128]{2,1,0:T(8,128)S(1)} all-to-all(f32[16,24,128]{2,1,0:T(8,128)} %get-tuple-element.42), channel_id=1, replica_groups={{0,2,4,6,8,10,12,14,16,18,20,22,24,26,28,30},{1,3,5,7,9,11,13,15,17,19,..., dimensions={0} | all-to-all | bytes 393216 | tf_op jit(solution)/shard_map/all_to_all | solution.py:557
  89.6 2.4 %invert.1.inv = s32[128,256]{1,0:T(8,128)} custom-call(s32[256,128]{1,0:T(8,128)} %get-tuple-element.32.came), custom_call_target="tpu_custom_call" | custom-call | tf_op jit(solution)/shard_map/invert/pallas_call | solution.py:321
  92.7 7.1 %fit.1 = (f32[32,256]{1,0:T(8,128)}, f32[32,256]{1,0:T(8,128)}, f32[32,256]{1,0:T(8,128)}, f32[32,256]{1,0:T(8,128)}) custom-call(s32[65]{0:T(128)} %get-tuple-element.30.bounds, s32[1]{0:T(128)} %bitcast.2.core, s32[32,8,128]{2,1,0:T(8,128)} %get-tuple-element.31.star, s32[128,256]{1,0:T(8,128)} %invert.1.inv, f32[160,8,128]{2,1,0:T(8,128)} %get-tuple-element.33.ps, ...), custom_call_target="tpu_custom_call" | custom-call | tf_op jit(solution)/shard_map/fit/pallas_call | solution.py:519
  99.8 1.4 %collective-permute-start.8 = (f32[32,256]{1,0:T(8,128)}, f32[32,256]{1,0:T(8,128)S(1)}, u32[]{:S(2)}, u32[]{:S(2)}) collective-permute-start(f32[32,256]{1,0:T(8,128)} %get-tuple-element.44), channel_id=1, source_target_pairs={{0,96},{32,0},{64,32},{96,64},{1,97},{33,1},{65,33},{97,65},{2,98}... | collective-permute-start | bytes 98312 | tf_op jit(solution)/shard_map/ppermute | solution.py:532
  101.1 3.2 %collective-permute-start.9 = (f32[32,256]{1,0:T(8,128)}, f32[32,256]{1,0:T(8,128)S(1)}, u32[]{:S(2)}, u32[]{:S(2)}) collective-permute-start(f32[32,256]{1,0:T(8,128)} %get-tuple-element.45), channel_id=1, source_target_pairs={{0,64},{32,96},{64,0},{96,32},{1,65},{33,97},{65,1},{97,33},{2,66}... | collective-permute-start | bytes 98312 | tf_op jit(solution)/shard_map/ppermute | solution.py:532
  104.4 1.3 %collective-permute-start.10 = (f32[32,256]{1,0:T(8,128)}, f32[32,256]{1,0:T(8,128)S(1)}, u32[]{:S(2)}, u32[]{:S(2)}) collective-permute-start(f32[32,256]{1,0:T(8,128)} %get-tuple-element.46), channel_id=1, source_target_pairs={{0,32},{32,64},{64,96},{96,0},{1,33},{33,65},{65,97},{97,1},{2,34}... | collective-permute-start | bytes 98312 | tf_op jit(solution)/shard_map/ppermute | solution.py:532
  105.7 1.2 %collective-permute-done.9.rows2 = f32[32,256]{1,0:T(8,128)S(1)} collective-permute-done((f32[32,256]{1,0:T(8,128)}, f32[32,256]{1,0:T(8,128)S(1)}, u32[]{:S(2)}, u32[]{:S(2)}) %collective-permute-start.9) | collective-permute-done | bytes 32800 | tf_op jit(solution)/shard_map/ppermute | solution.py:532
  106.9 2.8 %collective-permute-done.10.rows3 = f32[32,256]{1,0:T(8,128)S(1)} collective-permute-done((f32[32,256]{1,0:T(8,128)}, f32[32,256]{1,0:T(8,128)S(1)}, u32[]{:S(2)}, u32[]{:S(2)}) %collective-permute-start.10) | collective-permute-done | bytes 32800 | tf_op jit(solution)/shard_map/ppermute | solution.py:532
  110.3 1.7 %collect.1 = f32[64,256]{1,0:T(8,128)} custom-call(s32[64]{0:T(128)} %get-tuple-element.25.slots, s32[1]{0:T(128)S(6)} %copy.10.count, f32[32,256]{1,0:T(8,128)} %get-tuple-element.43.rows0, f32[32,256]{1,0:T(8,128)} %copy-done.9, f32[32,256]{1,0:T(8,128)} %copy-done.10, f32[32,256]{1,0:T(8,128)} %copy-done.11), custom_call_target="tpu_custom_call" | custom-call | tf_op jit(solution)/shard_map/collect/pallas_call | solution.py:81
  (37 shorter events, 4.9 us)
Async XLA Ops:
  2.0 18.9 %all-to-all-start = ((f32[32,8,128]{2,1,0:T(8,128)}), f32[32,8,128]{2,1,0:T(8,128)S(1)}, u32[]{:S(2)}, u32[]{:S(2)}) async-start(f32[32,8,128]{2,1,0:T(8,128)} %pieces.1), calls=%async_computation | async-start | bytes 262144 | tf_op jit(solution)/shard_map/all_to_all | solution.py:547
  14.1 15.4 %collective-permute-start = (f32[192,256]{1,0:T(8,128)}, f32[192,256]{1,0:T(8,128)S(1)}, u32[]{:S(2)}, u32[]{:S(2)}) collective-permute-start(f32[192,256]{1,0:T(8,128)} %get-tuple-element.27), channel_id=1, source_target_pairs={{0,32},{32,64},{64,96},{96,0},{1,33},{33,65},{65,97},{97,1},{2,34}... | collective-permute-start | bytes 589832 | tf_op jit(solution)/shard_map/ppermute | solution.py:532
  15.7 15.8 %collective-permute-start.1 = (f32[192,256]{1,0:T(8,128)}, f32[192,256]{1,0:T(8,128)S(1)}, u32[]{:S(2)}, u32[]{:S(2)}) collective-permute-start(f32[192,256]{1,0:T(8,128)} %get-tuple-element.28), channel_id=1, source_target_pairs={{0,64},{32,96},{64,0},{96,32},{1,65},{33,97},{65,1},{97,33},{2,66}... | collective-permute-start | bytes 589832 | tf_op jit(solution)/shard_map/ppermute | solution.py:532
  18.6 12.9 %collective-permute-start.2 = (f32[192,256]{1,0:T(8,128)}, f32[192,256]{1,0:T(8,128)S(1)}, u32[]{:S(2)}, u32[]{:S(2)}) collective-permute-start(f32[192,256]{1,0:T(8,128)} %get-tuple-element.29), channel_id=1, source_target_pairs={{0,96},{32,0},{64,32},{96,64},{1,97},{33,1},{65,33},{97,65},{2,98}... | collective-permute-start | bytes 589832 | tf_op jit(solution)/shard_map/ppermute | solution.py:532
  20.9 0.7 copy-start.1
  27.9 10.4 %collective-permute-start.3 = (f32[32,256]{1,0:T(8,128)}, f32[32,256]{1,0:T(8,128)S(1)}, u32[]{:S(2)}, u32[]{:S(2)}) collective-permute-start(f32[32,256]{1,0:T(8,128)} %get-tuple-element.37), channel_id=1, source_target_pairs={{0,32},{32,64},{64,96},{96,0},{1,33},{33,65},{65,97},{97,1},{2,34}... | collective-permute-start | bytes 98312 | tf_op jit(solution)/shard_map/ppermute | solution.py:532
  28.7 9.6 %collective-permute-start.4 = (f32[32,256]{1,0:T(8,128)}, f32[32,256]{1,0:T(8,128)S(1)}, u32[]{:S(2)}, u32[]{:S(2)}) collective-permute-start(f32[32,256]{1,0:T(8,128)} %get-tuple-element.38), channel_id=1, source_target_pairs={{0,64},{32,96},{64,0},{96,32},{1,65},{33,97},{65,1},{97,33},{2,66}... | collective-permute-start | bytes 98312 | tf_op jit(solution)/shard_map/ppermute | solution.py:532
  29.5 2.0 %copy-start.3 = (f32[192,256]{1,0:T(8,128)}, f32[192,256]{1,0:T(8,128)S(1)}, u32[]{:S(2)}) copy-start(f32[192,256]{1,0:T(8,128)S(1)} %collective-permute-done.inc1) | copy-start | bytes 589828
  29.5 8.9 %collective-permute-start.5 = (f32[32,256]{1,0:T(8,128)}, f32[32,256]{1,0:T(8,128)S(1)}, u32[]{:S(2)}, u32[]{:S(2)}) collective-permute-start(f32[32,256]{1,0:T(8,128)} %get-tuple-element.39), channel_id=1, source_target_pairs={{0,96},{32,0},{64,32},{96,64},{1,97},{33,1},{65,33},{97,65},{2,98}... | collective-permute-start | bytes 98312 | tf_op jit(solution)/shard_map/ppermute | solution.py:532
  31.5 0.7 copy-start.4
  31.5 0.7 copy-start.5
  38.3 0.6 copy-start.6
  38.3 0.6 copy-start.7
  38.4 0.6 copy-start.8
  52.0 2.3 %collective-permute-start.6 = (f32[16,40,256]{2,1,0:T(8,128)}, f32[16,40,256]{2,1,0:T(8,128)S(1)}, u32[]{:S(2)}, u32[]{:S(2)}) collective-permute-start(f32[16,40,256]{2,1,0:T(8,128)} %get-tuple-element.41), channel_id=1, source_target_pairs={{0,1},{1,0},{2,3},{3,2},{4,5},{5,4},{6,7},{7,6},{8,9},{9,8},{10,11... | collective-permute-start | bytes 1966088 | tf_op jit(solution)/shard_map/ppermute | solution.py:554
  89.6 2.5 %copy-start = (f32[16,24,128]{2,1,0:T(8,128)}, f32[16,24,128]{2,1,0:T(8,128)S(1)}, u32[]{:S(2)}) copy-start(f32[16,24,128]{2,1,0:T(8,128)S(1)} %all_to_all.16.near) | copy-start | bytes 589828
  89.6 2.5 %collective-permute-start.7 = (f32[16,24,128]{2,1,0:T(8,128)S(1)}, f32[16,24,128]{2,1,0:T(8,128)S(1)}, u32[]{:S(2)}, u32[]{:S(2)}) collective-permute-start(f32[16,24,128]{2,1,0:T(8,128)S(1)} %all_to_all.16.near), channel_id=1, source_target_pairs={{0,1},{1,0},{2,3},{3,2},{4,5},{5,4},{6,7},{7,6},{8,9},{9,8},{10,11... | collective-permute-start | bytes 589832 | tf_op jit(solution)/shard_map/ppermute | solution.py:559
  92.0 0.7 copy-start.2
  99.8 5.9 %collective-permute-start.8 = (f32[32,256]{1,0:T(8,128)}, f32[32,256]{1,0:T(8,128)S(1)}, u32[]{:S(2)}, u32[]{:S(2)}) collective-permute-start(f32[32,256]{1,0:T(8,128)} %get-tuple-element.44), channel_id=1, source_target_pairs={{0,96},{32,0},{64,32},{96,64},{1,97},{33,1},{65,33},{97,65},{2,98}... | collective-permute-start | bytes 98312 | tf_op jit(solution)/shard_map/ppermute | solution.py:532
  101.1 5.8 %collective-permute-start.9 = (f32[32,256]{1,0:T(8,128)}, f32[32,256]{1,0:T(8,128)S(1)}, u32[]{:S(2)}, u32[]{:S(2)}) collective-permute-start(f32[32,256]{1,0:T(8,128)} %get-tuple-element.45), channel_id=1, source_target_pairs={{0,64},{32,96},{64,0},{96,32},{1,65},{33,97},{65,1},{97,33},{2,66}... | collective-permute-start | bytes 98312 | tf_op jit(solution)/shard_map/ppermute | solution.py:532
  104.4 5.3 %collective-permute-start.10 = (f32[32,256]{1,0:T(8,128)}, f32[32,256]{1,0:T(8,128)S(1)}, u32[]{:S(2)}, u32[]{:S(2)}) collective-permute-start(f32[32,256]{1,0:T(8,128)} %get-tuple-element.46), channel_id=1, source_target_pairs={{0,32},{32,64},{64,96},{96,0},{1,33},{33,65},{65,97},{97,1},{2,34}... | collective-permute-start | bytes 98312 | tf_op jit(solution)/shard_map/ppermute | solution.py:532
  105.7 4.0 %copy-start.9 = (f32[32,256]{1,0:T(8,128)}, f32[32,256]{1,0:T(8,128)S(1)}, u32[]{:S(2)}) copy-start(f32[32,256]{1,0:T(8,128)S(1)} %collective-permute-done.8.rows1) | copy-start | bytes 98308
  106.9 2.8 %copy-start.10 = (f32[32,256]{1,0:T(8,128)}, f32[32,256]{1,0:T(8,128)S(1)}, u32[]{:S(2)}) copy-start(f32[32,256]{1,0:T(8,128)S(1)} %collective-permute-done.9.rows2) | copy-start | bytes 98308
  109.7 0.6 copy-start.11

commit v5 on v4

--- a/solution.py
+++ b/solution.py
@@ -19,6 +19,7 @@
 BF16 = jnp.bfloat16
 I32 = jnp.int32
 VM = pl.BlockSpec(memory_space=pltpu.VMEM)
+ROOM = pltpu.CompilerParams(vmem_limit_bytes=24 << 20)
 SM = pl.BlockSpec(memory_space=pltpu.SMEM)
 
 
@@ -57,6 +58,7 @@
     *slabs, slots = pl.pallas_call(
         pack_kernel,
         name="pack",
+        compiler_params=ROOM,
         out_shape=(shape((192, ROWS)),) * 4 + (shape((NBLK,), I32),),
         in_specs=[SM, SM, SM, VM, VM],
         out_specs=(VM,) * 4 + (SM,),
@@ -81,6 +83,7 @@
     return pl.pallas_call(
         collect_kernel,
         name="collect",
+        compiler_params=ROOM,
         out_shape=shape((NBLK, ROWS)),
         in_specs=[SM, SM] + [VM] * 4,
         out_specs=VM,
@@ -96,7 +99,7 @@
 
 def pieces(attitude, copies):
     return pl.pallas_call(
-        piece_kernel, name="pieces", out_shape=shape((copies, 8, 128)), in_specs=[VM], out_specs=VM
+        piece_kernel, name="pieces", compiler_params=ROOM, out_shape=shape((copies, 8, 128)), in_specs=[VM], out_specs=VM
     )(attitude)
 
 
@@ -113,10 +116,10 @@
         def place(b, carry):
             tile = tiles[b]
             after = jnp.minimum(tile + 1, 63)
-            shift[pl.ds(b, 1), :] = jnp.full((1, 128), start[b] % 128, I32)
+            shift[pl.ds(b, 1), :] = jnp.full((1, 128), start[b] & 127, I32)
             for axis in range(3):
-                near[axis, pl.ds(b, 1), :] = knots[tile // 2, pl.ds(3 * (tile % 2) + axis, 1), :]
-                far[axis, pl.ds(b, 1), :] = knots[after // 2, pl.ds(3 * (after % 2) + axis, 1), :]
+                near[axis, pl.ds(b, 1), :] = knots[tile >> 1, pl.ds(3 * (tile & 1) + axis, 1), :]
+                far[axis, pl.ds(b, 1), :] = knots[after >> 1, pl.ds(3 * (after & 1) + axis, 1), :]
             return carry
 
         lax.fori_loop(0, NBLK, place, 0, unroll=4)
@@ -153,6 +156,7 @@
     return pl.pallas_call(
         residual_kernel,
         name="residuals",
+        compiler_params=ROOM,
         grid=(NBLK // STEP,),
         out_shape=(shape((CAP, ROWS)),) * 4,
         in_specs=[
@@ -297,6 +301,7 @@
     return pl.pallas_call(
         sort_kernel,
         name="sort",
+        compiler_params=ROOM,
         out_shape=(
             shape((32, 8, 128), I32),
             shape((4, 128, 128), I32),
@@ -319,7 +324,7 @@
 
 def invert(came):
     return pl.pallas_call(
-        invert_kernel, name="invert", out_shape=shape((SLOTS, ROWS), I32), in_specs=[VM], out_specs=VM
+        invert_kernel, name="invert", compiler_params=ROOM, out_shape=shape((SLOTS, ROWS), I32), in_specs=[VM], out_specs=VM
     )(came)
 
 
@@ -396,6 +401,7 @@
     return pl.pallas_call(
         scatter_kernel,
         name="scatter",
+        compiler_params=ROOM,
         out_shape=(shape((16, 40, 256)), shape((16, 40, 256))),
         in_specs=[SM, SM] + [VM] * 8,
         out_specs=(VM, VM),
@@ -457,6 +463,7 @@
     return pl.pallas_call(
         solve_kernel,
         name="solve",
+        compiler_params=ROOM,
         out_shape=(shape((5, STAR_DEV)), shape((16, 24, 128))),
         in_specs=[VM],
         out_specs=(VM, VM),
@@ -519,6 +526,7 @@
     return pl.pallas_call(
         fit_kernel,
         name="fit",
+        compiler_params=ROOM,
         out_shape=(shape((CAP, ROWS)),) * 4,
         in_specs=[SM, SM] + [VM] * 9,
         out_specs=(VM,) * 4,
@@ -534,19 +542,28 @@
     return [slabs[0]] + [moved[d] for d in (1, 2, 3)]
 
 
+def in_hbm(x):
+    return pltpu.with_memory_space_constraint(x, pltpu.HBM)
+
+
 def steps(attitude, win_start, design, obs_value, star_design, star_local, block_dest, block_count):
+    attitude, starts, obs_value, star_local, block_dest = map(
+        in_hbm, (attitude, win_start, obs_value, star_local, block_dest)
+    )
+    partials = in_hbm(star_design.transpose(1, 0, 2))
+    design_t = in_hbm(design.transpose(0, 2, 1))
     tm = lax.axis_size("tm")
     core = (lax.axis_index("tm") % 2).astype(I32)
     swap = [(i, i ^ 1) for i in range(tm)]
     chips = [list(range(0, tm, 2)), list(range(1, tm, 2))]
 
     sky = lax.axis_index("sky").astype(I32)[None]
-    outgoing, slots = pack(sky, block_dest, block_count, star_design.transpose(1, 0, 2), star_local)
+    outgoing, slots = pack(sky, block_dest, block_count, partials, star_local)
     incoming = to_sky(outgoing, 1)
 
     knots = lax.all_to_all(pieces(attitude, tm), "tm", 0, 0, tiled=True)
     tiles = win_start >> 7
-    out_res = residuals(win_start, tiles, slots, block_count, knots, obs_value, design.transpose(0, 2, 1))
+    out_res = residuals(starts, tiles, slots, block_count, knots, obs_value, design_t)
     in_res = to_sky(out_res, 1)
 
     star, skt, rank, came, ps, bounds = sort_slots(incoming)

time: 113 us -> 97.4 us (0.86)
  Pallas kernels: 43.1 us -> 33.1 us
  local copies, waits for them, and re-layouts: 3.3 us -> 0 us
  other arithmetic: 2.34 us -> 0.74 us
    pallas_call x9, Pallas kernels: 43.1 us -> 33.1 us  [the longest x1 11.3 us: scatter(): pl.pallas_call(scatter_kernel, name='scatter', compiler_params=ROOM, out_...]
    unnamed x24 -> x0, local copies, waits for them, and re-layouts: 3.3 us -> none
  transfers between devices with their start and end apart: 12 -> 12, of which waited for: 3 -> 4; matrix products, arithmetic and copies ran while one was open for 1% -> 1% of each run, Pallas kernels for 16% -> 13%
where the time goes in v5:
time: 97.4 us; the launch traced here: 97.1 us
  Pallas kernels  33.1 us (34%)
  blocking collectives  31.5 us (32%)
  starting transfers between devices  23.8 us (24%)
  waiting for transfers between devices  6.51 us (7%)
  between operations  1.38 us (1%)
    all_to_all x1, blocking collectives, steps(): lax.all_to_all(pair_sum, 'tm', 0, 0, tiled=True, axis_index_groups=chips)  20.1 us
    ppermute x9, starting transfers between devices, to_sky(): lax.ppermute(slabs[d], 'sky', [(i, (i + sign * d) % n) for i in range(n)])  15.5 us
    all_to_all x1, blocking collectives, steps(): lax.all_to_all(packed, 'tm', 0, 0, tiled=True, axis_index_groups=chips)  11.4 us
    pallas_call x1, Pallas kernels, scatter(): pl.pallas_call(scatter_kernel, name='scatter', compiler_params=ROOM, out_...  11.3 us
    all_to_all x1, starting transfers between devices, steps(): knots = lax.all_to_all(pieces(attitude, tm), 'tm', 0, 0, tiled=True)  8.27 us
    pallas_call x1, Pallas kernels, apply_fit(): pl.pallas_call(fit_kernel, name='fit', compiler_params=ROOM, out_shape=(s...  5.6 us
    pallas_call x1, Pallas kernels, residuals(): pl.pallas_call(residual_kernel, name='residuals', compiler_params=ROOM, g...  4.99 us
    pallas_call x1, Pallas kernels, sort_slots(): pl.pallas_call(sort_kernel, name='sort', compiler_params=ROOM, out_shape=...  4.01 us
  transfers between devices with their start and end apart: 12, of which 4 were waited for; matrix products, arithmetic and copies ran while one was open for 1% of the time, Pallas kernels for 13%

profile of v5, /device:TPU:0, one launch (start us, length us, event | category | flops | bytes accessed | tf_op | source)
XLA Modules:
  0.0 97.1 jit_solution(5131548189583897275)
XLA Ops:
  0.6 1.4 %pieces.1 = f32[32,8,128]{2,1,0:T(8,128)} custom-call(bf16[3,256]{1,0:T(4,128)(2,1)} %attitude.1), custom_call_target="tpu_custom_call" | custom-call | tf_op jit(solution)/shard_map/pieces/pallas_call | solution.py:101
  2.0 8.3 %all-to-all-start = ((f32[32,8,128]{2,1,0:T(8,128)}), f32[32,8,128]{2,1,0:T(8,128)S(1)}, u32[]{:S(2)}, u32[]{:S(2)}) async-start(f32[32,8,128]{2,1,0:T(8,128)} %pieces.1), calls=%async_computation | async-start | bytes 262144 | tf_op jit(solution)/shard_map/all_to_all | solution.py:564
  10.9 2.8 %pack.1 = (f32[192,256]{1,0:T(8,128)S(1)}, f32[192,256]{1,0:T(8,128)S(1)}, f32[192,256]{1,0:T(8,128)S(1)}, f32[192,256]{1,0:T(8,128)S(1)}, s32[64]{0:T(128)S(1)}) custom-call(s32[1]{0:T(128)} %bitcast.sky, s32[64]{0:T(128)} %dest.1, s32[1]{0:T(128)S(6)} %copy.10.count, f32[5,64,256]{2,1,0:T(8,128)} %bitcast.5, s32[64,256]{1,0:T(8,128)} %stars.1), custom_call_target="tpu_custom_call" | custom-call | tf_op jit(solution)/shard_map/pack/pallas_call | solution.py:58
  13.7 1.6 %collective-permute-start = (f32[192,256]{1,0:T(8,128)S(1)}, f32[192,256]{1,0:T(8,128)S(1)}, u32[]{:S(2)}, u32[]{:S(2)}) collective-permute-start(f32[192,256]{1,0:T(8,128)S(1)} %get-tuple-element.27), channel_id=1, source_target_pairs={{0,32},{32,64},{64,96},{96,0},{1,33},{33,65},{65,97},{97,1},{2,34}... | collective-permute-start | bytes 589832 | tf_op jit(solution)/shard_map/ppermute | solution.py:540
  15.4 2.9 %collective-permute-start.1 = (f32[192,256]{1,0:T(8,128)S(1)}, f32[192,256]{1,0:T(8,128)S(1)}, u32[]{:S(2)}, u32[]{:S(2)}) collective-permute-start(f32[192,256]{1,0:T(8,128)S(1)} %get-tuple-element.28), channel_id=1, source_target_pairs={{0,64},{32,96},{64,0},{96,32},{1,65},{33,97},{65,1},{97,33},{2,66}... | collective-permute-start | bytes 589832 | tf_op jit(solution)/shard_map/ppermute | solution.py:540
  18.2 1.2 %collective-permute-start.2 = (f32[192,256]{1,0:T(8,128)S(1)}, f32[192,256]{1,0:T(8,128)S(1)}, u32[]{:S(2)}, u32[]{:S(2)}) collective-permute-start(f32[192,256]{1,0:T(8,128)S(1)} %get-tuple-element.29), channel_id=1, source_target_pairs={{0,96},{32,0},{64,32},{96,64},{1,97},{33,1},{65,33},{97,65},{2,98}... | collective-permute-start | bytes 589832 | tf_op jit(solution)/shard_map/ppermute | solution.py:540
  20.1 5.0 %residuals.1 = (f32[32,256]{1,0:T(8,128)S(1)}, f32[32,256]{1,0:T(8,128)S(1)}, f32[32,256]{1,0:T(8,128)S(1)}, f32[32,256]{1,0:T(8,128)S(1)}) custom-call(s32[64]{0:T(128)} %start.1, s32[64]{0:T(128)S(1)} %broadcast_shift-right-arithmetic_fusion.tiles, s32[64]{0:T(128)S(1)} %get-tuple-element.25.slots, s32[1]{0:T(128)S(6)} %copy.10.count, ...), custom_call_target="tpu_custom_call" | custom-call | tf_op jit(solution)/shard_map/residuals/pallas_call | solution.py:156
  25.1 0.9 collective-permute-start.3
  26.0 1.6 %collective-permute-start.4 = (f32[32,256]{1,0:T(8,128)S(1)}, f32[32,256]{1,0:T(8,128)S(1)}, u32[]{:S(2)}, u32[]{:S(2)}) collective-permute-start(f32[32,256]{1,0:T(8,128)S(1)} %get-tuple-element.38), channel_id=1, source_target_pairs={{0,64},{32,96},{64,0},{96,32},{1,65},{33,97},{65,1},{97,33},{2,66}... | collective-permute-start | bytes 98312 | tf_op jit(solution)/shard_map/ppermute | solution.py:540
  27.6 1.3 %collective-permute-start.5 = (f32[32,256]{1,0:T(8,128)S(1)}, f32[32,256]{1,0:T(8,128)S(1)}, u32[]{:S(2)}, u32[]{:S(2)}) collective-permute-start(f32[32,256]{1,0:T(8,128)S(1)} %get-tuple-element.39), channel_id=1, source_target_pairs={{0,96},{32,0},{64,32},{96,64},{1,97},{33,1},{65,33},{97,65},{2,98}... | collective-permute-start | bytes 98312 | tf_op jit(solution)/shard_map/ppermute | solution.py:540
  28.9 4.0 %sort.1 = (s32[32,8,128]{2,1,0:T(8,128)S(1)}, s32[4,128,128]{2,1,0:T(8,128)S(1)}, s32[128,256]{1,0:T(8,128)S(1)}, s32[256,128]{1,0:T(8,128)S(1)}, f32[160,8,128]{2,1,0:T(8,128)S(1)}, /*index=5*/s32[65]{0:T(128)S(1)}) custom-call(f32[192,256]{1,0:T(8,128)S(1)} %get-tuple-element.26.inc0, f32[192,256]{1,0:T(8,128)S(1)} %collective-permute-done.inc1, ...), custom_call_target="tpu_custom_call" | custom-call | tf_op jit(solution)/shard_map/sort/pallas_call | solution.py:301
  32.9 11.3 %scatter.1 = (f32[16,40,256]{2,1,0:T(8,128)S(1)}, f32[16,40,256]{2,1,0:T(8,128)S(1)}) custom-call(s32[65]{0:T(128)S(1)} %get-tuple-element.30.bounds, s32[1]{0:T(128)} %bitcast.2.core, s32[32,8,128]{2,1,0:T(8,128)S(1)} %get-tuple-element.31.star, s32[4,128,128]{2,1,0:T(8,128)S(1)} %get-tuple-element.34.skt, s32[128,256]{1,0:T(8,128)S(1)} %get-tuple-element.35.rank, ...), custom_call_target="tpu_custom_call" | custom-call | tf_op jit(solution)/shard_map/scatter/pallas_call | solution.py:401
  44.3 2.1 %collective-permute-done.6 = f32[16,40,256]{2,1,0:T(8,128)S(1)} collective-permute-done((f32[16,40,256]{2,1,0:T(8,128)S(1)}, f32[16,40,256]{2,1,0:T(8,128)S(1)}, u32[]{:S(2)}, u32[]{:S(2)}) %collective-permute-start.6) | collective-permute-done | bytes 655392 | tf_op jit(solution)/shard_map/ppermute | solution.py:571
  46.5 20.1 %all_to_all.15.parts = f32[16,40,256]{2,1,0:T(8,128)S(1)} all-to-all(f32[16,40,256]{2,1,0:T(8,128)S(1)} %add.8), channel_id=1, replica_groups={{0,2,4,6,8,10,12,14,16,18,20,22,24,26,28,30},{1,3,5,7,9,11,13,15,17,19,..., dimensions={0} | all-to-all | bytes 1310720 | tf_op jit(solution)/shard_map/all_to_all | solution.py:572
  66.6 0.8 solve.1
  67.3 11.4 %all_to_all.16.near = f32[16,24,128]{2,1,0:T(8,128)S(1)} all-to-all(f32[16,24,128]{2,1,0:T(8,128)S(1)} %get-tuple-element.42), channel_id=1, replica_groups={{0,2,4,6,8,10,12,14,16,18,20,22,24,26,28,30},{1,3,5,7,9,11,13,15,17,19,..., dimensions={0} | all-to-all | bytes 393216 | tf_op jit(solution)/shard_map/all_to_all | solution.py:574
  78.7 0.8 invert.1.inv
  80.2 5.6 %fit.1 = (f32[32,256]{1,0:T(8,128)S(1)}, f32[32,256]{1,0:T(8,128)S(1)}, f32[32,256]{1,0:T(8,128)S(1)}, f32[32,256]{1,0:T(8,128)S(1)}) custom-call(s32[65]{0:T(128)S(1)} %get-tuple-element.30.bounds, s32[1]{0:T(128)} %bitcast.2.core, s32[32,8,128]{2,1,0:T(8,128)S(1)} %get-tuple-element.31.star, s32[128,256]{1,0:T(8,128)S(1)} %invert.1.inv, ...), custom_call_target="tpu_custom_call" | custom-call | tf_op jit(solution)/shard_map/fit/pallas_call | solution.py:526
  85.8 1.4 %collective-permute-start.8 = (f32[32,256]{1,0:T(8,128)S(1)}, f32[32,256]{1,0:T(8,128)S(1)}, u32[]{:S(2)}, u32[]{:S(2)}) collective-permute-start(f32[32,256]{1,0:T(8,128)S(1)} %get-tuple-element.44), channel_id=1, source_target_pairs={{0,96},{32,0},{64,32},{96,64},{1,97},{33,1},{65,33},{97,65},{2,98}... | collective-permute-start | bytes 98312 | tf_op jit(solution)/shard_map/ppermute | solution.py:540
  87.2 3.3 %collective-permute-start.9 = (f32[32,256]{1,0:T(8,128)S(1)}, f32[32,256]{1,0:T(8,128)S(1)}, u32[]{:S(2)}, u32[]{:S(2)}) collective-permute-start(f32[32,256]{1,0:T(8,128)S(1)} %get-tuple-element.45), channel_id=1, source_target_pairs={{0,64},{32,96},{64,0},{96,32},{1,65},{33,97},{65,1},{97,33},{2,66}... | collective-permute-start | bytes 98312 | tf_op jit(solution)/shard_map/ppermute | solution.py:540
  90.5 1.3 %collective-permute-start.10 = (f32[32,256]{1,0:T(8,128)S(1)}, f32[32,256]{1,0:T(8,128)S(1)}, u32[]{:S(2)}, u32[]{:S(2)}) collective-permute-start(f32[32,256]{1,0:T(8,128)S(1)} %get-tuple-element.46), channel_id=1, source_target_pairs={{0,32},{32,64},{64,96},{96,0},{1,33},{33,65},{65,97},{97,1},{2,34}... | collective-permute-start | bytes 98312 | tf_op jit(solution)/shard_map/ppermute | solution.py:540
  91.8 1.1 %collective-permute-done.9.rows2 = f32[32,256]{1,0:T(8,128)S(1)} collective-permute-done((f32[32,256]{1,0:T(8,128)S(1)}, f32[32,256]{1,0:T(8,128)S(1)}, u32[]{:S(2)}, u32[]{:S(2)}) %collective-permute-start.9) | collective-permute-done | bytes 32800 | tf_op jit(solution)/shard_map/ppermute | solution.py:540
  92.9 2.7 %collective-permute-done.10.rows3 = f32[32,256]{1,0:T(8,128)S(1)} collective-permute-done((f32[32,256]{1,0:T(8,128)S(1)}, f32[32,256]{1,0:T(8,128)S(1)}, u32[]{:S(2)}, u32[]{:S(2)}) %collective-permute-start.10) | collective-permute-done | bytes 32800 | tf_op jit(solution)/shard_map/ppermute | solution.py:540
  95.6 1.5 %collect.1 = f32[64,256]{1,0:T(8,128)} custom-call(s32[64]{0:T(128)S(1)} %get-tuple-element.25.slots, s32[1]{0:T(128)S(6)} %copy.10.count, f32[32,256]{1,0:T(8,128)S(1)} %get-tuple-element.43.rows0, f32[32,256]{1,0:T(8,128)S(1)} %collective-permute-done.8.rows1, f32[32,256]{1,0:T(8,128)S(1)} %collective-permute-done.9.rows2, ...), custom_call_target="tpu_custom_call" | custom-call | tf_op jit(solution)/shard_map/collect/pallas_call | solution.py:83
  (13 shorter events, 1.5 us)
Async XLA Ops:
  2.0 18.1 %all-to-all-start = ((f32[32,8,128]{2,1,0:T(8,128)}), f32[32,8,128]{2,1,0:T(8,128)S(1)}, u32[]{:S(2)}, u32[]{:S(2)}) async-start(f32[32,8,128]{2,1,0:T(8,128)} %pieces.1), calls=%async_computation | async-start | bytes 262144 | tf_op jit(solution)/shard_map/all_to_all | solution.py:564
  13.7 13.8 %collective-permute-start = (f32[192,256]{1,0:T(8,128)S(1)}, f32[192,256]{1,0:T(8,128)S(1)}, u32[]{:S(2)}, u32[]{:S(2)}) collective-permute-start(f32[192,256]{1,0:T(8,128)S(1)} %get-tuple-element.27), channel_id=1, source_target_pairs={{0,32},{32,64},{64,96},{96,0},{1,33},{33,65},{65,97},{97,1},{2,34}... | collective-permute-start | bytes 589832 | tf_op jit(solution)/shard_map/ppermute | solution.py:540
  15.4 13.5 %collective-permute-start.1 = (f32[192,256]{1,0:T(8,128)S(1)}, f32[192,256]{1,0:T(8,128)S(1)}, u32[]{:S(2)}, u32[]{:S(2)}) collective-permute-start(f32[192,256]{1,0:T(8,128)S(1)} %get-tuple-element.28), channel_id=1, source_target_pairs={{0,64},{32,96},{64,0},{96,32},{1,65},{33,97},{65,1},{97,33},{2,66}... | collective-permute-start | bytes 589832 | tf_op jit(solution)/shard_map/ppermute | solution.py:540
  18.2 10.6 %collective-permute-start.2 = (f32[192,256]{1,0:T(8,128)S(1)}, f32[192,256]{1,0:T(8,128)S(1)}, u32[]{:S(2)}, u32[]{:S(2)}) collective-permute-start(f32[192,256]{1,0:T(8,128)S(1)} %get-tuple-element.29), channel_id=1, source_target_pairs={{0,96},{32,0},{64,32},{96,64},{1,97},{33,1},{65,33},{97,65},{2,98}... | collective-permute-start | bytes 589832 | tf_op jit(solution)/shard_map/ppermute | solution.py:540
  25.1 7.8 %collective-permute-start.3 = (f32[32,256]{1,0:T(8,128)S(1)}, f32[32,256]{1,0:T(8,128)S(1)}, u32[]{:S(2)}, u32[]{:S(2)}) collective-permute-start(f32[32,256]{1,0:T(8,128)S(1)} %get-tuple-element.37), channel_id=1, source_target_pairs={{0,32},{32,64},{64,96},{96,0},{1,33},{33,65},{65,97},{97,1},{2,34}... | collective-permute-start | bytes 98312 | tf_op jit(solution)/shard_map/ppermute | solution.py:540
  26.0 6.9 %collective-permute-start.4 = (f32[32,256]{1,0:T(8,128)S(1)}, f32[32,256]{1,0:T(8,128)S(1)}, u32[]{:S(2)}, u32[]{:S(2)}) collective-permute-start(f32[32,256]{1,0:T(8,128)S(1)} %get-tuple-element.38), channel_id=1, source_target_pairs={{0,64},{32,96},{64,0},{96,32},{1,65},{33,97},{65,1},{97,33},{2,66}... | collective-permute-start | bytes 98312 | tf_op jit(solution)/shard_map/ppermute | solution.py:540
  27.6 5.3 %collective-permute-start.5 = (f32[32,256]{1,0:T(8,128)S(1)}, f32[32,256]{1,0:T(8,128)S(1)}, u32[]{:S(2)}, u32[]{:S(2)}) collective-permute-start(f32[32,256]{1,0:T(8,128)S(1)} %get-tuple-element.39), channel_id=1, source_target_pairs={{0,96},{32,0},{64,32},{96,64},{1,97},{33,1},{65,33},{97,65},{2,98}... | collective-permute-start | bytes 98312 | tf_op jit(solution)/shard_map/ppermute | solution.py:540
  44.3 2.2 %collective-permute-start.6 = (f32[16,40,256]{2,1,0:T(8,128)S(1)}, f32[16,40,256]{2,1,0:T(8,128)S(1)}, u32[]{:S(2)}, u32[]{:S(2)}) collective-permute-start(f32[16,40,256]{2,1,0:T(8,128)S(1)} %get-tuple-element.41), channel_id=1, source_target_pairs={{0,1},{1,0},{2,3},{3,2},{4,5},{5,4},{6,7},{7,6},{8,9},{9,8},{10,11... | collective-permute-start | bytes 1966088 | tf_op jit(solution)/shard_map/ppermute | solution.py:571
  78.7 1.4 %collective-permute-start.7 = (f32[16,24,128]{2,1,0:T(8,128)S(1)}, f32[16,24,128]{2,1,0:T(8,128)S(1)}, u32[]{:S(2)}, u32[]{:S(2)}) collective-permute-start(f32[16,24,128]{2,1,0:T(8,128)S(1)} %all_to_all.16.near), channel_id=1, source_target_pairs={{0,1},{1,0},{2,3},{3,2},{4,5},{5,4},{6,7},{7,6},{8,9},{9,8},{10,11... | collective-permute-start | bytes 589832 | tf_op jit(solution)/shard_map/ppermute | solution.py:576
  85.8 6.0 %collective-permute-start.8 = (f32[32,256]{1,0:T(8,128)S(1)}, f32[32,256]{1,0:T(8,128)S(1)}, u32[]{:S(2)}, u32[]{:S(2)}) collective-permute-start(f32[32,256]{1,0:T(8,128)S(1)} %get-tuple-element.44), channel_id=1, source_target_pairs={{0,96},{32,0},{64,32},{96,64},{1,97},{33,1},{65,33},{97,65},{2,98}... | collective-permute-start | bytes 98312 | tf_op jit(solution)/shard_map/ppermute | solution.py:540
  87.2 5.7 %collective-permute-start.9 = (f32[32,256]{1,0:T(8,128)S(1)}, f32[32,256]{1,0:T(8,128)S(1)}, u32[]{:S(2)}, u32[]{:S(2)}) collective-permute-start(f32[32,256]{1,0:T(8,128)S(1)} %get-tuple-element.45), channel_id=1, source_target_pairs={{0,64},{32,96},{64,0},{96,32},{1,65},{33,97},{65,1},{97,33},{2,66}... | collective-permute-start | bytes 98312 | tf_op jit(solution)/shard_map/ppermute | solution.py:540
  90.5 5.1 %collective-permute-start.10 = (f32[32,256]{1,0:T(8,128)S(1)}, f32[32,256]{1,0:T(8,128)S(1)}, u32[]{:S(2)}, u32[]{:S(2)}) collective-permute-start(f32[32,256]{1,0:T(8,128)S(1)} %get-tuple-element.46), channel_id=1, source_target_pairs={{0,32},{32,64},{64,96},{96,0},{1,33},{33,65},{65,97},{97,1},{2,34}... | collective-permute-start | bytes 98312 | tf_op jit(solution)/shard_map/ppermute | solution.py:540

commit v6 on v5

--- a/solution.py
+++ b/solution.py
@@ -12,7 +12,7 @@
 NBLK = 64
 SLOTS = 128
 STAR_DEV = 512
-PAIR = 8
+PAIR = 16
 HW = 12
 NHI = 64
 F32 = jnp.float32
@@ -29,27 +29,24 @@
 
 def pack_kernel(sky, dest, count, partials, stars, out0, out1, out2, out3, slots, out, used):
     out[...] = jnp.zeros_like(out)
-    out[:, 160:192, :] = lax.broadcasted_iota(I32, (4, 32, ROWS), 2).astype(F32) * (NHI * 256 // ROWS)
+    out[:, 160:192, :] = lax.broadcasted_iota(I32, (5, 32, ROWS), 2).astype(F32) * (NHI * 256 // ROWS)
     for g in range(4):
         used[g] = 0
 
     def place(b, carry):
+        live = b < count[0]
         g = (dest[b] - sky[0]) & 3
         k = used[g]
-        used[g] = k + 1
-        slots[b] = g * CAP + k
+        used[g] = k + live.astype(I32)
+        slots[b] = jnp.where(live, g * CAP + k, -1)
+        g = jnp.where(live, g, 4)
+        k = jnp.where(live, k, 0)
         for q in range(5):
             out[g, pl.ds(q * CAP + k, 1), :] = partials[q, pl.ds(b, 1), :]
         out[g, pl.ds(5 * CAP + k, 1), :] = stars[pl.ds(b, 1), :].astype(F32)
         return carry
 
-    lax.fori_loop(0, count[0], place, 0)
-
-    def skip(b, carry):
-        slots[b] = -1
-        return carry
-
-    lax.fori_loop(count[0], NBLK, skip, 0)
+    lax.fori_loop(0, NBLK, place, 0, unroll=4)
     for d, ref in enumerate((out0, out1, out2, out3)):
         ref[...] = out[d]
 
@@ -62,7 +59,7 @@
         out_shape=(shape((192, ROWS)),) * 4 + (shape((NBLK,), I32),),
         in_specs=[SM, SM, SM, VM, VM],
         out_specs=(VM,) * 4 + (SM,),
-        scratch_shapes=[pltpu.VMEM((4, 192, ROWS), F32), pltpu.SMEM((4,), I32)],
+        scratch_shapes=[pltpu.VMEM((5, 192, ROWS), F32), pltpu.SMEM((4,), I32)],
     )(sky, dest, count, partials, stars)
     return slabs, slots
 
@@ -107,14 +104,14 @@
 
 
 def residual_kernel(
-    start, tiles, slots, count, knots, obs, design, out0, out1, out2, out3, near, far, shift, win, res, out
+    start, slots, count, knots, obs, design, out0, out1, out2, out3, near, far, shift, win, res, out
 ):
     step = pl.program_id(0)
 
     @pl.when(step == 0)
     def _():
         def place(b, carry):
-            tile = tiles[b]
+            tile = start[b] >> 7
             after = jnp.minimum(tile + 1, 63)
             shift[pl.ds(b, 1), :] = jnp.full((1, 128), start[b] & 127, I32)
             for axis in range(3):
@@ -152,7 +149,7 @@
             ref[...] = out[d * CAP:(d + 1) * CAP]
 
 
-def residuals(start, tiles, slots, count, knots, obs, design):
+def residuals(start, slots, count, knots, obs, design):
     return pl.pallas_call(
         residual_kernel,
         name="residuals",
@@ -160,7 +157,6 @@
         grid=(NBLK // STEP,),
         out_shape=(shape((CAP, ROWS)),) * 4,
         in_specs=[
-            SM,
             SM,
             SM,
             SM,
@@ -177,7 +173,7 @@
             pltpu.VMEM((NBLK, ROWS), F32),
             pltpu.VMEM((SLOTS, ROWS), F32),
         ],
-    )(start, tiles, slots, count, knots, obs, design)
+    )(start, slots, count, knots, obs, design)
 
 
 def sort_rows(key):
@@ -547,13 +543,14 @@
 
 
 def steps(attitude, win_start, design, obs_value, star_design, star_local, block_dest, block_count):
-    attitude, starts, obs_value, star_local, block_dest = map(
+    attitude, win_start, obs_value, star_local, block_dest = map(
         in_hbm, (attitude, win_start, obs_value, star_local, block_dest)
     )
     partials = in_hbm(star_design.transpose(1, 0, 2))
     design_t = in_hbm(design.transpose(0, 2, 1))
     tm = lax.axis_size("tm")
-    core = (lax.axis_index("tm") % 2).astype(I32)
+    place = lax.axis_index("tm").astype(I32)
+    core = place & 1
     swap = [(i, i ^ 1) for i in range(tm)]
     chips = [list(range(0, tm, 2)), list(range(1, tm, 2))]
 
@@ -562,8 +559,7 @@
     incoming = to_sky(outgoing, 1)
 
     knots = lax.all_to_all(pieces(attitude, tm), "tm", 0, 0, tiled=True)
-    tiles = win_start >> 7
-    out_res = residuals(starts, tiles, slots, block_count, knots, obs_value, design_t)
+    out_res = residuals(win_start, slots, block_count, knots, obs_value, design_t)
     in_res = to_sky(out_res, 1)
 
     star, skt, rank, came, ps, bounds = sort_slots(incoming)

time: 97.4 us -> 100 us (1.027)
  blocking collectives: 31.5 us -> 43.6 us
  starting transfers between devices: 23.8 us -> 16.6 us
  Pallas kernels: 33.1 us -> 32 us
    all_to_all x0 -> x1, blocking collectives: none -> 15.7 us  [steps(): knots = lax.all_to_all(pieces(attitude, tm), 'tm', 0, 0, tiled=True)]
    all_to_all x1 -> x0, starting transfers between devices: 8.27 us -> none  [steps(): knots = lax.all_to_all(pieces(attitude, tm), 'tm', 0, 0, tiled=True)]
    all_to_all x1, blocking collectives: 20.1 us -> 16.5 us  [steps(): lax.all_to_all(pair_sum, 'tm', 0, 0, tiled=True, axis_index_groups=chips)]
    ppermute x9, starting transfers between devices: 15.5 us -> 16.6 us  [to_sky(): lax.ppermute(slabs[d], 'sky', [(i, (i + sign * d) % n) for i in range(n)])]
  transfers between devices with their start and end apart: 12 -> 11, of which waited for: 4 -> 4; matrix products, arithmetic and copies ran while one was open for 1% -> 0% of each run, Pallas kernels for 13% -> 11%
where the time goes in v6:
time: 100 us
  blocking collectives  43.6 us (44%)
  Pallas kernels  32 us (32%)
  starting transfers between devices  16.6 us (17%)
  waiting for transfers between devices  6.51 us (7%)
  between operations  1.37 us (1%)
    ppermute x9, starting transfers between devices, to_sky(): lax.ppermute(slabs[d], 'sky', [(i, (i + sign * d) % n) for i in range(n)])  16.6 us
    all_to_all x1, blocking collectives, steps(): lax.all_to_all(pair_sum, 'tm', 0, 0, tiled=True, axis_index_groups=chips)  16.5 us
    all_to_all x1, blocking collectives, steps(): knots = lax.all_to_all(pieces(attitude, tm), 'tm', 0, 0, tiled=True)  15.7 us
    all_to_all x1, blocking collectives, steps(): lax.all_to_all(packed, 'tm', 0, 0, tiled=True, axis_index_groups=chips)  11.4 us
    pallas_call x1, Pallas kernels, scatter(): pl.pallas_call(scatter_kernel, name='scatter', compiler_params=ROOM, out_...  10.7 us
    pallas_call x1, Pallas kernels, apply_fit(): pl.pallas_call(fit_kernel, name='fit', compiler_params=ROOM, out_shape=(s...  5.46 us
    pallas_call x1, Pallas kernels, residuals(): pl.pallas_call(residual_kernel, name='residuals', compiler_params=ROOM, g...  5.01 us
    pallas_call x1, Pallas kernels, sort_slots(): pl.pallas_call(sort_kernel, name='sort', compiler_params=ROOM, out_shape=...  4.01 us
  transfers between devices with their start and end apart: 11, of which 4 were waited for; matrix products, arithmetic and copies ran while one was open for 0% of the time, Pallas kernels for 11%

profile of v6, /device:TPU:0, one launch (start us, length us, event | category | flops | bytes accessed | tf_op | source)
XLA Modules:
  0.0 100.2 jit_solution(17248893813132103325)
XLA Ops:
  1.3 3.0 %pack.1 = (f32[192,256]{1,0:T(8,128)S(1)}, f32[192,256]{1,0:T(8,128)S(1)}, f32[192,256]{1,0:T(8,128)S(1)}, f32[192,256]{1,0:T(8,128)S(1)}, s32[64]{0:T(128)S(1)}) custom-call(s32[1]{0:T(128)} %bitcast.sky, s32[64]{0:T(128)} %dest.1, s32[1]{0:T(128)S(6)} %copy.10.count, f32[5,64,256]{2,1,0:T(8,128)} %bitcast.5, s32[64,256]{1,0:T(8,128)} %stars.1), custom_call_target="tpu_custom_call" | custom-call | tf_op jit(solution)/shard_map/pack/pallas_call | solution.py:55
  4.3 1.8 %collective-permute-start = (f32[192,256]{1,0:T(8,128)S(1)}, f32[192,256]{1,0:T(8,128)S(1)}, u32[]{:S(2)}, u32[]{:S(2)}) collective-permute-start(f32[192,256]{1,0:T(8,128)S(1)} %get-tuple-element.27), channel_id=1, source_target_pairs={{0,32},{32,64},{64,96},{96,0},{1,33},{33,65},{65,97},{97,1},{2,34}... | collective-permute-start | bytes 589832 | tf_op jit(solution)/shard_map/ppermute | solution.py:536
  6.1 2.9 %collective-permute-start.1 = (f32[192,256]{1,0:T(8,128)S(1)}, f32[192,256]{1,0:T(8,128)S(1)}, u32[]{:S(2)}, u32[]{:S(2)}) collective-permute-start(f32[192,256]{1,0:T(8,128)S(1)} %get-tuple-element.28), channel_id=1, source_target_pairs={{0,64},{32,96},{64,0},{96,32},{1,65},{33,97},{65,1},{97,33},{2,66}... | collective-permute-start | bytes 589832 | tf_op jit(solution)/shard_map/ppermute | solution.py:536
  9.0 1.3 %collective-permute-start.2 = (f32[192,256]{1,0:T(8,128)S(1)}, f32[192,256]{1,0:T(8,128)S(1)}, u32[]{:S(2)}, u32[]{:S(2)}) collective-permute-start(f32[192,256]{1,0:T(8,128)S(1)} %get-tuple-element.29), channel_id=1, source_target_pairs={{0,96},{32,0},{64,32},{96,64},{1,97},{33,1},{65,33},{97,65},{2,98}... | collective-permute-start | bytes 589832 | tf_op jit(solution)/shard_map/ppermute | solution.py:536
  10.3 0.7 pieces.1
  11.0 15.7 %all_to_all.15.knots = f32[32,8,128]{2,1,0:T(8,128)S(1)} all-to-all(f32[32,8,128]{2,1,0:T(8,128)S(1)} %pieces.1), channel_id=1, replica_groups=mesh['sky'=4,'tm'=32] {'tm'}, dimensions={0} | all-to-all | bytes 262144 | tf_op jit(solution)/shard_map/all_to_all | solution.py:561
  26.8 5.0 %residuals.1 = (f32[32,256]{1,0:T(8,128)S(1)}, f32[32,256]{1,0:T(8,128)S(1)}, f32[32,256]{1,0:T(8,128)S(1)}, f32[32,256]{1,0:T(8,128)S(1)}) custom-call(s32[64]{0:T(128)} %start.1, s32[64]{0:T(128)S(1)} %get-tuple-element.25.slots, s32[1]{0:T(128)S(6)} %copy.10.count, f32[32,8,128]{2,1,0:T(8,128)S(1)} %all_to_all.15.knots, f32[64,256]{1,0:T(8,128)} %obs.1, ...), custom_call_target="tpu_custom_call" | custom-call | tf_op jit(solution)/shard_map/residuals/pallas_call | solution.py:153
  31.8 0.7 collective-permute-start.3
  32.5 0.8 collective-permute-start.4
  33.3 2.0 %collective-permute-start.5 = (f32[32,256]{1,0:T(8,128)S(1)}, f32[32,256]{1,0:T(8,128)S(1)}, u32[]{:S(2)}, u32[]{:S(2)}) collective-permute-start(f32[32,256]{1,0:T(8,128)S(1)} %get-tuple-element.39), channel_id=1, source_target_pairs={{0,96},{32,0},{64,32},{96,64},{1,97},{33,1},{65,33},{97,65},{2,98}... | collective-permute-start | bytes 98312 | tf_op jit(solution)/shard_map/ppermute | solution.py:536
  35.3 4.0 %sort.1 = (s32[32,8,128]{2,1,0:T(8,128)S(1)}, s32[4,128,128]{2,1,0:T(8,128)S(1)}, s32[128,256]{1,0:T(8,128)S(1)}, s32[256,128]{1,0:T(8,128)S(1)}, f32[160,8,128]{2,1,0:T(8,128)S(1)}, /*index=5*/s32[65]{0:T(128)S(1)}) custom-call(f32[192,256]{1,0:T(8,128)S(1)} %get-tuple-element.26.inc0, f32[192,256]{1,0:T(8,128)S(1)} %collective-permute-done.inc1, ...), custom_call_target="tpu_custom_call" | custom-call | tf_op jit(solution)/shard_map/sort/pallas_call | solution.py:297
  39.3 10.7 %scatter.1 = (f32[16,40,256]{2,1,0:T(8,128)S(1)}, f32[16,40,256]{2,1,0:T(8,128)S(1)}) custom-call(s32[65]{0:T(128)S(1)} %get-tuple-element.30.bounds, s32[1]{0:T(128)} %bitcast.2.core, s32[32,8,128]{2,1,0:T(8,128)S(1)} %get-tuple-element.31.star, s32[4,128,128]{2,1,0:T(8,128)S(1)} %get-tuple-element.34.skt, s32[128,256]{1,0:T(8,128)S(1)} %get-tuple-element.35.rank, ...), custom_call_target="tpu_custom_call" | custom-call | tf_op jit(solution)/shard_map/scatter/pallas_call | solution.py:397
  50.1 2.1 %collective-permute-done.6 = f32[16,40,256]{2,1,0:T(8,128)S(1)} collective-permute-done((f32[16,40,256]{2,1,0:T(8,128)S(1)}, f32[16,40,256]{2,1,0:T(8,128)S(1)}, u32[]{:S(2)}, u32[]{:S(2)}) %collective-permute-start.6) | collective-permute-done | bytes 655392 | tf_op jit(solution)/shard_map/ppermute | solution.py:567
  52.3 16.5 %all_to_all.16.parts = f32[16,40,256]{2,1,0:T(8,128)S(1)} all-to-all(f32[16,40,256]{2,1,0:T(8,128)S(1)} %add.3), channel_id=1, replica_groups={{0,2,4,6,8,10,12,14,16,18,20,22,24,26,28,30},{1,3,5,7,9,11,13,15,17,19,..., dimensions={0} | all-to-all | bytes 1310720 | tf_op jit(solution)/shard_map/all_to_all | solution.py:568
  68.8 0.8 solve.1
  69.6 11.4 %all_to_all.17.near = f32[16,24,128]{2,1,0:T(8,128)S(1)} all-to-all(f32[16,24,128]{2,1,0:T(8,128)S(1)} %get-tuple-element.42), channel_id=1, replica_groups={{0,2,4,6,8,10,12,14,16,18,20,22,24,26,28,30},{1,3,5,7,9,11,13,15,17,19,..., dimensions={0} | all-to-all | bytes 393216 | tf_op jit(solution)/shard_map/all_to_all | solution.py:570
  81.0 0.8 invert.1.inv
  81.8 0.6 collective-permute-done.7.far
  82.4 5.5 %fit.1 = (f32[32,256]{1,0:T(8,128)S(1)}, f32[32,256]{1,0:T(8,128)S(1)}, f32[32,256]{1,0:T(8,128)S(1)}, f32[32,256]{1,0:T(8,128)S(1)}) custom-call(s32[65]{0:T(128)S(1)} %get-tuple-element.30.bounds, s32[1]{0:T(128)} %bitcast.2.core, s32[32,8,128]{2,1,0:T(8,128)S(1)} %get-tuple-element.31.star, s32[128,256]{1,0:T(8,128)S(1)} %invert.1.inv, ...), custom_call_target="tpu_custom_call" | custom-call | tf_op jit(solution)/shard_map/fit/pallas_call | solution.py:522
  87.9 1.5 %collective-permute-start.8 = (f32[32,256]{1,0:T(8,128)S(1)}, f32[32,256]{1,0:T(8,128)S(1)}, u32[]{:S(2)}, u32[]{:S(2)}) collective-permute-start(f32[32,256]{1,0:T(8,128)S(1)} %get-tuple-element.44), channel_id=1, source_target_pairs={{0,96},{32,0},{64,32},{96,64},{1,97},{33,1},{65,33},{97,65},{2,98}... | collective-permute-start | bytes 98312 | tf_op jit(solution)/shard_map/ppermute | solution.py:536
  89.4 4.2 %collective-permute-start.9 = (f32[32,256]{1,0:T(8,128)S(1)}, f32[32,256]{1,0:T(8,128)S(1)}, u32[]{:S(2)}, u32[]{:S(2)}) collective-permute-start(f32[32,256]{1,0:T(8,128)S(1)} %get-tuple-element.45), channel_id=1, source_target_pairs={{0,64},{32,96},{64,0},{96,32},{1,65},{33,97},{65,1},{97,33},{2,66}... | collective-permute-start | bytes 98312 | tf_op jit(solution)/shard_map/ppermute | solution.py:536
  93.6 1.3 %collective-permute-start.10 = (f32[32,256]{1,0:T(8,128)S(1)}, f32[32,256]{1,0:T(8,128)S(1)}, u32[]{:S(2)}, u32[]{:S(2)}) collective-permute-start(f32[32,256]{1,0:T(8,128)S(1)} %get-tuple-element.46), channel_id=1, source_target_pairs={{0,32},{32,64},{64,96},{96,0},{1,33},{33,65},{65,97},{97,1},{2,34}... | collective-permute-start | bytes 98312 | tf_op jit(solution)/shard_map/ppermute | solution.py:536
  95.5 3.2 %collective-permute-done.10.rows3 = f32[32,256]{1,0:T(8,128)S(1)} collective-permute-done((f32[32,256]{1,0:T(8,128)S(1)}, f32[32,256]{1,0:T(8,128)S(1)}, u32[]{:S(2)}, u32[]{:S(2)}) %collective-permute-start.10) | collective-permute-done | bytes 32800 | tf_op jit(solution)/shard_map/ppermute | solution.py:536
  98.7 1.5 %collect.1 = f32[64,256]{1,0:T(8,128)} custom-call(s32[64]{0:T(128)S(1)} %get-tuple-element.25.slots, s32[1]{0:T(128)S(6)} %copy.10.count, f32[32,256]{1,0:T(8,128)S(1)} %get-tuple-element.43.rows0, f32[32,256]{1,0:T(8,128)S(1)} %collective-permute-done.8.rows1, f32[32,256]{1,0:T(8,128)S(1)} %collective-permute-done.9.rows2, ...), custom_call_target="tpu_custom_call" | custom-call | tf_op jit(solution)/shard_map/collect/pallas_call | solution.py:80
  (11 shorter events, 0.8 us)
Async XLA Ops:
  4.3 29.0 %collective-permute-start = (f32[192,256]{1,0:T(8,128)S(1)}, f32[192,256]{1,0:T(8,128)S(1)}, u32[]{:S(2)}, u32[]{:S(2)}) collective-permute-start(f32[192,256]{1,0:T(8,128)S(1)} %get-tuple-element.27), channel_id=1, source_target_pairs={{0,32},{32,64},{64,96},{96,0},{1,33},{33,65},{65,97},{97,1},{2,34}... | collective-permute-start | bytes 589832 | tf_op jit(solution)/shard_map/ppermute | solution.py:536
  6.1 29.2 %collective-permute-start.1 = (f32[192,256]{1,0:T(8,128)S(1)}, f32[192,256]{1,0:T(8,128)S(1)}, u32[]{:S(2)}, u32[]{:S(2)}) collective-permute-start(f32[192,256]{1,0:T(8,128)S(1)} %get-tuple-element.28), channel_id=1, source_target_pairs={{0,64},{32,96},{64,0},{96,32},{1,65},{33,97},{65,1},{97,33},{2,66}... | collective-permute-start | bytes 589832 | tf_op jit(solution)/shard_map/ppermute | solution.py:536
  9.0 26.3 %collective-permute-start.2 = (f32[192,256]{1,0:T(8,128)S(1)}, f32[192,256]{1,0:T(8,128)S(1)}, u32[]{:S(2)}, u32[]{:S(2)}) collective-permute-start(f32[192,256]{1,0:T(8,128)S(1)} %get-tuple-element.29), channel_id=1, source_target_pairs={{0,96},{32,0},{64,32},{96,64},{1,97},{33,1},{65,33},{97,65},{2,98}... | collective-permute-start | bytes 589832 | tf_op jit(solution)/shard_map/ppermute | solution.py:536
  31.8 7.5 %collective-permute-start.3 = (f32[32,256]{1,0:T(8,128)S(1)}, f32[32,256]{1,0:T(8,128)S(1)}, u32[]{:S(2)}, u32[]{:S(2)}) collective-permute-start(f32[32,256]{1,0:T(8,128)S(1)} %get-tuple-element.37), channel_id=1, source_target_pairs={{0,32},{32,64},{64,96},{96,0},{1,33},{33,65},{65,97},{97,1},{2,34}... | collective-permute-start | bytes 98312 | tf_op jit(solution)/shard_map/ppermute | solution.py:536
  32.5 6.8 %collective-permute-start.4 = (f32[32,256]{1,0:T(8,128)S(1)}, f32[32,256]{1,0:T(8,128)S(1)}, u32[]{:S(2)}, u32[]{:S(2)}) collective-permute-start(f32[32,256]{1,0:T(8,128)S(1)} %get-tuple-element.38), channel_id=1, source_target_pairs={{0,64},{32,96},{64,0},{96,32},{1,65},{33,97},{65,1},{97,33},{2,66}... | collective-permute-start | bytes 98312 | tf_op jit(solution)/shard_map/ppermute | solution.py:536
  33.3 6.0 %collective-permute-start.5 = (f32[32,256]{1,0:T(8,128)S(1)}, f32[32,256]{1,0:T(8,128)S(1)}, u32[]{:S(2)}, u32[]{:S(2)}) collective-permute-start(f32[32,256]{1,0:T(8,128)S(1)} %get-tuple-element.39), channel_id=1, source_target_pairs={{0,96},{32,0},{64,32},{96,64},{1,97},{33,1},{65,33},{97,65},{2,98}... | collective-permute-start | bytes 98312 | tf_op jit(solution)/shard_map/ppermute | solution.py:536
  50.0 2.2 %collective-permute-start.6 = (f32[16,40,256]{2,1,0:T(8,128)S(1)}, f32[16,40,256]{2,1,0:T(8,128)S(1)}, u32[]{:S(2)}, u32[]{:S(2)}) collective-permute-start(f32[16,40,256]{2,1,0:T(8,128)S(1)} %get-tuple-element.41), channel_id=1, source_target_pairs={{0,1},{1,0},{2,3},{3,2},{4,5},{5,4},{6,7},{7,6},{8,9},{9,8},{10,11... | collective-permute-start | bytes 1966088 | tf_op jit(solution)/shard_map/ppermute | solution.py:567
  81.0 1.4 %collective-permute-start.7 = (f32[16,24,128]{2,1,0:T(8,128)S(1)}, f32[16,24,128]{2,1,0:T(8,128)S(1)}, u32[]{:S(2)}, u32[]{:S(2)}) collective-permute-start(f32[16,24,128]{2,1,0:T(8,128)S(1)} %all_to_all.17.near), channel_id=1, source_target_pairs={{0,1},{1,0},{2,3},{3,2},{4,5},{5,4},{6,7},{7,6},{8,9},{9,8},{10,11... | collective-permute-start | bytes 589832 | tf_op jit(solution)/shard_map/ppermute | solution.py:572
  87.9 7.0 %collective-permute-start.8 = (f32[32,256]{1,0:T(8,128)S(1)}, f32[32,256]{1,0:T(8,128)S(1)}, u32[]{:S(2)}, u32[]{:S(2)}) collective-permute-start(f32[32,256]{1,0:T(8,128)S(1)} %get-tuple-element.44), channel_id=1, source_target_pairs={{0,96},{32,0},{64,32},{96,64},{1,97},{33,1},{65,33},{97,65},{2,98}... | collective-permute-start | bytes 98312 | tf_op jit(solution)/shard_map/ppermute | solution.py:536
  89.4 6.1 %collective-permute-start.9 = (f32[32,256]{1,0:T(8,128)S(1)}, f32[32,256]{1,0:T(8,128)S(1)}, u32[]{:S(2)}, u32[]{:S(2)}) collective-permute-start(f32[32,256]{1,0:T(8,128)S(1)} %get-tuple-element.45), channel_id=1, source_target_pairs={{0,64},{32,96},{64,0},{96,32},{1,65},{33,97},{65,1},{97,33},{2,66}... | collective-permute-start | bytes 98312 | tf_op jit(solution)/shard_map/ppermute | solution.py:536
  93.6 5.1 %collective-permute-start.10 = (f32[32,256]{1,0:T(8,128)S(1)}, f32[32,256]{1,0:T(8,128)S(1)}, u32[]{:S(2)}, u32[]{:S(2)}) collective-permute-start(f32[32,256]{1,0:T(8,128)S(1)} %get-tuple-element.46), channel_id=1, source_target_pairs={{0,32},{32,64},{64,96},{96,0},{1,33},{33,65},{65,97},{97,1},{2,34}... | collective-permute-start | bytes 98312 | tf_op jit(solution)/shard_map/ppermute | solution.py:536
